TPU v7x, 32 devices: a whole 2x2x4 slice. The times are simulated.
32 devices in a mesh: dp: 4 (over z), fsdp: 8 (over y, x, core).
Axes of the slice: x: 2, y: 2, z: 4, core: 2. Of those that a mesh axis runs over, the one named last changes fastest.
Arguments:
- tokens: bfloat16 [4096, 2048], P(('dp', 'fsdp')), may hold values from -6 to 6
- ln_gain: float32 [2048], replicated, may hold values from 0.5 to 1.5
- ln_shift: float32 [2048], replicated, may hold values from -3 to 3
- w_qkv: bfloat16 [2048, 6144], P(('dp', 'fsdp')), may hold values from -0.125 to 0.125
- b_qkv: float32 [6144], replicated, may hold values from -3 to 3
- w_out: bfloat16 [2048, 2048], P(('dp', 'fsdp')), may hold values from -0.5 to 0.5
- w_gate: bfloat16 [2048, 5632], P(('dp', 'fsdp')), may hold values from -0.125 to 0.125
- w_up: bfloat16 [2048, 5632], P(('dp', 'fsdp')), may hold values from -0.125 to 0.125
- w_down: bfloat16 [5632, 2048], P(('dp', 'fsdp')), may hold values from -0.078125 to 0.078125
- grad_out: bfloat16 [4096, 2048], P(('dp', 'fsdp')), may hold values from -6 to 6
- seq_lengths: int32 [32, 4], P(('dp', 'fsdp')), may hold values from 0 to 128, as said below
Outputs:
- output: bfloat16 [4096, 2048], P(('dp', 'fsdp'))
- grad_tokens: bfloat16 [4096, 2048], P(('dp', 'fsdp'))
- grad_w_qkv: float32 [2048, 6144], P(('dp', 'fsdp'))
- grad_w_out: float32 [2048, 2048], P(('dp', 'fsdp'))
- grad_w_gate: float32 [2048, 5632], P(('dp', 'fsdp'))
- grad_w_up: float32 [2048, 5632], P(('dp', 'fsdp'))
- grad_w_down: float32 [5632, 2048], P(('dp', 'fsdp'))
- grad_gain: float32 [2048], P(('dp', 'fsdp'))
- grad_shift: float32 [2048], P(('dp', 'fsdp'))
- grad_bias: float32 [6144], P(('dp', 'fsdp'))
Inputs may be any that keep to these rules, and one draw needn't show every extreme that they name: `seq_lengths`: each device's row of lengths sums to at most 128; some device holds a single sequence of exactly 128 tokens, and some slots are empty (length 0).
All inputs are finite; a program needn't handle non-finite values.
Results may differ from a plain program's by a relative error of at most 0.012.
Values may be sent and summed in bfloat16 or wider, within the bound.
No kernel may reach another device: no remote copies, remote signals or barrier semaphores. Data moves between devices by JAX's collectives and lax.ppermute only.
A program may use at most 256 MiB of HBM per device.

v0:
```python
import functools
import math

import jax
import jax.numpy as jnp
from jax import lax
from jax.experimental import pallas as pl
from jax.experimental.pallas import tpu as pltpu
from jax.sharding import PartitionSpec as P

HD = 64
ROT = 16
EPS = 1e-05
NEG = -1e30
TILE = 128
AXES = ("dp", "fsdp")
BF = jnp.bfloat16
F32 = jnp.float32
CONTRACT_ROWS = (((0,), (0,)), ((), ()))
CONTRACT_COLS = (((1,), (1,)), ((), ()))


def block_terms(lengths_row, rows_tok):
    ends = jnp.cumsum(lengths_row)
    place = jnp.arange(rows_tok, dtype=jnp.int32)
    segment = jnp.sum((place[:, None] >= ends[None, :]).astype(jnp.int32), axis=1)
    starts = jnp.concatenate([ends - lengths_row, ends[-1:]])
    labels = jnp.arange(starts.shape[0], dtype=jnp.int32)
    begin = jnp.sum(jnp.where(segment[:, None] == labels[None, :], starts[None, :], 0), axis=1)
    position = (place - begin).astype(F32)
    valid = segment < lengths_row.shape[0]
    label_tok = jnp.where(valid, segment, lengths_row.shape[0] + place)
    allowed = (label_tok[:, None] == label_tok[None, :]) & (place[None, :] <= place[:, None])
    return (position, valid, allowed)


def turn_tables(position):
    half = ROT // 2
    freq = jnp.exp(jnp.arange(half, dtype=F32) * (-2.0 * math.log(10000.0) / ROT))
    turn = position.reshape(-1)[:, None] * freq[None, :]
    cosine, sine = jnp.cos(turn), jnp.sin(turn)
    rest = (turn.shape[0], HD - ROT)
    cos_t = jnp.concatenate([cosine, cosine, jnp.ones(rest, F32)], axis=1)
    sin_t = jnp.concatenate([-sine, sine, jnp.zeros(rest, F32)], axis=1)
    return (jnp.tile(cos_t, (1, 2)), jnp.tile(sin_t, (1, 2)))


def tie(*values):
    return lax.optimization_barrier(values)


def turned(v, cos_t, sin_t, low_half):
    partner = jnp.where(low_half, pltpu.roll(v, TILE - ROT // 2, 1), pltpu.roll(v, ROT // 2, 1))
    return v * cos_t + partner * sin_t

def stacked(v, first):
    zero = jnp.zeros_like(v)
    return jnp.concatenate([jnp.where(first, v, zero), jnp.where(first, zero, v)], axis=0)

def softmax_of(query2, keys, bias2):
    scores = lax.dot_general(query2, keys, (((1,), (1,)), ((), ())), preferred_element_type=F32)
    scores = scores * 0.125 + bias2
    lifted = jnp.exp(scores - jnp.max(scores, axis=1, keepdims=True))
    return lifted / jnp.sum(lifted, axis=1, keepdims=True)

def attend_rows(cols, main, rest, at, pq_ref, pf_ref, bias_ref, tables, joined_ref, qkv_ref):
    cos_t, sin_t, bias2, first, low_half = tables
    size = cos_t.shape[0]
    rows = slice(at, at + size)
    for pair in range(cols // TILE):
        places = [g * cols + pair * TILE for g in range(3)]
        query, keys, values = (
            pq_ref[rows, p : p + TILE] + bias_ref[0:1, p : p + TILE] for p in places
        )
        query = turned(query, cos_t, sin_t, low_half).astype(BF)
        keys = turned(keys, cos_t, sin_t, low_half).astype(BF)
        values = values.astype(BF)
        for p, v in zip(places, (query, keys, values)):
            qkv_ref[rows, p : p + TILE] = v
        probs = softmax_of(stacked(query, first), keys, bias2).astype(BF)
        mixed = jnp.dot(probs, values, preferred_element_type=F32)
        joined_ref[rows, pair * TILE : (pair + 1) * TILE] = jnp.where(
            first, mixed[:size], mixed[size:]
        ).astype(BF)
    for j in range(main // TILE):
        gate = pf_ref[rows, j * TILE : (j + 1) * TILE]
        up = pf_ref[rows, main + j * TILE : main + (j + 1) * TILE]
        hid = gate * jax.nn.sigmoid(gate) * up
        joined_ref[rows, cols + j * TILE : cols + (j + 1) * TILE] = hid.astype(BF)
    if rest:
        tail = pf_ref[rows, 2 * main :]
        up = pltpu.roll(tail, rest, 1)
        hid = tail * jax.nn.sigmoid(tail) * up
        joined_ref[rows, cols + main :] = hid[:, :rest].astype(BF)


def attend_back_rows(cols, main, rest, at, pf_ref, back_ref, qkv_ref, tables, gq_ref, gf_ref, sum_ref):
    cos_t, sin_t, bias2, first, low_half = tables
    size = cos_t.shape[0]
    rows = slice(at, at + size)
    across = (((0,), (0,)), ((), ()))
    for pair in range(cols // TILE):
        places = [g * cols + pair * TILE for g in range(3)]
        query, keys, values = (qkv_ref[rows, p : p + TILE] for p in places)
        query2 = stacked(query, first)
        mixed2 = stacked(back_ref[rows, pair * TILE : (pair + 1) * TILE].astype(BF), first)
        probs = softmax_of(query2, keys, bias2)
        grad_probs = lax.dot_general(
            mixed2, values, (((1,), (1,)), ((), ())), preferred_element_type=F32
        )
        inner = jnp.sum(probs * grad_probs, axis=1, keepdims=True)
        grad_scores = (probs * (grad_probs - inner)).astype(BF)
        gq = jnp.dot(grad_scores, keys, preferred_element_type=F32)
        gq = jnp.where(first, gq[:size], gq[size:]) * 0.125
        gk = lax.dot_general(grad_scores, query2, across, preferred_element_type=F32) * 0.125
        gv = lax.dot_general(probs.astype(BF), mixed2, across, preferred_element_type=F32)
        gq = turned(gq, cos_t, -sin_t, low_half)
        gk = turned(gk, cos_t, -sin_t, low_half)
        for p, v in zip(places, (gq, gk, gv)):
            low = v.astype(BF)
            gq_ref[rows, p : p + TILE] = low
            sum_ref[0:1, p : p + TILE] += jnp.sum(low.astype(F32), axis=0, keepdims=True)

    def gates(gate, up, grad_hid):
        sigma = jax.nn.sigmoid(gate)
        slope = sigma * (1.0 + gate * (1.0 - sigma))
        return (grad_hid * up * slope, grad_hid * (gate * sigma))

    for j in range(main // TILE):
        p, q = j * TILE, main + j * TILE
        grad_hid = back_ref[rows, cols + j * TILE : cols + (j + 1) * TILE]
        gg, gu = gates(pf_ref[rows, p : p + TILE], pf_ref[rows, q : q + TILE], grad_hid)
        gf_ref[rows, p : p + TILE] = gg.astype(BF)
        gf_ref[rows, q : q + TILE] = gu.astype(BF)
    if rest:
        tail = pf_ref[rows, 2 * main :]
        short = back_ref[rows, cols + main :]
        grad_hid = jnp.concatenate([short, jnp.zeros_like(short)], axis=1)
        gg, gu = gates(tail, pltpu.roll(tail, rest, 1), grad_hid)
        lane = lax.broadcasted_iota(jnp.int32, (size, TILE), 1)
        both = jnp.where(lane < rest, gg, pltpu.roll(gu, rest, 1))
        gf_ref[rows, 2 * main :] = both.astype(BF)


def block_tables(cos_ref, sin_ref, mask_ref, block, size):
    lane = lax.broadcasted_iota(jnp.int32, (size, TILE), 1)
    rows = slice(block * size, (block + 1) * size)
    mask = mask_ref[block]
    return (
        cos_ref[rows, :],
        sin_ref[rows, :],
        jnp.concatenate([mask, mask], axis=0),
        lane < HD,
        lane % HD < ROT // 2,
    )


def stack_copies(pieces, whole, sem, start):
    copies, count = [], len(pieces) // 2
    edge = pieces[0].shape[1]
    for group, columns in enumerate((pl.ds(0, edge), pl.ds(edge, whole.shape[1] - edge))):
        at = 0
        for i in range(group * count, (group + 1) * count):
            size = pieces[i].shape[0]
            dst = whole.at[pl.ds(at, size), columns]
            copies.append(pltpu.make_async_copy(pieces[i], dst, sem.at[start + i]))
            at += size
    return copies


def forward_kernel(sizes, count, block, *refs):
    cols, main, rest = sizes
    normed_ref, bias_ref, cos_ref, sin_ref, mask_ref = refs[:5]
    pieces, mixer_any = refs[5 : 5 + count], refs[5 + count]
    joined_ref, qkv_ref, pf_ref, branch_ref = refs[6 + count : 10 + count]
    entry, wm, pq, sem = refs[10 + count :]
    groups = [
        stack_copies(pieces, entry, sem, 0),
        [pltpu.make_async_copy(mixer_any, wm, sem.at[count])],
    ]
    opening = pl.program_id(0) == 0

    @pl.when(opening)
    def _():
        for group in groups:
            for copy in group:
                copy.start()

    def arrive(group):
        @pl.when(opening)
        def _():
            for copy in groups[group]:
                copy.wait()

    normed = normed_ref[...]
    arrive(0)
    pq[...] = jnp.dot(normed, entry[:, : 3 * cols], preferred_element_type=F32)
    pf_ref[...] = jnp.dot(normed, entry[:, 3 * cols :], preferred_element_type=F32)
    for i in range(normed.shape[0] // block):
        tables = block_tables(cos_ref, sin_ref, mask_ref, i, block)
        attend_rows(
            cols, main, rest, i * block, pq, pf_ref, bias_ref, tables, joined_ref, qkv_ref
        )
    arrive(1)
    branch = jnp.dot(joined_ref[...], wm[...], preferred_element_type=F32)
    branch_ref[...] = branch.astype(BF)


def backward_kernel(sizes, count, block, *refs):
    cols, main, rest = sizes
    masked_ref, pf_ref, qkv_ref, cos_ref, sin_ref, mask_ref, mixer_any = refs[:7]
    pieces = refs[7 : 7 + count]
    gq_ref, gf_ref, norm_ref, sum_ref = refs[7 + count : 11 + count]
    wm, entry, back, sem = refs[11 + count :]
    mixer_copy = pltpu.make_async_copy(mixer_any, wm, sem.at[count])
    copies = stack_copies(pieces, entry, sem, 0)
    opening = pl.program_id(0) == 0

    @pl.when(opening)
    def _():
        mixer_copy.start()
        for copy in copies:
            copy.start()
        sum_ref[...] = jnp.zeros_like(sum_ref)
        mixer_copy.wait()

    back[...] = lax.dot_general(
        masked_ref[...], wm[...], CONTRACT_COLS, preferred_element_type=F32
    )
    for i in range(masked_ref.shape[0] // block):
        tables = block_tables(cos_ref, sin_ref, mask_ref, i, block)
        attend_back_rows(
            cols, main, rest, i * block, pf_ref, back, qkv_ref, tables, gq_ref, gf_ref, sum_ref
        )

    @pl.when(opening)
    def _():
        for copy in copies:
            copy.wait()

    cut = 3 * cols
    total = lax.dot_general(
        gq_ref[...], entry[:, :cut], CONTRACT_COLS, preferred_element_type=F32
    )
    total += lax.dot_general(
        gf_ref[...], entry[:, cut:], CONTRACT_COLS, preferred_element_type=F32
    )
    norm_ref[...] = total.astype(BF)


STEP = 256
HIDDEN_COST = pl.CostEstimate(flops=1, bytes_accessed=1, transcendentals=0)


def row_spec(width, rows=STEP):
    return pl.BlockSpec((rows, width), lambda i: (i, 0))


ANYWHERE = pl.BlockSpec(memory_space=pl.ANY)
HELD = pl.BlockSpec(memory_space=pltpu.VMEM)


def kept(*arrays):
    return [pltpu.with_memory_space_constraint(array, pltpu.HBM) for array in arrays]


def stepping(limit):
    return pltpu.CompilerParams(
        dimension_semantics=("arbitrary",), vmem_limit_bytes=limit << 20
    )


def forward_call(normed, bias, cos_t, sin_t, mask, pieces, mixer, sizes):
    cols, main, rest = sizes
    everyone, width = normed.shape
    block = mask.shape[1]
    count = len(pieces)
    joint = cols + main + rest
    return pl.pallas_call(
        functools.partial(forward_kernel, sizes, count, block),
        grid=(everyone // STEP,),
        in_specs=[
            row_spec(width),
            pl.BlockSpec((8, 3 * cols), lambda i: (0, 0)),
            row_spec(TILE),
            row_spec(TILE),
            pl.BlockSpec((STEP // block, block, block), lambda i: (i, 0, 0)),
        ]
        + [ANYWHERE] * (count + 1),
        out_specs=[
            row_spec(joint),
            row_spec(3 * cols),
            row_spec(2 * (main + rest)),
            row_spec(width),
        ],
        out_shape=[
            pltpu.HBM((everyone, joint), BF),
            pltpu.HBM((everyone, 3 * cols), BF),
            pltpu.HBM((everyone, 2 * (main + rest)), F32),
            pltpu.HBM((everyone, width), BF),
        ],
        scratch_shapes=[
            pltpu.VMEM((width, 3 * cols + 2 * (main + rest)), BF),
            pltpu.VMEM((joint, width), BF),
            pltpu.VMEM((STEP, 3 * cols), F32),
            pltpu.SemaphoreType.DMA((count + 1,)),
        ],
        compiler_params=stepping(36),
        cost_estimate=HIDDEN_COST,
        name="forward",
    )(*kept(normed, bias, cos_t, sin_t, mask, *pieces, mixer))


def backward_call(masked, pf, qkv, cos_t, sin_t, mask, mixer, pieces, sizes):
    cols, main, rest = sizes
    everyone, width = masked.shape
    block = mask.shape[1]
    count = len(pieces)
    joint = cols + main + rest
    total = 3 * cols + 2 * (main + rest)
    return pl.pallas_call(
        functools.partial(backward_kernel, sizes, count, block),
        grid=(everyone // STEP,),
        in_specs=[
            row_spec(width),
            row_spec(2 * (main + rest)),
            row_spec(3 * cols),
            row_spec(TILE),
            row_spec(TILE),
            pl.BlockSpec((STEP // block, block, block), lambda i: (i, 0, 0)),
        ]
        + [ANYWHERE] * (count + 1),
        out_specs=[
            row_spec(3 * cols),
            row_spec(2 * (main + rest)),
            row_spec(width),
            pl.BlockSpec((8, 3 * cols), lambda i: (0, 0)),
        ],
        out_shape=[
            pltpu.HBM((everyone, 3 * cols), BF),
            pltpu.HBM((everyone, 2 * (main + rest)), BF),
            pltpu.HBM((everyone, width), BF),
            pltpu.HBM((8, 3 * cols), F32),
        ],
        scratch_shapes=[
            pltpu.VMEM((joint, width), BF),
            pltpu.VMEM((width, total), BF),
            pltpu.VMEM((STEP, joint), F32),
            pltpu.SemaphoreType.DMA((count + 1,)),
        ],
        compiler_params=stepping(36),
        cost_estimate=HIDDEN_COST,
        name="backward",
    )(*kept(masked, pf, qkv, cos_t, sin_t, mask, mixer, *pieces))


def product_call(normed, grad, groups, size):
    low, width = 0, grad.shape[1]
    slabs = [slab for group in groups for slab in group]
    places = [(g, at) for g, group in enumerate(groups) for at in range(len(group))]
    count = len(slabs)

    def kernel(table_ref, lhs_any, grad_any, *refs):
        outs, (lhs, grad, held, sem) = refs[: len(groups)], refs[len(groups) :]
        loads = [pltpu.make_async_copy(grad_any.at[:, pl.ds(low, width)], grad, sem.at[2 * count])]
        copies = []
        for i, (g, at) in enumerate(places):
            slab = pl.multiple_of(table_ref[i] * size, size)
            src = lhs_any.at[:, pl.ds(slab, size)]
            loads.append(pltpu.make_async_copy(src, lhs.at[i], sem.at[count + i]))
            dst = outs[g].at[pl.ds(at * size, size), :]
            copies.append(pltpu.make_async_copy(held.at[i], dst, sem.at[i]))
        for load in loads:
            load.start()
        loads[0].wait()

        def step(i, _):
            for j in range(count):
                pl.when(i == j)(loads[1 + j].wait)
            held[i] = lax.dot_general(
                lhs[i], grad[...], CONTRACT_ROWS, preferred_element_type=F32
            ).astype(BF)
            for j, copy in enumerate(copies):
                pl.when(i == j)(copy.start)

        lax.fori_loop(0, count, step, None)
        for copy in copies:
            copy.wait()

    everyone = normed.shape[0]
    return pl.pallas_call(
        kernel,
        in_specs=[pl.BlockSpec(memory_space=pltpu.SMEM), ANYWHERE, ANYWHERE],
        out_specs=[pl.BlockSpec(memory_space=pltpu.HBM)] * len(groups),
        out_shape=[pltpu.HBM((len(group) * size, width), BF) for group in groups],
        scratch_shapes=[
            pltpu.VMEM((count, everyone, size), BF),
            pltpu.VMEM((everyone, width), BF),
            pltpu.VMEM((count, size, width), BF),
            pltpu.SemaphoreType.DMA((2 * count + 1,)),
        ],
        compiler_params=pltpu.CompilerParams(vmem_limit_bytes=24 << 20),
        cost_estimate=HIDDEN_COST,
        name="weight_grad",
    )(jnp.array(slabs, jnp.int32), *kept(normed, grad))


def mixer_grad_call(lane, joined, masked, wide, own, own_ff, cut):
    everyone, joint = joined.shape
    width = masked.shape[1]
    rest = own + own_ff - cut

    def kernel(lane_ref, joined_ref, masked_ref, *refs):
        to_x, to_y, x_high, y_low, own_low, own_high, whole, sem = refs
        masked = masked_ref[...]

        def product(at, size):
            whole[pl.ds(at, size), :] = lax.dot_general(
                joined_ref[:, pl.ds(at, size)],
                masked,
                CONTRACT_ROWS,
                preferred_element_type=F32,
            ).astype(BF)

        lax.fori_loop(
            0, joint // STEP, lambda i, _: product(pl.multiple_of(i * STEP, STEP), STEP), None
        )
        if joint % STEP:
            product(joint // STEP * STEP, joint % STEP)
        halves = [
            own_low,
            own_high,
            to_x.at[pl.ds(cut, cut), :],
            x_high,
            y_low,
            to_y.at[pl.ds(rest, rest), :],
            to_x.at[pl.ds(0, cut), :],
            to_y.at[pl.ds(0, rest), :],
        ]
        pairs = row_spans(wide, own, own_ff, cut, lane_ref[0], halves, whole)
        run_copies([(there, here) for here, there in pairs], sem)

    shapes = [(size, width) for size in (2 * cut, 2 * rest, rest, cut, cut, rest)]
    return pl.pallas_call(
        kernel,
        in_specs=[pl.BlockSpec(memory_space=pltpu.SMEM), HELD, HELD],
        out_specs=[pl.BlockSpec(memory_space=pltpu.HBM)] * len(shapes),
        out_shape=[pltpu.HBM(shape, BF) for shape in shapes],
        scratch_shapes=[
            pltpu.VMEM((joint, width), BF),
            pltpu.SemaphoreType.DMA((3 * wide,)),
        ],
        compiler_params=pltpu.CompilerParams(vmem_limit_bytes=40 << 20),
        cost_estimate=HIDDEN_COST,
        name="mixer_grad",
    )(lane, joined, masked)


def column_plan(member, outer, wide, cores, own, own_ff, cols, main, rest):
    z, c = member // cores, member % cores
    out = []
    for g in range(3):
        for k in range(wide):
            src = (((g * outer + z) * wide + k) * cores + c) * own
            out.append((0, src, 0, g * cols + k * own, own))
    for which in range(2):
        for k in range(wide):
            src = ((z * wide + k) * cores + c) * own_ff
            lo, hi = k * own_ff, (k + 1) * own_ff
            cut = min(hi, main)
            if cut > lo:
                out.append((1 + which, src, 1, which * main + lo, cut - lo))
            low = max(lo, main)
            if hi > low:
                at = 2 * main + which * rest + low - main
                out.append((1 + which, src + low - lo, 1, at, hi - low))
    return out


def pack_kernel(plan, tp, bases, *refs):
    arrays, packed = refs[:3], refs[3:]
    rows = arrays[0].shape[0]
    edge = packed[0].shape[1]
    for member in range(tp):
        at = slice(member * rows, (member + 1) * rows)
        for which, src, part, dst, width in plan(member):
            dst += bases[part]
            for ref, low, high in ((packed[0], 0, edge), (packed[1], edge, sum(bases))):
                start, stop = max(dst, low), min(dst + width, high)
                if start < stop:
                    there = slice(src + start - dst, src + stop - dst)
                    ref[at, start - low : stop - low] = arrays[which][:, there]


def pack_call(arrays, plan, tp, widths):
    rows = arrays[0].shape[0]
    total = sum(widths)
    edge = (total // 2 + TILE - 1) // TILE * TILE
    return pl.pallas_call(
        functools.partial(pack_kernel, plan, tp, (0, widths[0], total - widths[0])),
        in_specs=[HELD] * 3,
        out_specs=[HELD] * 2,
        out_shape=[jax.ShapeDtypeStruct((tp * rows, w), BF) for w in (edge, total - edge)],
        compiler_params=pltpu.CompilerParams(vmem_limit_bytes=32 << 20),
        name="pack_columns",
    )(*arrays)


def unpack_kernel(plan, tp, part, *refs):
    packed, outs = refs[0], refs[1:]
    rows = outs[0].shape[0]
    for member in range(tp):
        at = slice(member * rows, (member + 1) * rows)
        for which, src, source, dst, width in plan(member):
            if source == part:
                out = outs[which - part]
                out[:, src : src + width] = packed[at, dst : dst + width].astype(F32)


def unpack_call(packed, part, plan, tp, widths):
    rows = packed.shape[0] // tp
    return pl.pallas_call(
        functools.partial(unpack_kernel, plan, tp, part),
        in_specs=[HELD],
        out_specs=[HELD] * len(widths),
        out_shape=[jax.ShapeDtypeStruct((rows, width), F32) for width in widths],
        compiler_params=pltpu.CompilerParams(vmem_limit_bytes=32 << 20),
        cost_estimate=HIDDEN_COST,
        name="unpack_columns",
    )(packed)


def join_kernel(count, *refs):
    ins, out, sem = refs[:count], refs[count], refs[count + 1]
    copies, at = [], 0
    for i, ref in enumerate(ins):
        size = ref.shape[0]
        copies.append(pltpu.make_async_copy(ref, out.at[pl.ds(at, size), :], sem.at[i]))
        at += size
    for copy in copies:
        copy.start()
    for copy in copies:
        copy.wait()


def join_call(arrays):
    count = len(arrays)
    rows, width = sum(array.shape[0] for array in arrays), arrays[0].shape[1]
    return pl.pallas_call(
        functools.partial(join_kernel, count),
        in_specs=[pl.BlockSpec(memory_space=pl.ANY)] * count,
        out_specs=pl.BlockSpec(memory_space=pltpu.VMEM),
        out_shape=jax.ShapeDtypeStruct((rows, width), BF),
        scratch_shapes=[pltpu.SemaphoreType.DMA((count,))],
        compiler_params=pltpu.CompilerParams(vmem_limit_bytes=16 << 20),
        name="join_rows",
    )(*arrays)


def row_spans(wide, own, own_ff, cut, lane, halves, whole):
    spans = []
    base = wide * own
    for j in range(wide):
        spot = lax.bitwise_xor(lane, j)
        down = pl.multiple_of(base + spot * own_ff, 16)
        down_low = pl.multiple_of(base + spot * own_ff + cut, 16)
        out = pl.multiple_of(spot * own, 16)
        low, high = halves[2 * j : 2 * j + 2]
        rest = own_ff - cut
        spans.append((low, whole.at[pl.ds(down, cut), :]))
        spans.append((high.at[pl.ds(0, rest), :], whole.at[pl.ds(down_low, rest), :]))
        spans.append((high.at[pl.ds(rest, own), :], whole.at[pl.ds(out, own), :]))
    return spans


def run_copies(pairs, sem):
    copies = [pltpu.make_async_copy(src, dst, sem.at[i]) for i, (src, dst) in enumerate(pairs)]
    for copy in copies:
        copy.start()
    for copy in copies:
        copy.wait()


def place_call(lane, halves, wide, own, own_ff, cut):
    width = halves[0].shape[1]

    def kernel(lane_ref, *refs):
        ins, out, sem = refs[:-2], refs[-2], refs[-1]
        run_copies(row_spans(wide, own, own_ff, cut, lane_ref[0], ins, out), sem)

    return pl.pallas_call(
        kernel,
        in_specs=[pl.BlockSpec(memory_space=pltpu.SMEM)]
        + [pl.BlockSpec(memory_space=pl.ANY)] * len(halves),
        out_specs=pl.BlockSpec(memory_space=pltpu.VMEM),
        out_shape=jax.ShapeDtypeStruct((wide * (own + own_ff), width), BF),
        scratch_shapes=[pltpu.SemaphoreType.DMA((3 * wide,))],
        compiler_params=pltpu.CompilerParams(vmem_limit_bytes=16 << 20),
        name="place_rows",
    )(lane, *halves)


def mixer_product(joined, masked):
    return lax.dot_general(joined, masked, CONTRACT_ROWS, preferred_element_type=F32).astype(BF)


class Plain:
    def __init__(self, outer, inner):
        self.tp, self.wide, self.cores, self.outer = outer, inner, 1, outer
        self.member = lax.axis_index("dp")
        self.token_axes, self.token_groups = "dp", None
        self.weight_axes, self.weight_groups = "fsdp", None

    def gather_tokens(self, block):
        return lax.all_gather(
            block, self.token_axes, axis=0, tiled=True, axis_index_groups=self.token_groups
        )

    def scatter_tokens(self, part):
        return lax.psum_scatter(
            part.astype(BF),
            self.token_axes,
            scatter_dimension=0,
            tiled=True,
            axis_index_groups=self.token_groups,
        ).astype(F32)

    def exchange(self, part):
        return lax.all_to_all(
            part,
            self.token_axes,
            split_axis=0,
            concat_axis=0,
            tiled=True,
            axis_index_groups=self.token_groups,
        )

    def gather_weights(self, block):
        return lax.all_gather(
            block, self.weight_axes, axis=0, tiled=True, axis_index_groups=self.weight_groups
        )

    def scatter_weights(self, part):
        return lax.psum_scatter(
            part,
            self.weight_axes,
            scatter_dimension=0,
            tiled=True,
            axis_index_groups=self.weight_groups,
        )

    def inputs(self, packed, w_out, w_down, normed, masked, lengths, make_tables):
        mixer = jnp.concatenate([self.gather_weights(w) for w in (w_out, w_down)], axis=0)
        entry = [self.gather_weights(self.exchange(part)) for part in packed]
        tokens = [self.gather_tokens(block) for block in (normed, masked)]
        lengths = lax.all_gather(lengths, "dp", axis=0, tiled=True)
        return entry, mixer, tokens[0], tokens[1], make_tables(lengths)

    def outputs(self, joined, masked, branch, back_call, tail, normed, own, own_ff):
        cols = self.wide * own
        part = mixer_product(joined, masked)
        grads = [self.scatter_weights(p).astype(F32) for p in (part[:cols], part[cols:])]
        grad_qkv, grad_ff, norm, bias_part = back_call(masked)
        parts = []
        for grad in (grad_qkv, grad_ff):
            part = lax.dot_general(normed, grad, CONTRACT_ROWS, preferred_element_type=F32)
            parts.append(self.scatter_weights(part.astype(BF)))
        norm, branch = self.scatter_tokens(norm), self.scatter_tokens(branch)
        part_qkv, part_ff = [self.exchange(part) for part in parts]
        grad_tokens, stats = tail(norm, bias_part)
        stats = self.scatter_stats(stats)
        return grads[0], grads[1], part_qkv, part_ff, branch, grad_tokens, stats

    def relative(self, blocks, axis):
        return blocks

    def scatter_stats(self, stats):
        parts = lax.all_to_all(stats, AXES, split_axis=0, concat_axis=0, tiled=True)
        return jnp.sum(parts, axis=0)


class Linked(Plain):
    def __init__(self, outer, inner):
        self.outer, self.cores, self.wide = outer, 2, inner // 2
        self.tp = outer * 2
        flat = lax.axis_index("fsdp")
        self.lane = flat // 2
        self.member = lax.axis_index("dp") * 2 + lax.rem(flat, 2)
        spots = [
            [[(z * self.wide + k) * 2 + c for c in range(2)] for k in range(self.wide)]
            for z in range(outer)
        ]
        self.token_axes = self.weight_axes = AXES
        self.token_groups = [
            [spots[z][k][c] for z in range(outer) for c in range(2)] for k in range(self.wide)
        ]
        self.weight_groups = [
            [spots[z][k][c] for k in range(self.wide)] for z in range(outer) for c in range(2)
        ]
        self.spots = spots
        self.lane_index = self.lane.astype(jnp.int32).reshape(1)

    def send(self, value, step=0, dz=0, dc=0):
        pairs = [
            (self.spots[z][k][c], self.spots[z ^ dz][k ^ step][c ^ dc])
            for z in range(self.outer)
            for k in range(self.wide)
            for c in range(2)
        ]
        return lax.ppermute(value, AXES, pairs)

    def gather_lengths(self, lengths):
        parts = [lengths] + [self.send(lengths, dz=dz) for dz in range(1, self.outer)]
        return jnp.concatenate(parts, axis=0)

    def order_lengths(self, mine, other):
        both = jnp.stack([mine, other], axis=1).reshape(self.tp, -1)
        spot = lax.bitwise_xor(jnp.arange(self.tp, dtype=jnp.int32), self.member)
        pick = spot[:, None] == jnp.arange(self.tp, dtype=jnp.int32)[None, :]
        return jnp.sum(jnp.where(pick[:, :, None], both[None], 0), axis=1)

    def inputs(self, packed, w_out, w_down, normed, masked, lengths, make_tables):
        own, own_ff = w_out.shape[0], w_down.shape[0]
        cut = own_ff // 32 * 16 + 32
        half = packed[0].shape[0] // 2
        rows, left, right, lengths = tie(join_call([w_down, w_out]), *packed, lengths)
        mix_x, mix_y = self.send(rows, 1), self.send(rows, 2)
        lengths = self.gather_lengths(lengths)
        left = self.exchange(left)
        left, right, mix_x, mix_y = tie(left, right, mix_x, mix_y)
        left_x, left_y = self.send(left, 1), self.send(left, 2)
        right = self.exchange(right)
        right, left_x, left_y, normed, masked, lengths = tie(
            right, left_x, left_y, normed, masked, lengths
        )
        tables = make_tables(self.order_lengths(lengths, self.send(lengths, dc=1)))
        normed_all = self.gather_tokens(normed)
        right_x, right_y = self.send(right, 1), self.send(right, 2)
        left_low, left_high = self.send(left_x[:half], 2), self.send(left_y[half:], 1)
        mix_low, mix_high = self.send(mix_x[:cut], 2), self.send(mix_y[cut:], 1)
        halves = [part for b in (rows, mix_x, mix_y) for part in (b[:cut], b[cut:])]
        right_x, right_y, left_low, left_high, mix_low, mix_high, masked, *others = tie(
            right_x, right_y, left_low, left_high, mix_low, mix_high, masked, *halves, *tables
        )
        halves, tables = others[: len(halves)], others[len(halves) :]
        masked_all = self.gather_tokens(masked)
        right_low, right_high = self.send(right_x[:half], 2), self.send(right_y[half:], 1)
        halves += [mix_low, mix_high]
        mixer = place_call(self.lane_index, halves, self.wide, own, own_ff, cut)
        entry = [left, left_x, left_y, left_low, left_high]
        entry += [right, right_x, right_y, right_low, right_high]
        return entry, mixer, normed_all, masked_all, tables

    def first_sends(self, to_x, to_y):
        return self.send(to_x, 1), self.send(to_y, 2)

    def last_sends(self, got, x_high, y_low):
        from_x, from_y = got
        low, high = from_x[: y_low.shape[0]], from_y[: x_high.shape[0]]
        return (
            self.send((x_high.astype(F32) + high.astype(F32)).astype(BF), 1),
            self.send((y_low.astype(F32) + low.astype(F32)).astype(BF), 2),
        )

    def lane_sum(self, own_low, own_high, first, last):
        low = own_low.astype(F32) + first[0][own_low.shape[0] :].astype(F32)
        high = own_high.astype(F32) + first[1][own_high.shape[0] :].astype(F32)
        return low + last[1].astype(F32), high + last[0].astype(F32)

    def outputs(self, joined, masked, branch, back_call, tail, normed, own, own_ff):
        cut = own_ff // 32 * 16 + 32
        rest = own_ff - cut
        size = normed.shape[1] // self.wide // 2
        first, last = ((6, 2), (7, 5)), ((3,), (4,), (0,), (1,))

        branch = self.scatter_tokens(branch)
        mix = mixer_grad_call(self.lane_index, joined, masked, self.wide, own, own_ff, cut)
        *mix, masked = tie(*mix, masked)
        mix_first = self.first_sends(mix[0], mix[1])
        grad_qkv, grad_ff, norm, bias_part = back_call(masked)
        *mix_first, norm, grad_ff, grad_qkv = tie(*mix_first, norm, grad_ff, grad_qkv)
        norm = self.scatter_tokens(norm)
        to_x, to_y = product_call(normed, grad_ff, first, size)
        to_x, to_y, grad_ff = tie(to_x, to_y, grad_ff)
        ff_first = self.first_sends(to_x, to_y)
        x_high, y_low, ff_low, ff_high = product_call(normed, grad_ff, last, size)
        ff_low, grad_qkv = tie(ff_low, grad_qkv)
        to_x, to_y = product_call(normed, grad_qkv, first, size)
        to_x, grad_qkv = tie(to_x, grad_qkv)
        qkv_x, qkv_y, qkv_low, qkv_high = product_call(normed, grad_qkv, last, size)
        branch, to_x, to_y, x_high, y_low, qkv_low, *ff_first = tie(
            branch, to_x, to_y, x_high, y_low, qkv_low, *ff_first
        )
        ff_last = self.last_sends(ff_first, x_high, y_low)
        part_ff = self.joined_sum((x_high, y_low, ff_low, ff_high), ff_first, ff_last)
        part_ff, to_x, to_y = tie(part_ff, to_x, to_y)
        qkv_first = self.first_sends(to_x, to_y)
        part_ff = self.exchange(part_ff)
        results = tail(norm, bias_part)
        *qkv_first, grad_tokens, stats = tie(*qkv_first, *results)
        qkv_last = self.last_sends(qkv_first, qkv_x, qkv_y)
        part_qkv = self.joined_sum((qkv_x, qkv_y, qkv_low, qkv_high), qkv_first, qkv_last)
        part_ff, part_qkv, stats = tie(part_ff, part_qkv, stats)
        part_qkv = self.exchange(part_qkv)
        stats = self.chip_stats(stats)
        stats, *mix = tie(stats, *mix_first, *mix[2:])
        mix_first, mix = mix[:2], mix[2:]
        mix_last = self.last_sends(mix_first, mix[0], mix[1])
        stats = self.scatter_stats(stats)
        low, high = self.lane_sum(mix[2], mix[3], mix_first, mix_last)
        grad_w_out, grad_w_down = high[rest:], jnp.concatenate([low, high[:rest]], axis=0)
        return grad_w_out, grad_w_down, part_qkv, part_ff, branch, grad_tokens, stats

    def joined_sum(self, late, first, last):
        low, high = self.lane_sum(late[2], late[3], first, last)
        return jnp.concatenate([low, high], axis=0).astype(BF)

    def keep(self, values, axis, place, count, name):
        pick = lambda spot: lax.dynamic_index_in_dim(values, spot, axis, keepdims=False)
        got = [self.send(pick(lax.bitwise_xor(place, j)), **{name: j}) for j in range(1, count)]
        return pick(place) + sum(got)

    def chip_stats(self, stats):
        split = stats.reshape(self.outer, self.wide, 2, -1)
        return self.keep(split, 2, lax.rem(self.member, 2), 2, "dc")

    def scatter_stats(self, split):
        split = self.keep(split, 1, self.lane, self.wide, "step")
        return self.keep(split, 0, self.member // 2, self.outer, "dz")

    def relative(self, blocks, axis):
        shape = blocks.shape
        split = blocks.reshape(shape[:axis] + (2, 2) + shape[axis + 1 :])
        split = jnp.where(self.lane >= 2, jnp.flip(split, axis), split)
        split = jnp.where(lax.rem(self.lane, 2) == 1, jnp.flip(split, axis + 1), split)
        return split.reshape(shape)


def on_device(
    tokens, ln_gain, ln_shift, w_qkv, b_qkv, w_out, w_gate, w_up, w_down, grad_out, seq_lengths
):
    outer, inner = lax.axis_size("dp"), lax.axis_size("fsdp")
    linked = outer == 4 and inner == 8
    net = Linked(outer, inner) if linked else Plain(outer, inner)
    tp, wide, cores = net.tp, net.wide, net.cores
    rows_tok, width = tokens.shape
    own = w_qkv.shape[0]
    own_ff = w_down.shape[0]
    cols, cols_ff = wide * own, wide * own_ff
    main = cols_ff // TILE * TILE
    rest = cols_ff - main
    widths = (3 * cols, 2 * cols_ff)
    plan = lambda member: column_plan(
        member, outer, wide, cores, own, own_ff, cols, main, rest
    )

    _, valid, _ = block_terms(seq_lengths[0], rows_tok)
    keep_row = valid.astype(F32)[:, None]
    widened = tokens.astype(F32)
    centered = widened - jnp.mean(widened, axis=1, keepdims=True)
    inv_std = lax.rsqrt(jnp.mean(centered * centered, axis=1, keepdims=True) + EPS)
    scaled = centered * inv_std
    normed = (scaled * ln_gain + ln_shift).astype(BF)
    masked = (grad_out.astype(F32) * keep_row).astype(BF)

    def lanes_first(x):
        split = x.reshape(rows_tok, outer, wide, cores * own)
        return net.relative(jnp.swapaxes(split, 1, 2), 1).reshape(rows_tok, width)

    def lanes_back(x):
        split = net.relative(x.reshape(rows_tok, wide, outer, cores * own), 1)
        return jnp.swapaxes(split, 1, 2).reshape(rows_tok, width)

    lengths = seq_lengths
    arrays = [w_qkv, w_gate, w_up]

    def make_tables(lengths):
        position, _, allowed = jax.vmap(lambda row: block_terms(row, rows_tok))(lengths)
        return [*turn_tables(position), jnp.where(allowed, 0.0, NEG)]

    entry, mixer, normed_all, masked_all, (cos_t, sin_t, mask) = net.inputs(
        pack_call(arrays, plan, tp, widths),
        w_out,
        w_down,
        lanes_first(normed),
        masked,
        lengths,
        make_tables,
    )
    bias = lax.dynamic_index_in_dim(
        jnp.transpose(b_qkv.reshape(3, outer, wide, cores, own), (1, 3, 0, 2, 4)).reshape(tp, -1),
        net.member,
        0,
    )
    bias = jnp.broadcast_to(bias, (8, 3 * cols))

    sizes = (cols, main, rest)
    joined, qkv, proj_ff, branch = forward_call(
        normed_all, bias, cos_t, sin_t, mask, entry, mixer, sizes
    )
    back_call = lambda masked: backward_call(
        masked, proj_ff, qkv, cos_t, sin_t, mask, mixer, entry, sizes
    )

    def tail(grad_norm, bias_part):
        grad_norm = lanes_back(grad_norm)
        lifted_grad = grad_norm * ln_gain
        grad_in = inv_std * (
            lifted_grad
            - jnp.mean(lifted_grad, axis=1, keepdims=True)
            - scaled * jnp.mean(lifted_grad * scaled, axis=1, keepdims=True)
        )
        grad_tokens = (grad_out.astype(F32) + grad_in).astype(BF)
        shards = outer * inner
        gain_part = jnp.sum(grad_norm * scaled, axis=0)
        shift_part = jnp.sum(grad_norm, axis=0)
        bias_full = lax.dynamic_update_index_in_dim(
            jnp.zeros((tp, 3 * cols), F32), bias_part[0], net.member, 0
        )
        bias_full = jnp.transpose(bias_full.reshape(outer, cores, 3, wide, own), (2, 0, 3, 1, 4))
        stats = jnp.concatenate(
            [
                gain_part.reshape(shards, own),
                shift_part.reshape(shards, own),
                bias_full.reshape(shards, 3 * own),
            ],
            axis=1,
        )
        return grad_tokens, stats

    grad_w_out, grad_w_down, part_qkv, part_ff, branch, grad_tokens, stats = net.outputs(
        joined, masked_all, branch, back_call, tail, normed_all, own, own_ff
    )
    output = (widened + keep_row * branch).astype(BF)
    grad_w_gate, grad_w_up = unpack_call(
        part_ff, 1, plan, tp, [w_gate.shape[1], w_up.shape[1]]
    )
    part_qkv, stats, grad_w_gate, grad_w_up = tie(part_qkv, stats, grad_w_gate, grad_w_up)
    (grad_w_qkv,) = unpack_call(part_qkv, 0, plan, tp, [w_qkv.shape[1]])
    return (
        output,
        grad_tokens,
        grad_w_qkv,
        grad_w_out,
        grad_w_gate,
        grad_w_up,
        grad_w_down,
        stats[:own],
        stats[own : 2 * own],
        stats[2 * own :],
    )


def solution(mesh):
    rows = P(AXES, None)
    return jax.shard_map(
        on_device,
        mesh=mesh,
        in_specs=(rows, P(), P(), rows, P(), rows, rows, rows, rows, rows, rows),
        out_specs=(rows,) * 7 + (P(AXES),) * 3,
        check_vma=False,
    )
```

profile of v0, /device:TPU:0, one launch (start us, length us, event | category | flops | bytes accessed | tf_op | source)
XLA Modules:
  0.0 380.8 jit_solution(1214876884258796027)
XLA Ops:
  13.3 6.5 %all-to-all-start = ((bf16[8,64,1152]{2,1,0:T(8,128)(2,1)}), bf16[8,64,1152]{2,1,0:T(8,128)(2,1)S(1)}, u32[]{:S(2)}, u32[]{:S(2)}) async-start(bf16[8,64,1152]{2,1,0:T(8,128)(2,1)} %bitcast.2), calls=%async_computation | async-start | bytes 2359296 | tf_op jit(solution)/shard_map/all_to_all | solution.py:629
  22.8 3.8 %collective-permute-start.6 = (s32[1,4]{1,0:T(1,128)S(1)}, s32[1,4]{1,0:T(1,128)S(1)}, u32[]{:S(2)}, u32[]{:S(2)}) collective-permute-start(s32[1,4]{1,0:T(1,128)S(1)} %copy-done.34), channel_id=1, source_target_pairs={{0,24},{1,25},{2,26},{3,27},{4,28},{5,29},{6,30},{7,31},{8,16},{9,... | collective-permute-start | bytes 56 | tf_op jit(solution)/shard_map/ppermute | solution.py:710
  27.7 16.4 %collective-permute-done.1 = bf16[240,2048]{1,0:T(8,128)(2,1)} collective-permute-done((bf16[240,2048]{1,0:T(8,128)(2,1)S(1)}, bf16[240,2048]{1,0:T(8,128)(2,1)}, u32[]{:S(2)}, u32[]{:S(2)}) %collective-permute-start.1) | collective-permute-done | bytes 983072 | tf_op jit(solution)/shard_map/ppermute | solution.py:710
  45.3 3.9 %all-to-all-done = bf16[8,64,1152]{2,1,0:T(8,128)(2,1)S(1)} async-done(((bf16[8,64,1152]{2,1,0:T(8,128)(2,1)}), bf16[8,64,1152]{2,1,0:T(8,128)(2,1)S(1)}, u32[]{:S(2)}, u32[]{:S(2)}) %all-to-all-start) | async-done | bytes 1179680 | tf_op jit(solution)/shard_map/all_to_all | solution.py:629
  49.2 4.3 %all-to-all-start.1 = ((bf16[8,64,1024]{2,1,0:T(8,128)(2,1)}), bf16[8,64,1024]{2,1,0:T(8,128)(2,1)}, u32[]{:S(2)}, u32[]{:S(2)}) async-start(bf16[8,64,1024]{2,1,0:T(8,128)(2,1)} %bitcast.4), calls=%async_computation.1 | async-start | bytes 2097152 | tf_op jit(solution)/shard_map/all_to_all | solution.py:629
  67.4 16.1 %collective-permute-done.3.refs_7_.refs_9_ = bf16[512,1152]{1,0:T(8,128)(2,1)S(1)} collective-permute-done((bf16[512,1152]{1,0:T(8,128)(2,1)S(1)}, bf16[512,1152]{1,0:T(8,128)(2,1)S(1)}, u32[]{:S(2)}, u32[]{:S(2)}) %collective-permute-start.3) | collective-permute-done | bytes 1179680 | tf_op jit(solution)/shard_map/ppermute | solution.py:710
  101.1 3.9 %collective-permute-done.11.refs_6_ = bf16[112,2048]{1,0:T(8,128)(2,1)} collective-permute-done((bf16[112,2048]{1,0:T(8,128)(2,1)S(1)}, bf16[112,2048]{1,0:T(8,128)(2,1)}, u32[]{:S(2)}, u32[]{:S(2)}) %collective-permute-start.11) | collective-permute-done | bytes 458784 | tf_op jit(solution)/shard_map/ppermute | solution.py:710
  108.0 32.0 %collective-permute-done.10.refs_9_.refs_11_ = bf16[256,1152]{1,0:T(8,128)(2,1)} collective-permute-done((bf16[256,1152]{1,0:T(8,128)(2,1)}, bf16[256,1152]{1,0:T(8,128)(2,1)}, u32[]{:S(2)}, u32[]{:S(2)}) %collective-permute-start.10) | collective-permute-done | bytes 589856 | tf_op jit(solution)/shard_map/ppermute | solution.py:710
  160.2 24.2 %forward.1 = (bf16[1024,960]{1,0:T(8,128)(2,1)}, bf16[1024,768]{1,0:T(8,128)(2,1)}, f32[1024,1408]{1,0:T(8,128)}, bf16[1024,2048]{1,0:T(8,128)(2,1)}) custom-call(bf16[1024,2048]{1,0:T(8,128)(2,1)} %all-gather.3.cloned.1.call-done.refs_0_.lhs_any, f32[8,768]{1,0:T(8,128)} %broadcast_in_dim.58.refs_1_, f32[1024,128]{1,0:T(8,128)} %copy.48.refs_2_.refs_3_, ...), custom_call_target="tpu_custom_call" | custom-call | flops 1 | bytes 1 | tf_op jit(solution)/shard_map/forward/pallas_call | solution.py:279
  184.7 5.2 %all-gather.5.cloned.1.call-done.masked_ref.refs_0_ = bf16[1024,2048]{1,0:T(8,128)(2,1)} async-done(((bf16[128,2048]{1,0:T(8,128)(2,1)}), bf16[1024,2048]{1,0:T(8,128)(2,1)}) %all-gather.5.cloned.1.call-update) | async-done | bytes 4194320 | tf_op jit(solution)/shard_map/all_gather | solution.py:615
  192.1 7.2 %mixer_grad.1 = (bf16[224,2048]{1,0:T(8,128)(2,1)}, bf16[256,2048]{1,0:T(8,128)(2,1)}, bf16[128,2048]{1,0:T(8,128)(2,1)}, bf16[112,2048]{1,0:T(8,128)(2,1)}, bf1...) custom-call(s32[1]{0:T(128)} %bitcast.15.lane_ref, bf16[1024,960]{1,0:T(8,128)(2,1)S(1)} %copy-done.2, ...), custom_call_target="tpu_custom_call" | custom-call | flops 1 | bytes 1 | tf_op jit(solution)/shard_map/mixer_grad/pallas_call | solution.py:444
  202.4 29.8 %backward.1 = (bf16[1024,768]{1,0:T(8,128)(2,1)}, bf16[1024,1408]{1,0:T(8,128)(2,1)}, bf16[1024,2048]{1,0:T(8,128)(2,1)}, f32[8,768]{1,0:T(8,128)}) custom-call(bf16[1024,2048]{1,0:T(8,128)(2,1)} %all-gather.5.cloned.1.call-done.masked_ref.refs_0_, f32[1024,1408]{1,0:T(8,128)} %get-tuple-element.161.refs_1_, bf16[1024,768]{1,0:T(8,128)(2,1)} %get-tuple-element.162.refs_2_, ...), custom_call_target="tpu_custom_call" | custom-call | flops 1 | bytes 1 | tf_op jit(solution)/shard_map/backward/pallas_call | solution.py:321
  232.9 7.5 %weight_grad.4 = (bf16[512,1408]{1,0:T(8,128)(2,1)}, bf16[512,1408]{1,0:T(8,128)(2,1)}) custom-call(s32[4]{0:T(128)S(1)} %copy-done.9, bf16[1024,2048]{1,0:T(8,128)(2,1)} %all-gather.3.cloned.1.call-done.refs_0_.lhs_any, bf16[1024,1408]{1,0:T(8,128)(2,1)} %get-tuple-element.169.grad_any), custom_call_target="tpu_custom_call" | custom-call | flops 1 | bytes 1 | tf_op jit(solution)/shard_map/weight_grad/pallas_call | solution.py:391
  241.5 7.5 %weight_grad.5 = (bf16[256,1408]{1,0:T(8,128)(2,1)}, bf16[256,1408]{1,0:T(8,128)(2,1)}, bf16[256,1408]{1,0:T(8,128)(2,1)}, bf16[256,1408]{1,0:T(8,128)(2,1)}) custom-call(s32[4]{0:T(128)S(1)} %copy-done.8, bf16[1024,2048]{1,0:T(8,128)(2,1)} %all-gather.3.cloned.1.call-done.refs_0_.lhs_any, bf16[1024,1408]{1,0:T(8,128)(2,1)} %get-tuple-element.169.grad_any), custom_call_target="tpu_custom_call" | custom-call | flops 1 | bytes 1 | tf_op jit(solution)/shard_map/weight_grad/pallas_call | solution.py:391
  248.9 5.4 %weight_grad.6 = (bf16[512,768]{1,0:T(8,128)(2,1)}, bf16[512,768]{1,0:T(8,128)(2,1)}) custom-call(s32[4]{0:T(128)S(1)} %copy-done.9, bf16[1024,2048]{1,0:T(8,128)(2,1)} %all-gather.3.cloned.1.call-done.refs_0_.lhs_any, bf16[1024,768]{1,0:T(8,128)(2,1)} %get-tuple-element.178.grad_any), custom_call_target="tpu_custom_call" | custom-call | flops 1 | bytes 1 | tf_op jit(solution)/shard_map/weight_grad/pallas_call | solution.py:391
  254.3 5.4 %weight_grad.7 = (bf16[256,768]{1,0:T(8,128)(2,1)}, bf16[256,768]{1,0:T(8,128)(2,1)}, bf16[256,768]{1,0:T(8,128)(2,1)}, bf16[256,768]{1,0:T(8,128)(2,1)}) custom-call(s32[4]{0:T(128)S(1)} %copy-done.8, bf16[1024,2048]{1,0:T(8,128)(2,1)} %all-gather.3.cloned.1.call-done.refs_0_.lhs_any, bf16[1024,768]{1,0:T(8,128)(2,1)} %get-tuple-element.178.grad_any), custom_call_target="tpu_custom_call" | custom-call | flops 1 | bytes 1 | tf_op jit(solution)/shard_map/weight_grad/pallas_call | solution.py:391
  262.0 11.8 %collective-permute-done.18 = bf16[512,1408]{1,0:T(8,128)(2,1)S(1)} collective-permute-done((bf16[512,1408]{1,0:T(8,128)(2,1)}, bf16[512,1408]{1,0:T(8,128)(2,1)S(1)}, u32[]{:S(2)}, u32[]{:S(2)}) %collective-permute-start.18) | collective-permute-done | bytes 1441824 | tf_op jit(solution)/shard_map/ppermute | solution.py:710
  279.8 12.3 %collective-permute-done.21 = bf16[256,1408]{1,0:T(8,128)(2,1)} collective-permute-done((bf16[256,1408]{1,0:T(8,128)(2,1)}, bf16[256,1408]{1,0:T(8,128)(2,1)}, u32[]{:S(2)}, u32[]{:S(2)}) %collective-permute-start.21) | collective-permute-done | bytes 720928 | tf_op jit(solution)/shard_map/ppermute | solution.py:710
  296.9 3.8 all-to-all-start.2
  315.9 3.1 fusion.14
  325.9 7.4 %collective-permute-done.25 = bf16[256,768]{1,0:T(8,128)(2,1)S(1)} collective-permute-done((bf16[256,768]{1,0:T(8,128)(2,1)}, bf16[256,768]{1,0:T(8,128)(2,1)S(1)}, u32[]{:S(2)}, u32[]{:S(2)}) %collective-permute-start.25) | collective-permute-done | bytes 393248 | tf_op jit(solution)/shard_map/ppermute | solution.py:710
  337.4 5.0 %all-to-all-start.3 = ((bf16[8,64,768]{2,1,0:T(8,128)(2,1)}), bf16[8,64,768]{2,1,0:T(8,128)(2,1)S(1)}, u32[]{:S(2)}, u32[]{:S(2)}) async-start(bf16[8,64,768]{2,1,0:T(8,128)(2,1)} %bitcast.22), calls=%async_computation.5 | async-start | bytes 1572864 | tf_op jit(solution)/shard_map/all_to_all | solution.py:629
  357.1 6.4 %collective-permute-done.31 = f32[320]{0:T(512)S(1)} collective-permute-done((f32[320]{0:T(512)S(1)}, f32[320]{0:T(512)S(1)}, u32[]{:S(2)}, u32[]{:S(2)}) %collective-permute-start.31) | collective-permute-done | bytes 1312 | tf_op jit(solution)/shard_map/ppermute | solution.py:710
  364.8 3.4 collective-permute-done.33
  (255 shorter events, 133.9 us)
Async XLA Ops:
  13.3 35.9 %all-to-all-start = ((bf16[8,64,1152]{2,1,0:T(8,128)(2,1)}), bf16[8,64,1152]{2,1,0:T(8,128)(2,1)S(1)}, u32[]{:S(2)}, u32[]{:S(2)}) async-start(bf16[8,64,1152]{2,1,0:T(8,128)(2,1)} %bitcast.2), calls=%async_computation | async-start | bytes 2359296 | tf_op jit(solution)/shard_map/all_to_all | solution.py:629
  19.8 24.3 %collective-permute-start.1 = (bf16[240,2048]{1,0:T(8,128)(2,1)S(1)}, bf16[240,2048]{1,0:T(8,128)(2,1)}, u32[]{:S(2)}, u32[]{:S(2)}) collective-permute-start(bf16[240,2048]{1,0:T(8,128)(2,1)S(1)} %join_rows.1), channel_id=1, source_target_pairs={{0,4},{1,5},{2,6},{3,7},{4,0},{5,1},{6,2},{7,3},{8,12},{9,13},{10,... | collective-permute-start | bytes 2949128 | tf_op jit(solution)/shard_map/ppermute | solution.py:710
  21.3 24.0 %collective-permute-start = (bf16[240,2048]{1,0:T(8,128)(2,1)S(1)}, bf16[240,2048]{1,0:T(8,128)(2,1)}, u32[]{:S(2)}, u32[]{:S(2)}) collective-permute-start(bf16[240,2048]{1,0:T(8,128)(2,1)S(1)} %join_rows.1), channel_id=1, source_target_pairs={{0,2},{1,3},{2,0},{3,1},{4,6},{5,7},{6,4},{7,5},{8,10},{9,11},{10,... | collective-permute-start | bytes 2949128 | tf_op jit(solution)/shard_map/ppermute | solution.py:710
  22.8 44.6 %collective-permute-start.6 = (s32[1,4]{1,0:T(1,128)S(1)}, s32[1,4]{1,0:T(1,128)S(1)}, u32[]{:S(2)}, u32[]{:S(2)}) collective-permute-start(s32[1,4]{1,0:T(1,128)S(1)} %copy-done.34), channel_id=1, source_target_pairs={{0,24},{1,25},{2,26},{3,27},{4,28},{5,29},{6,30},{7,31},{8,16},{9,... | collective-permute-start | bytes 56 | tf_op jit(solution)/shard_map/ppermute | solution.py:710
  26.6 40.8 %collective-permute-start.5 = (s32[1,4]{1,0:T(1,128)S(1)}, s32[1,4]{1,0:T(1,128)S(1)}, u32[]{:S(2)}, u32[]{:S(2)}) collective-permute-start(s32[1,4]{1,0:T(1,128)S(1)} %copy-done.34), channel_id=1, source_target_pairs={{0,16},{1,17},{2,18},{3,19},{4,20},{5,21},{6,22},{7,23},{8,24},{9,... | collective-permute-start | bytes 56 | tf_op jit(solution)/shard_map/ppermute | solution.py:710
  26.6 40.8 %collective-permute-start.4 = (s32[1,4]{1,0:T(1,128)S(1)}, s32[1,4]{1,0:T(1,128)S(1)}, u32[]{:S(2)}, u32[]{:S(2)}) collective-permute-start(s32[1,4]{1,0:T(1,128)S(1)} %copy-done.34), channel_id=1, source_target_pairs={{0,8},{1,9},{2,10},{3,11},{4,12},{5,13},{6,14},{7,15},{8,0},{9,1},... | collective-permute-start | bytes 56 | tf_op jit(solution)/shard_map/ppermute | solution.py:710
  49.2 35.7 %all-to-all-start.1 = ((bf16[8,64,1024]{2,1,0:T(8,128)(2,1)}), bf16[8,64,1024]{2,1,0:T(8,128)(2,1)}, u32[]{:S(2)}, u32[]{:S(2)}) async-start(bf16[8,64,1024]{2,1,0:T(8,128)(2,1)} %bitcast.4), calls=%async_computation.1 | async-start | bytes 2097152 | tf_op jit(solution)/shard_map/all_to_all | solution.py:629
  53.5 106.1 %all-gather.3.cloned.1.call-start = ((), (), s32[]{:S(2)}) async-start(), calls=%async_computation.6 | async-start | bytes 4718592 | tf_op jit(solution)/shard_map/all_gather | solution.py:615
  55.4 28.2 %collective-permute-start.3 = (bf16[512,1152]{1,0:T(8,128)(2,1)S(1)}, bf16[512,1152]{1,0:T(8,128)(2,1)S(1)}, u32[]{:S(2)}, u32[]{:S(2)}) collective-permute-start(bf16[512,1152]{1,0:T(8,128)(2,1)S(1)} %bitcast.49), channel_id=1, source_target_pairs={{0,4},{1,5},{2,6},{3,7},{4,0},{5,1},{6,2},{7,3},{8,12},{9,13},{10,... | collective-permute-start | bytes 3538952 | tf_op jit(solution)/shard_map/ppermute | solution.py:710
  56.9 28.0 %collective-permute-start.2 = (bf16[512,1152]{1,0:T(8,128)(2,1)S(1)}, bf16[512,1152]{1,0:T(8,128)(2,1)}, u32[]{:S(2)}, u32[]{:S(2)}) collective-permute-start(bf16[512,1152]{1,0:T(8,128)(2,1)S(1)} %bitcast.50), channel_id=1, source_target_pairs={{0,2},{1,3},{2,0},{3,1},{4,6},{5,7},{6,4},{7,5},{8,10},{9,11},{10,... | collective-permute-start | bytes 3538952 | tf_op jit(solution)/shard_map/ppermute | solution.py:710
  85.0 105.0 %all-gather.5.cloned.1.call-start = ((), (), s32[]{:S(2)}) async-start(), calls=%async_computation.8 | async-start | bytes 4718592 | tf_op jit(solution)/shard_map/all_gather | solution.py:615
  93.5 46.6 %collective-permute-start.8 = (bf16[512,1024]{1,0:T(8,128)(2,1)}, bf16[512,1024]{1,0:T(8,128)(2,1)}, u32[]{:S(2)}, u32[]{:S(2)}) collective-permute-start(bf16[512,1024]{1,0:T(8,128)(2,1)} %bitcast.5.refs_10_.refs_12_), channel_id=1, source_target_pairs={{0,4},{1,5},{2,6},{3,7},{4,0},{5,1},{6,2},{7,3},{8,12},{9,13},{10,... | collective-permute-start | bytes 3145736 | tf_op jit(solution)/shard_map/ppermute | solution.py:710
  95.0 45.1 %collective-permute-start.7 = (bf16[512,1024]{1,0:T(8,128)(2,1)}, bf16[512,1024]{1,0:T(8,128)(2,1)}, u32[]{:S(2)}, u32[]{:S(2)}) collective-permute-start(bf16[512,1024]{1,0:T(8,128)(2,1)} %bitcast.5.refs_10_.refs_12_), channel_id=1, source_target_pairs={{0,2},{1,3},{2,0},{3,1},{4,6},{5,7},{6,4},{7,5},{8,10},{9,11},{10,... | collective-permute-start | bytes 3145736 | tf_op jit(solution)/shard_map/ppermute | solution.py:710
  98.3 41.7 %collective-permute-start.10 = (bf16[256,1152]{1,0:T(8,128)(2,1)}, bf16[256,1152]{1,0:T(8,128)(2,1)}, u32[]{:S(2)}, u32[]{:S(2)}) collective-permute-start(bf16[256,1152]{1,0:T(8,128)(2,1)} %slice.90), channel_id=1, source_target_pairs={{0,2},{1,3},{2,0},{3,1},{4,6},{5,7},{6,4},{7,5},{8,10},{9,11},{10,... | collective-permute-start | bytes 1769480 | tf_op jit(solution)/shard_map/ppermute | solution.py:710
  105.0 35.0 %collective-permute-start.9 = (bf16[256,1152]{1,0:T(8,128)(2,1)}, bf16[256,1152]{1,0:T(8,128)(2,1)}, u32[]{:S(2)}, u32[]{:S(2)}) collective-permute-start(bf16[256,1152]{1,0:T(8,128)(2,1)} %slice.89), channel_id=1, source_target_pairs={{0,4},{1,5},{2,6},{3,7},{4,0},{5,1},{6,2},{7,3},{8,12},{9,13},{10,... | collective-permute-start | bytes 1769480 | tf_op jit(solution)/shard_map/ppermute | solution.py:710
  141.8 118.0 %reduce-scatter.3.cloned.1.call-start = ((), (), s32[]{:S(2)}) async-start(), calls=%async_computation.7 | async-start | bytes 4718592 | tf_op jit(solution)/shard_map/reduce_scatter | solution.py:620
  184.5 117.7 %reduce-scatter.5.cloned.1.call-start = ((), (), s32[]{:S(2)}) async-start(), calls=%async_computation.9 | async-start | bytes 4718592 | tf_op jit(solution)/shard_map/reduce_scatter | solution.py:620
  199.3 32.9 %collective-permute-start.17 = (bf16[256,2048]{1,0:T(8,128)(2,1)}, bf16[256,2048]{1,0:T(8,128)(2,1)}, u32[]{:S(2)}, u32[]{:S(2)}) collective-permute-start(bf16[256,2048]{1,0:T(8,128)(2,1)} %get-tuple-element.159), channel_id=1, source_target_pairs={{0,4},{1,5},{2,6},{3,7},{4,0},{5,1},{6,2},{7,3},{8,12},{9,13},{10,... | collective-permute-start | bytes 3145736 | tf_op jit(solution)/shard_map/ppermute | solution.py:710
  200.9 31.3 %collective-permute-start.16 = (bf16[224,2048]{1,0:T(8,128)(2,1)}, bf16[224,2048]{1,0:T(8,128)(2,1)}, u32[]{:S(2)}, u32[]{:S(2)}) collective-permute-start(bf16[224,2048]{1,0:T(8,128)(2,1)} %get-tuple-element.158), channel_id=1, source_target_pairs={{0,2},{1,3},{2,0},{3,1},{4,6},{5,7},{6,4},{7,5},{8,10},{9,11},{10,... | collective-permute-start | bytes 2752520 | tf_op jit(solution)/shard_map/ppermute | solution.py:710
  240.4 33.4 %collective-permute-start.18 = (bf16[512,1408]{1,0:T(8,128)(2,1)}, bf16[512,1408]{1,0:T(8,128)(2,1)S(1)}, u32[]{:S(2)}, u32[]{:S(2)}) collective-permute-start(bf16[512,1408]{1,0:T(8,128)(2,1)} %get-tuple-element.180), channel_id=1, source_target_pairs={{0,2},{1,3},{2,0},{3,1},{4,6},{5,7},{6,4},{7,5},{8,10},{9,11},{10,... | collective-permute-start | bytes 4325384 | tf_op jit(solution)/shard_map/ppermute | solution.py:710
  240.9 33.1 %collective-permute-start.19 = (bf16[512,1408]{1,0:T(8,128)(2,1)}, bf16[512,1408]{1,0:T(8,128)(2,1)S(1)}, u32[]{:S(2)}, u32[]{:S(2)}) collective-permute-start(bf16[512,1408]{1,0:T(8,128)(2,1)} %get-tuple-element.181), channel_id=1, source_target_pairs={{0,4},{1,5},{2,6},{3,7},{4,0},{5,1},{6,2},{7,3},{8,12},{9,13},{10,... | collective-permute-start | bytes 4325384 | tf_op jit(solution)/shard_map/ppermute | solution.py:710
  296.9 40.3 %all-to-all-start.2 = ((bf16[8,64,1408]{2,1,0:T(8,128)(2,1)}), bf16[8,64,1408]{2,1,0:T(8,128)(2,1)S(1)}, u32[]{:S(2)}, u32[]{:S(2)}) async-start(bf16[8,64,1408]{2,1,0:T(8,128)(2,1)} %bitcast.20), calls=%async_computation.4 | async-start | bytes 2883584 | tf_op jit(solution)/shard_map/all_to_all | solution.py:629
  300.7 19.9 %collective-permute-start.22 = (bf16[512,768]{1,0:T(8,128)(2,1)}, bf16[512,768]{1,0:T(8,128)(2,1)}, u32[]{:S(2)}, u32[]{:S(2)}) collective-permute-start(bf16[512,768]{1,0:T(8,128)(2,1)} %get-tuple-element.191), channel_id=1, source_target_pairs={{0,2},{1,3},{2,0},{3,1},{4,6},{5,7},{6,4},{7,5},{8,10},{9,11},{10,... | collective-permute-start | bytes 2359304 | tf_op jit(solution)/shard_map/ppermute | solution.py:710
  337.4 34.2 %all-to-all-start.3 = ((bf16[8,64,768]{2,1,0:T(8,128)(2,1)}), bf16[8,64,768]{2,1,0:T(8,128)(2,1)S(1)}, u32[]{:S(2)}, u32[]{:S(2)}) async-start(bf16[8,64,768]{2,1,0:T(8,128)(2,1)} %bitcast.22), calls=%async_computation.5 | async-start | bytes 1572864 | tf_op jit(solution)/shard_map/all_to_all | solution.py:629
  (54 other events, 546.9 us)
Sparse Core Ops, SparseCore 0:
  85.1 47.3 all-gather.2
  141.9 47.9 all-gather.4
  192.2 48.7 reduce-scatter.2
  243.1 48.1 reduce-scatter.4
where the time goes:
time: 383 us; the launch traced here: 381 us
  waiting for transfers between devices  126 us (33%)
  Pallas kernels  95.5 us (25%)
  starting transfers between devices  58.3 us (15%)
  other arithmetic  44 us (11%)
  local copies, waits for them, and re-layouts  42.8 us (11%)
  between operations  14.5 us (4%)
    ppermute x35, waiting for transfers between devices, send(): return lax.ppermute(value, AXES, pairs)  116 us
    ppermute x35, starting transfers between devices, send(): return lax.ppermute(value, AXES, pairs)  38.5 us
    pallas_call x1, Pallas kernels, backward_call(): pl.pallas_call(functools.partial(backward_kernel, sizes, count, block), g...  29.8 us
    pallas_call x4, Pallas kernels, product_call(): pl.pallas_call(kernel, in_specs=[pl.BlockSpec(memory_space=pltpu.SMEM), A...  25.7 us
    pallas_call x1, Pallas kernels, forward_call(): pl.pallas_call(functools.partial(forward_kernel, sizes, count, block), gr...  24.2 us
    all_to_all x4, starting transfers between devices, exchange(): lax.all_to_all(part, self.token_axes, split_axis=0, concat_axis=0, tiled=...  19.5 us
    unnamed x74, local copies, waits for them, and re-layouts  8.15 us
  transfers between devices with their start and end apart: 43, of which 20 were waited for; matrix products, arithmetic and copies ran while one was open for 20% of the time, Pallas kernels for 24%

commit v1 on v0

--- a/solution.py
+++ b/solution.py
@@ -495,7 +495,7 @@
 def pack_call(arrays, plan, tp, widths):
     rows = arrays[0].shape[0]
     total = sum(widths)
-    edge = (total // 2 + TILE - 1) // TILE * TILE
+    edge = total // 2 // TILE * TILE
     return pl.pallas_call(
         functools.partial(pack_kernel, plan, tp, (0, widths[0], total - widths[0])),
         in_specs=[HELD] * 3,
@@ -730,23 +730,21 @@
         left, right, mix_x, mix_y = tie(left, right, mix_x, mix_y)
         left_x, left_y = self.send(left, 1), self.send(left, 2)
         right = self.exchange(right)
-        right, left_x, left_y, normed, masked, lengths = tie(
-            right, left_x, left_y, normed, masked, lengths
-        )
+        halves = [part for b in (rows, mix_x, mix_y) for part in (b[:cut], b[cut:])]
+        right, left_x, left_y, normed, masked, lengths, *halves = tie(
+            right, left_x, left_y, normed, masked, lengths, *halves
+        )
+        normed_all, masked_all = self.gather_tokens(normed), self.gather_tokens(masked)
+        right_x, right_y = self.send(right, 1), self.send(right, 2)
+        mix_low, mix_high = self.send(halves[2], 2), self.send(halves[5], 1)
+        left_low, left_high = self.send(left_x[:half], 2), self.send(left_y[half:], 1)
         tables = make_tables(self.order_lengths(lengths, self.send(lengths, dc=1)))
-        normed_all = self.gather_tokens(normed)
-        right_x, right_y = self.send(right, 1), self.send(right, 2)
-        left_low, left_high = self.send(left_x[:half], 2), self.send(left_y[half:], 1)
-        mix_low, mix_high = self.send(mix_x[:cut], 2), self.send(mix_y[cut:], 1)
-        halves = [part for b in (rows, mix_x, mix_y) for part in (b[:cut], b[cut:])]
-        right_x, right_y, left_low, left_high, mix_low, mix_high, masked, *others = tie(
-            right_x, right_y, left_low, left_high, mix_low, mix_high, masked, *halves, *tables
-        )
-        halves, tables = others[: len(halves)], others[len(halves) :]
-        masked_all = self.gather_tokens(masked)
-        right_low, right_high = self.send(right_x[:half], 2), self.send(right_y[half:], 1)
         halves += [mix_low, mix_high]
         mixer = place_call(self.lane_index, halves, self.wide, own, own_ff, cut)
+        right_x, right_y, left_low, left_high, mixer, *tables = tie(
+            right_x, right_y, left_low, left_high, *kept(mixer, *tables)
+        )
+        right_low, right_high = self.send(right_x[:half], 2), self.send(right_y[half:], 1)
         entry = [left, left_x, left_y, left_low, left_high]
         entry += [right, right_x, right_y, right_low, right_high]
         return entry, mixer, normed_all, masked_all, tables
@@ -800,10 +798,9 @@
         *qkv_first, grad_tokens, stats = tie(*qkv_first, *results)
         qkv_last = self.last_sends(qkv_first, qkv_x, qkv_y)
         part_qkv = self.joined_sum((qkv_x, qkv_y, qkv_low, qkv_high), qkv_first, qkv_last)
-        part_ff, part_qkv, stats = tie(part_ff, part_qkv, stats)
+        part_ff, part_qkv, stats, *mix = tie(part_ff, part_qkv, stats, *mix_first, *mix[2:])
         part_qkv = self.exchange(part_qkv)
         stats = self.chip_stats(stats)
-        stats, *mix = tie(stats, *mix_first, *mix[2:])
         mix_first, mix = mix[:2], mix[2:]
         mix_last = self.last_sends(mix_first, mix[0], mix[1])
         stats = self.scatter_stats(stats)
@@ -874,11 +871,18 @@
     lengths = seq_lengths
     arrays = [w_qkv, w_gate, w_up]
 
+    bias = lax.dynamic_index_in_dim(
+        jnp.transpose(b_qkv.reshape(3, outer, wide, cores, own), (1, 3, 0, 2, 4)).reshape(tp, -1),
+        net.member,
+        0,
+    )
+    bias = jnp.broadcast_to(bias, (8, 3 * cols))
+
     def make_tables(lengths):
         position, _, allowed = jax.vmap(lambda row: block_terms(row, rows_tok))(lengths)
-        return [*turn_tables(position), jnp.where(allowed, 0.0, NEG)]
-
-    entry, mixer, normed_all, masked_all, (cos_t, sin_t, mask) = net.inputs(
+        return [*turn_tables(position), jnp.where(allowed, 0.0, NEG), bias]
+
+    entry, mixer, normed_all, masked_all, (cos_t, sin_t, mask, bias) = net.inputs(
         pack_call(arrays, plan, tp, widths),
         w_out,
         w_down,
@@ -887,13 +891,6 @@
         lengths,
         make_tables,
     )
-    bias = lax.dynamic_index_in_dim(
-        jnp.transpose(b_qkv.reshape(3, outer, wide, cores, own), (1, 3, 0, 2, 4)).reshape(tp, -1),
-        net.member,
-        0,
-    )
-    bias = jnp.broadcast_to(bias, (8, 3 * cols))
-
     sizes = (cols, main, rest)
     joined, qkv, proj_ff, branch = forward_call(
         normed_all, bias, cos_t, sin_t, mask, entry, mixer, sizes

time: 383 us -> 364 us (0.950)
  other arithmetic: 44 us -> 33.6 us
  local copies, waits for them, and re-layouts: 42.8 us -> 36.7 us
  waiting for transfers between devices: 126 us -> 120 us
  starting transfers between devices: 58.3 us -> 62.6 us
    all_gather x2, waiting for transfers between devices: 5.21 us -> 0.02 us  [gather_tokens(): lax.all_gather(block, self.token_axes, axis=0, tiled=True, axis_index_gro...]
    ppermute x35, starting transfers between devices: 38.5 us -> 42.8 us  [send(): return lax.ppermute(value, AXES, pairs)]
    unnamed x74 -> x82, local copies, waits for them, and re-layouts: 8.15 us -> 10.6 us
  transfers between devices with their start and end apart: 43 -> 43, of which waited for: 20 -> 20; matrix products, arithmetic and copies ran while one was open for 20% -> 16% of each run, Pallas kernels for 24% -> 25%
where the time goes in v1:
time: 364 us; the launch traced here: 362 us
  waiting for transfers between devices  120 us (33%)
  Pallas kernels  95 us (26%)
  starting transfers between devices  62.6 us (17%)
  local copies, waits for them, and re-layouts  36.7 us (10%)
  other arithmetic  33.6 us (9%)
  between operations  14.7 us (4%)
    ppermute x35, waiting for transfers between devices, send(): return lax.ppermute(value, AXES, pairs)  117 us
    ppermute x35, starting transfers between devices, send(): return lax.ppermute(value, AXES, pairs)  42.8 us
    pallas_call x1, Pallas kernels, backward_call(): pl.pallas_call(functools.partial(backward_kernel, sizes, count, block), g...  29.8 us
    pallas_call x4, Pallas kernels, product_call(): pl.pallas_call(kernel, in_specs=[pl.BlockSpec(memory_space=pltpu.SMEM), A...  25.8 us
    pallas_call x1, Pallas kernels, forward_call(): pl.pallas_call(functools.partial(forward_kernel, sizes, count, block), gr...  24.2 us
    all_to_all x4, starting transfers between devices, exchange(): lax.all_to_all(part, self.token_axes, split_axis=0, concat_axis=0, tiled=...  19.5 us
    unnamed x82, local copies, waits for them, and re-layouts  10.6 us
  transfers between devices with their start and end apart: 43, of which 20 were waited for; matrix products, arithmetic and copies ran while one was open for 16% of the time, Pallas kernels for 25%

profile of v1, /device:TPU:0, one launch (start us, length us, event | category | flops | bytes accessed | tf_op | source)
XLA Modules:
  0.0 362.1 jit_solution(8687554834211737943)
XLA Ops:
  13.3 6.5 %all-to-all-start = ((bf16[8,64,1024]{2,1,0:T(8,128)(2,1)}), bf16[8,64,1024]{2,1,0:T(8,128)(2,1)}, u32[]{:S(2)}, u32[]{:S(2)}) async-start(bf16[8,64,1024]{2,1,0:T(8,128)(2,1)} %bitcast.2), calls=%async_computation | async-start | bytes 2097152 | tf_op jit(solution)/shard_map/all_to_all | solution.py:629
  22.8 3.8 %collective-permute-start.6 = (s32[1,4]{1,0:T(1,128)S(1)}, s32[1,4]{1,0:T(1,128)S(1)}, u32[]{:S(2)}, u32[]{:S(2)}) collective-permute-start(s32[1,4]{1,0:T(1,128)S(1)} %copy-done.38), channel_id=1, source_target_pairs={{0,24},{1,25},{2,26},{3,27},{4,28},{5,29},{6,30},{7,31},{8,16},{9,... | collective-permute-start | bytes 56 | tf_op jit(solution)/shard_map/ppermute | solution.py:710
  27.7 16.3 %collective-permute-done.1 = bf16[240,2048]{1,0:T(8,128)(2,1)S(1)} collective-permute-done((bf16[240,2048]{1,0:T(8,128)(2,1)S(1)}, bf16[240,2048]{1,0:T(8,128)(2,1)S(1)}, u32[]{:S(2)}, u32[]{:S(2)}) %collective-permute-start.1) | collective-permute-done | bytes 983072 | tf_op jit(solution)/shard_map/ppermute | solution.py:710
  46.5 4.3 %all-to-all-start.1 = ((bf16[8,64,1152]{2,1,0:T(8,128)(2,1)}), bf16[8,64,1152]{2,1,0:T(8,128)(2,1)}, u32[]{:S(2)}, u32[]{:S(2)}) async-start(bf16[8,64,1152]{2,1,0:T(8,128)(2,1)} %bitcast.4), calls=%async_computation.1 | async-start | bytes 2359296 | tf_op jit(solution)/shard_map/all_to_all | solution.py:629
  61.5 16.5 %collective-permute-done.3.refs_7_.refs_9_ = bf16[512,1024]{1,0:T(8,128)(2,1)} collective-permute-done((bf16[512,1024]{1,0:T(8,128)(2,1)}, bf16[512,1024]{1,0:T(8,128)(2,1)}, u32[]{:S(2)}, u32[]{:S(2)}) %collective-permute-start.3) | collective-permute-done | bytes 1048608 | tf_op jit(solution)/shard_map/ppermute | solution.py:710
  93.3 28.2 %collective-permute-done.11.refs_6_ = bf16[112,2048]{1,0:T(8,128)(2,1)S(1)} collective-permute-done((bf16[112,2048]{1,0:T(8,128)(2,1)S(1)}, bf16[112,2048]{1,0:T(8,128)(2,1)S(1)}, u32[]{:S(2)}, u32[]{:S(2)}) %collective-permute-start.11) | collective-permute-done | bytes 458784 | tf_op jit(solution)/shard_map/ppermute | solution.py:710
  124.8 9.3 %collective-permute-done.12.refs_7_ = bf16[128,2048]{1,0:T(8,128)(2,1)S(1)} collective-permute-done((bf16[128,2048]{1,0:T(8,128)(2,1)S(1)}, bf16[128,2048]{1,0:T(8,128)(2,1)S(1)}, u32[]{:S(2)}, u32[]{:S(2)}) %collective-permute-start.12) | collective-permute-done | bytes 524320 | tf_op jit(solution)/shard_map/ppermute | solution.py:710
  143.8 9.3 %collective-permute-done.15.refs_14_.refs_16_ = bf16[256,1152]{1,0:T(8,128)(2,1)S(1)} collective-permute-done((bf16[256,1152]{1,0:T(8,128)(2,1)}, bf16[256,1152]{1,0:T(8,128)(2,1)S(1)}, u32[]{:S(2)}, u32[]{:S(2)}) %collective-permute-start.15) | collective-permute-done | bytes 589856 | tf_op jit(solution)/shard_map/ppermute | solution.py:710
  154.8 24.2 %forward.1 = (bf16[1024,960]{1,0:T(8,128)(2,1)}, bf16[1024,768]{1,0:T(8,128)(2,1)}, f32[1024,1408]{1,0:T(8,128)}, bf16[1024,2048]{1,0:T(8,128)(2,1)}) custom-call(bf16[1024,2048]{1,0:T(8,128)(2,1)} %all-gather.3.cloned.1.call-done.refs_0_.lhs_any, f32[8,768]{1,0:T(8,128)} %broadcast_in_dim.101.refs_1_, f32[1024,128]{1,0:T(8,128)} %copy.48.refs_2_.refs_3_, ...), custom_call_target="tpu_custom_call" | custom-call | flops 1 | bytes 1 | tf_op jit(solution)/shard_map/forward/pallas_call | solution.py:279
  183.2 7.2 %mixer_grad.1 = (bf16[224,2048]{1,0:T(8,128)(2,1)}, bf16[256,2048]{1,0:T(8,128)(2,1)}, bf16[128,2048]{1,0:T(8,128)(2,1)}, bf16[112,2048]{1,0:T(8,128)(2,1)}, bf1...) custom-call(s32[1]{0:T(128)} %bitcast.8.lane_ref, bf16[1024,960]{1,0:T(8,128)(2,1)S(1)} %copy-done.2, ...), custom_call_target="tpu_custom_call" | custom-call | flops 1 | bytes 1 | tf_op jit(solution)/shard_map/mixer_grad/pallas_call | solution.py:444
  191.0 29.8 %backward.1 = (bf16[1024,768]{1,0:T(8,128)(2,1)}, bf16[1024,1408]{1,0:T(8,128)(2,1)}, bf16[1024,2048]{1,0:T(8,128)(2,1)}, f32[8,768]{1,0:T(8,128)}) custom-call(bf16[1024,2048]{1,0:T(8,128)(2,1)} %all-gather.5.cloned.1.call-done.masked_ref.refs_0_, f32[1024,1408]{1,0:T(8,128)} %get-tuple-element.158.refs_1_, bf16[1024,768]{1,0:T(8,128)(2,1)} %get-tuple-element.159.refs_2_, ...), custom_call_target="tpu_custom_call" | custom-call | flops 1 | bytes 1 | tf_op jit(solution)/shard_map/backward/pallas_call | solution.py:321
  223.4 7.5 %weight_grad.4 = (bf16[512,1408]{1,0:T(8,128)(2,1)}, bf16[512,1408]{1,0:T(8,128)(2,1)}) custom-call(s32[4]{0:T(128)S(1)} %copy-done.9, bf16[1024,2048]{1,0:T(8,128)(2,1)} %all-gather.3.cloned.1.call-done.refs_0_.lhs_any, bf16[1024,1408]{1,0:T(8,128)(2,1)} %get-tuple-element.166.grad_any), custom_call_target="tpu_custom_call" | custom-call | flops 1 | bytes 1 | tf_op jit(solution)/shard_map/weight_grad/pallas_call | solution.py:391
  234.5 7.5 %weight_grad.5 = (bf16[256,1408]{1,0:T(8,128)(2,1)}, bf16[256,1408]{1,0:T(8,128)(2,1)}, bf16[256,1408]{1,0:T(8,128)(2,1)}, bf16[256,1408]{1,0:T(8,128)(2,1)}) custom-call(s32[4]{0:T(128)S(1)} %copy-done.8, bf16[1024,2048]{1,0:T(8,128)(2,1)} %all-gather.3.cloned.1.call-done.refs_0_.lhs_any, bf16[1024,1408]{1,0:T(8,128)(2,1)} %get-tuple-element.166.grad_any), custom_call_target="tpu_custom_call" | custom-call | flops 1 | bytes 1 | tf_op jit(solution)/shard_map/weight_grad/pallas_call | solution.py:391
  242.0 5.5 %weight_grad.6 = (bf16[512,768]{1,0:T(8,128)(2,1)}, bf16[512,768]{1,0:T(8,128)(2,1)}) custom-call(s32[4]{0:T(128)S(1)} %copy-done.9, bf16[1024,2048]{1,0:T(8,128)(2,1)} %all-gather.3.cloned.1.call-done.refs_0_.lhs_any, bf16[1024,768]{1,0:T(8,128)(2,1)} %get-tuple-element.175.grad_any), custom_call_target="tpu_custom_call" | custom-call | flops 1 | bytes 1 | tf_op jit(solution)/shard_map/weight_grad/pallas_call | solution.py:391
  247.4 5.4 %weight_grad.7 = (bf16[256,768]{1,0:T(8,128)(2,1)}, bf16[256,768]{1,0:T(8,128)(2,1)}, bf16[256,768]{1,0:T(8,128)(2,1)}, bf16[256,768]{1,0:T(8,128)(2,1)}) custom-call(s32[4]{0:T(128)S(1)} %copy-done.8, bf16[1024,2048]{1,0:T(8,128)(2,1)} %all-gather.3.cloned.1.call-done.refs_0_.lhs_any, bf16[1024,768]{1,0:T(8,128)(2,1)} %get-tuple-element.175.grad_any), custom_call_target="tpu_custom_call" | custom-call | flops 1 | bytes 1 | tf_op jit(solution)/shard_map/weight_grad/pallas_call | solution.py:391
  255.1 6.4 %collective-permute-done.18 = bf16[512,1408]{1,0:T(8,128)(2,1)S(1)} collective-permute-done((bf16[512,1408]{1,0:T(8,128)(2,1)}, bf16[512,1408]{1,0:T(8,128)(2,1)S(1)}, u32[]{:S(2)}, u32[]{:S(2)}) %collective-permute-start.18) | collective-permute-done | bytes 1441824 | tf_op jit(solution)/shard_map/ppermute | solution.py:710
  268.2 8.7 %collective-permute-done.21 = bf16[256,1408]{1,0:T(8,128)(2,1)} collective-permute-done((bf16[256,1408]{1,0:T(8,128)(2,1)S(1)}, bf16[256,1408]{1,0:T(8,128)(2,1)}, u32[]{:S(2)}, u32[]{:S(2)}) %collective-permute-start.21) | collective-permute-done | bytes 720928 | tf_op jit(solution)/shard_map/ppermute | solution.py:710
  281.3 3.8 %all-to-all-start.2 = ((bf16[8,64,1408]{2,1,0:T(8,128)(2,1)}), bf16[8,64,1408]{2,1,0:T(8,128)(2,1)S(1)}, u32[]{:S(2)}, u32[]{:S(2)}) async-start(bf16[8,64,1408]{2,1,0:T(8,128)(2,1)} %bitcast.20), calls=%async_computation.4 | async-start | bytes 2883584 | tf_op jit(solution)/shard_map/all_to_all | solution.py:629
  291.6 2.7 reshape.221
  301.1 3.1 fusion.14
  311.5 6.6 %collective-permute-done.25 = bf16[256,768]{1,0:T(8,128)(2,1)S(1)} collective-permute-done((bf16[256,768]{1,0:T(8,128)(2,1)}, bf16[256,768]{1,0:T(8,128)(2,1)S(1)}, u32[]{:S(2)}, u32[]{:S(2)}) %collective-permute-start.25) | collective-permute-done | bytes 393248 | tf_op jit(solution)/shard_map/ppermute | solution.py:710
  321.9 5.0 %all-to-all-start.3 = ((bf16[8,64,768]{2,1,0:T(8,128)(2,1)}), bf16[8,64,768]{2,1,0:T(8,128)(2,1)S(1)}, u32[]{:S(2)}, u32[]{:S(2)}) async-start(bf16[8,64,768]{2,1,0:T(8,128)(2,1)} %bitcast.22), calls=%async_computation.5 | async-start | bytes 1572864 | tf_op jit(solution)/shard_map/all_to_all | solution.py:629
  333.9 3.0 collective-permute-start.31
  341.8 6.3 %collective-permute-done.31 = f32[320]{0:T(512)S(1)} collective-permute-done((f32[320]{0:T(512)S(1)}, f32[320]{0:T(512)S(1)}, u32[]{:S(2)}, u32[]{:S(2)}) %collective-permute-start.31) | collective-permute-done | bytes 1312 | tf_op jit(solution)/shard_map/ppermute | solution.py:710
  (263 shorter events, 120.8 us)
Async XLA Ops:
  13.3 33.2 %all-to-all-start = ((bf16[8,64,1024]{2,1,0:T(8,128)(2,1)}), bf16[8,64,1024]{2,1,0:T(8,128)(2,1)}, u32[]{:S(2)}, u32[]{:S(2)}) async-start(bf16[8,64,1024]{2,1,0:T(8,128)(2,1)} %bitcast.2), calls=%async_computation | async-start | bytes 2097152 | tf_op jit(solution)/shard_map/all_to_all | solution.py:629
  19.8 24.2 %collective-permute-start.1 = (bf16[240,2048]{1,0:T(8,128)(2,1)S(1)}, bf16[240,2048]{1,0:T(8,128)(2,1)S(1)}, u32[]{:S(2)}, u32[]{:S(2)}) collective-permute-start(bf16[240,2048]{1,0:T(8,128)(2,1)S(1)} %join_rows.1), channel_id=1, source_target_pairs={{0,4},{1,5},{2,6},{3,7},{4,0},{5,1},{6,2},{7,3},{8,12},{9,13},{10,... | collective-permute-start | bytes 2949128 | tf_op jit(solution)/shard_map/ppermute | solution.py:710
  21.3 24.0 %collective-permute-start = (bf16[240,2048]{1,0:T(8,128)(2,1)S(1)}, bf16[240,2048]{1,0:T(8,128)(2,1)}, u32[]{:S(2)}, u32[]{:S(2)}) collective-permute-start(bf16[240,2048]{1,0:T(8,128)(2,1)S(1)} %join_rows.1), channel_id=1, source_target_pairs={{0,2},{1,3},{2,0},{3,1},{4,6},{5,7},{6,4},{7,5},{8,10},{9,11},{10,... | collective-permute-start | bytes 2949128 | tf_op jit(solution)/shard_map/ppermute | solution.py:710
  22.8 35.3 %collective-permute-start.6 = (s32[1,4]{1,0:T(1,128)S(1)}, s32[1,4]{1,0:T(1,128)S(1)}, u32[]{:S(2)}, u32[]{:S(2)}) collective-permute-start(s32[1,4]{1,0:T(1,128)S(1)} %copy-done.38), channel_id=1, source_target_pairs={{0,24},{1,25},{2,26},{3,27},{4,28},{5,29},{6,30},{7,31},{8,16},{9,... | collective-permute-start | bytes 56 | tf_op jit(solution)/shard_map/ppermute | solution.py:710
  26.6 31.4 %collective-permute-start.5 = (s32[1,4]{1,0:T(1,128)S(1)}, s32[1,4]{1,0:T(1,128)S(1)}, u32[]{:S(2)}, u32[]{:S(2)}) collective-permute-start(s32[1,4]{1,0:T(1,128)S(1)} %copy-done.38), channel_id=1, source_target_pairs={{0,16},{1,17},{2,18},{3,19},{4,20},{5,21},{6,22},{7,23},{8,24},{9,... | collective-permute-start | bytes 56 | tf_op jit(solution)/shard_map/ppermute | solution.py:710
  26.6 31.4 %collective-permute-start.4 = (s32[1,4]{1,0:T(1,128)S(1)}, s32[1,4]{1,0:T(1,128)S(1)}, u32[]{:S(2)}, u32[]{:S(2)}) collective-permute-start(s32[1,4]{1,0:T(1,128)S(1)} %copy-done.38), channel_id=1, source_target_pairs={{0,8},{1,9},{2,10},{3,11},{4,12},{5,13},{6,14},{7,15},{8,0},{9,1},... | collective-permute-start | bytes 56 | tf_op jit(solution)/shard_map/ppermute | solution.py:710
  46.5 33.7 %all-to-all-start.1 = ((bf16[8,64,1152]{2,1,0:T(8,128)(2,1)}), bf16[8,64,1152]{2,1,0:T(8,128)(2,1)}, u32[]{:S(2)}, u32[]{:S(2)}) async-start(bf16[8,64,1152]{2,1,0:T(8,128)(2,1)} %bitcast.4), calls=%async_computation.1 | async-start | bytes 2359296 | tf_op jit(solution)/shard_map/all_to_all | solution.py:629
  50.8 103.2 %all-gather.3.cloned.1.call-start = ((), (), s32[]{:S(2)}) async-start(), calls=%async_computation.6 | async-start | bytes 4718592 | tf_op jit(solution)/shard_map/all_gather | solution.py:615
  52.2 25.8 %collective-permute-start.3 = (bf16[512,1024]{1,0:T(8,128)(2,1)}, bf16[512,1024]{1,0:T(8,128)(2,1)}, u32[]{:S(2)}, u32[]{:S(2)}) collective-permute-start(bf16[512,1024]{1,0:T(8,128)(2,1)} %bitcast.3.refs_5_.refs_7_), channel_id=1, source_target_pairs={{0,4},{1,5},{2,6},{3,7},{4,0},{5,1},{6,2},{7,3},{8,12},{9,13},{10,... | collective-permute-start | bytes 3145736 | tf_op jit(solution)/shard_map/ppermute | solution.py:710
  53.8 25.4 %collective-permute-start.2 = (bf16[512,1024]{1,0:T(8,128)(2,1)}, bf16[512,1024]{1,0:T(8,128)(2,1)}, u32[]{:S(2)}, u32[]{:S(2)}) collective-permute-start(bf16[512,1024]{1,0:T(8,128)(2,1)} %bitcast.3.refs_5_.refs_7_), channel_id=1, source_target_pairs={{0,2},{1,3},{2,0},{3,1},{4,6},{5,7},{6,4},{7,5},{8,10},{9,11},{10,... | collective-permute-start | bytes 3145736 | tf_op jit(solution)/shard_map/ppermute | solution.py:710
  80.2 99.1 %all-gather.5.cloned.1.call-start = ((), (), s32[]{:S(2)}) async-start(), calls=%async_computation.8 | async-start | bytes 4718592 | tf_op jit(solution)/shard_map/all_gather | solution.py:615
  81.0 171.9 %reduce-scatter.3.cloned.1.call-start = ((), (), s32[]{:S(2)}) async-start(), calls=%async_computation.7 | async-start | bytes 4718592 | tf_op jit(solution)/shard_map/reduce_scatter | solution.py:620
  82.6 52.8 %collective-permute-start.8 = (bf16[512,1152]{1,0:T(8,128)(2,1)}, bf16[512,1152]{1,0:T(8,128)(2,1)}, u32[]{:S(2)}, u32[]{:S(2)}) collective-permute-start(bf16[512,1152]{1,0:T(8,128)(2,1)} %bitcast.5.refs_10_.refs_12_), channel_id=1, source_target_pairs={{0,4},{1,5},{2,6},{3,7},{4,0},{5,1},{6,2},{7,3},{8,12},{9,13},{10,... | collective-permute-start | bytes 3538952 | tf_op jit(solution)/shard_map/ppermute | solution.py:710
  84.1 51.3 %collective-permute-start.7 = (bf16[512,1152]{1,0:T(8,128)(2,1)}, bf16[512,1152]{1,0:T(8,128)(2,1)}, u32[]{:S(2)}, u32[]{:S(2)}) collective-permute-start(bf16[512,1152]{1,0:T(8,128)(2,1)} %bitcast.5.refs_10_.refs_12_), channel_id=1, source_target_pairs={{0,2},{1,3},{2,0},{3,1},{4,6},{5,7},{6,4},{7,5},{8,10},{9,11},{10,... | collective-permute-start | bytes 3538952 | tf_op jit(solution)/shard_map/ppermute | solution.py:710
  85.6 35.9 %collective-permute-start.11 = (bf16[112,2048]{1,0:T(8,128)(2,1)S(1)}, bf16[112,2048]{1,0:T(8,128)(2,1)S(1)}, u32[]{:S(2)}, u32[]{:S(2)}) collective-permute-start(bf16[112,2048]{1,0:T(8,128)(2,1)S(1)} %slice.89.refs_2_), channel_id=1, source_target_pairs={{0,4},{1,5},{2,6},{3,7},{4,0},{5,1},{6,2},{7,3},{8,12},{9,13},{10,... | collective-permute-start | bytes 1376264 | tf_op jit(solution)/shard_map/ppermute | solution.py:710
  89.9 45.5 %collective-permute-start.10 = (bf16[256,1024]{1,0:T(8,128)(2,1)}, bf16[256,1024]{1,0:T(8,128)(2,1)}, u32[]{:S(2)}, u32[]{:S(2)}) collective-permute-start(bf16[256,1024]{1,0:T(8,128)(2,1)} %slice.94), channel_id=1, source_target_pairs={{0,2},{1,3},{2,0},{3,1},{4,6},{5,7},{6,4},{7,5},{8,10},{9,11},{10,... | collective-permute-start | bytes 1572872 | tf_op jit(solution)/shard_map/ppermute | solution.py:710
  90.4 45.0 %collective-permute-start.9 = (bf16[256,1024]{1,0:T(8,128)(2,1)}, bf16[256,1024]{1,0:T(8,128)(2,1)}, u32[]{:S(2)}, u32[]{:S(2)}) collective-permute-start(bf16[256,1024]{1,0:T(8,128)(2,1)} %slice.93), channel_id=1, source_target_pairs={{0,4},{1,5},{2,6},{3,7},{4,0},{5,1},{6,2},{7,3},{8,12},{9,13},{10,... | collective-permute-start | bytes 1572872 | tf_op jit(solution)/shard_map/ppermute | solution.py:710
  179.1 108.8 %reduce-scatter.5.cloned.1.call-start = ((), (), s32[]{:S(2)}) async-start(), calls=%async_computation.9 | async-start | bytes 4718592 | tf_op jit(solution)/shard_map/reduce_scatter | solution.py:620
  190.4 30.4 %collective-permute-start.17 = (bf16[256,2048]{1,0:T(8,128)(2,1)}, bf16[256,2048]{1,0:T(8,128)(2,1)S(1)}, u32[]{:S(2)}, u32[]{:S(2)}) collective-permute-start(bf16[256,2048]{1,0:T(8,128)(2,1)} %get-tuple-element.156), channel_id=1, source_target_pairs={{0,4},{1,5},{2,6},{3,7},{4,0},{5,1},{6,2},{7,3},{8,12},{9,13},{10,... | collective-permute-start | bytes 3145736 | tf_op jit(solution)/shard_map/ppermute | solution.py:710
  190.5 30.3 %collective-permute-start.16 = (bf16[224,2048]{1,0:T(8,128)(2,1)}, bf16[224,2048]{1,0:T(8,128)(2,1)S(1)}, u32[]{:S(2)}, u32[]{:S(2)}) collective-permute-start(bf16[224,2048]{1,0:T(8,128)(2,1)} %get-tuple-element.155), channel_id=1, source_target_pairs={{0,2},{1,3},{2,0},{3,1},{4,6},{5,7},{6,4},{7,5},{8,10},{9,11},{10,... | collective-permute-start | bytes 2752520 | tf_op jit(solution)/shard_map/ppermute | solution.py:710
  230.9 30.6 %collective-permute-start.18 = (bf16[512,1408]{1,0:T(8,128)(2,1)}, bf16[512,1408]{1,0:T(8,128)(2,1)S(1)}, u32[]{:S(2)}, u32[]{:S(2)}) collective-permute-start(bf16[512,1408]{1,0:T(8,128)(2,1)} %get-tuple-element.177), channel_id=1, source_target_pairs={{0,2},{1,3},{2,0},{3,1},{4,6},{5,7},{6,4},{7,5},{8,10},{9,11},{10,... | collective-permute-start | bytes 4325384 | tf_op jit(solution)/shard_map/ppermute | solution.py:710
  232.6 29.6 %collective-permute-start.19 = (bf16[512,1408]{1,0:T(8,128)(2,1)}, bf16[512,1408]{1,0:T(8,128)(2,1)}, u32[]{:S(2)}, u32[]{:S(2)}) collective-permute-start(bf16[512,1408]{1,0:T(8,128)(2,1)} %get-tuple-element.178), channel_id=1, source_target_pairs={{0,4},{1,5},{2,6},{3,7},{4,0},{5,1},{6,2},{7,3},{8,12},{9,13},{10,... | collective-permute-start | bytes 4325384 | tf_op jit(solution)/shard_map/ppermute | solution.py:710
  281.3 40.3 %all-to-all-start.2 = ((bf16[8,64,1408]{2,1,0:T(8,128)(2,1)}), bf16[8,64,1408]{2,1,0:T(8,128)(2,1)S(1)}, u32[]{:S(2)}, u32[]{:S(2)}) async-start(bf16[8,64,1408]{2,1,0:T(8,128)(2,1)} %bitcast.20), calls=%async_computation.4 | async-start | bytes 2883584 | tf_op jit(solution)/shard_map/all_to_all | solution.py:629
  321.9 31.0 %all-to-all-start.3 = ((bf16[8,64,768]{2,1,0:T(8,128)(2,1)}), bf16[8,64,768]{2,1,0:T(8,128)(2,1)S(1)}, u32[]{:S(2)}, u32[]{:S(2)}) async-start(bf16[8,64,768]{2,1,0:T(8,128)(2,1)} %bitcast.22), calls=%async_computation.5 | async-start | bytes 1572864 | tf_op jit(solution)/shard_map/all_to_all | solution.py:629
  (58 other events, 496.9 us)
Sparse Core Ops, SparseCore 0:
  80.4 46.3 all-gather.2
  128.9 45.7 all-gather.4
  179.2 47.1 reduce-scatter.2
  228.5 48.1 reduce-scatter.4

commit v2 on v1

--- a/solution.py
+++ b/solution.py
@@ -405,13 +405,84 @@
     )(jnp.array(slabs, jnp.int32), *kept(normed, grad))
 
 
+def sum_kernel(own_low, own_high, from_x, from_y, last_x, last_y, out_ref):
+    def total(*refs):
+        return sum(ref[...].astype(F32) for ref in refs).astype(BF)
+
+    out_ref[0] = total(own_low, from_x, last_y)
+    out_ref[1] = total(own_high, from_y, last_x)
+
+
+def sum_call(own_low, own_high, first, last):
+    half, width = own_low.shape
+    rows = half // 2
+    near = pl.BlockSpec((rows, width), lambda i: (i, 0))
+    second = pl.BlockSpec((rows, width), lambda i: (i + 2, 0))
+    out = pl.pallas_call(
+        sum_kernel,
+        grid=(2,),
+        in_specs=[near, near, second, second, near, near],
+        out_specs=pl.BlockSpec((2, rows, width), lambda i: (0, i, 0)),
+        out_shape=pltpu.HBM((2, half, width), BF),
+        compiler_params=stepping(24),
+        cost_estimate=HIDDEN_COST,
+        name="sum_lanes",
+    )(*kept(own_low, own_high, *first, *last))
+    return out.reshape(2 * half, width)
+
+
+def add_kernel(from_x, from_y, x_high, y_low, to_x, to_y):
+    to_x[...] = (x_high[...].astype(F32) + from_y[...].astype(F32)).astype(BF)
+    to_y[...] = (y_low[...].astype(F32) + from_x[...].astype(F32)).astype(BF)
+
+
+def add_call(got, x_high, y_low):
+    high, low = x_high.shape, y_low.shape
+    block = lambda shape: pl.BlockSpec(shape, lambda i: (0, 0))
+    return pl.pallas_call(
+        add_kernel,
+        grid=(1,),
+        in_specs=[block(low), block(high), block(high), block(low)],
+        out_specs=[block(high), block(low)],
+        out_shape=[pltpu.HBM(high, BF), pltpu.HBM(low, BF)],
+        compiler_params=stepping(24),
+        cost_estimate=HIDDEN_COST,
+        name="add_halves",
+    )(*kept(*got, x_high, y_low))
+
+
+def mixer_sum_call(own_low, own_high, first, last, own):
+    (low, width), high = own_low.shape, own_high.shape[0]
+    rest = high - own
+
+    def kernel(low_ref, high_ref, x_ref, y_ref, last_x, last_y, out_ref, down_ref):
+        low_sum = low_ref[...].astype(F32) + x_ref[...].astype(F32) + last_y[...].astype(F32)
+        high_sum = high_ref[...].astype(F32) + y_ref[...].astype(F32) + last_x[...].astype(F32)
+        down_ref[:low, :] = low_sum
+        down_ref[low:, :] = high_sum[:rest]
+        out_ref[...] = high_sum[rest:]
+
+    block = lambda rows, at=0: pl.BlockSpec((rows, width), lambda i: (at, 0))
+    return pl.pallas_call(
+        kernel,
+        grid=(1,),
+        in_specs=[block(low), block(high), block(low, 1), block(high, 1), block(high), block(low)],
+        out_specs=[block(own), block(low + rest)],
+        out_shape=[pltpu.HBM((own, width), F32), pltpu.HBM((low + rest, width), F32)],
+        compiler_params=stepping(24),
+        cost_estimate=HIDDEN_COST,
+        name="sum_mixer",
+    )(*kept(own_low, own_high, *first, *last))
+
+
 def mixer_grad_call(lane, joined, masked, wide, own, own_ff, cut):
     everyone, joint = joined.shape
     width = masked.shape[1]
     rest = own + own_ff - cut
 
-    def kernel(lane_ref, joined_ref, masked_ref, *refs):
-        to_x, to_y, x_high, y_low, own_low, own_high, whole, sem = refs
+    def kernel(lane_ref, joined_any, masked_any, *refs):
+        to_x, to_y, x_high, y_low, own_low, own_high, joined_ref, masked_ref, whole, sem = refs
+        run_copies([(joined_any, joined_ref), (masked_any, masked_ref)], sem)
         masked = masked_ref[...]
 
         def product(at, size):
@@ -443,17 +514,19 @@
     shapes = [(size, width) for size in (2 * cut, 2 * rest, rest, cut, cut, rest)]
     return pl.pallas_call(
         kernel,
-        in_specs=[pl.BlockSpec(memory_space=pltpu.SMEM), HELD, HELD],
+        in_specs=[pl.BlockSpec(memory_space=pltpu.SMEM), ANYWHERE, ANYWHERE],
         out_specs=[pl.BlockSpec(memory_space=pltpu.HBM)] * len(shapes),
         out_shape=[pltpu.HBM(shape, BF) for shape in shapes],
         scratch_shapes=[
+            pltpu.VMEM((everyone, joint), BF),
+            pltpu.VMEM((everyone, width), BF),
             pltpu.VMEM((joint, width), BF),
             pltpu.SemaphoreType.DMA((3 * wide,)),
         ],
         compiler_params=pltpu.CompilerParams(vmem_limit_bytes=40 << 20),
         cost_estimate=HIDDEN_COST,
         name="mixer_grad",
-    )(lane, joined, masked)
+    )(lane, *kept(joined, masked))
 
 
 def column_plan(member, outer, wide, cores, own, own_ff, cols, main, rest):
@@ -798,19 +871,18 @@
         *qkv_first, grad_tokens, stats = tie(*qkv_first, *results)
         qkv_last = self.last_sends(qkv_first, qkv_x, qkv_y)
         part_qkv = self.joined_sum((qkv_x, qkv_y, qkv_low, qkv_high), qkv_first, qkv_last)
+        stats = self.keep(self.chip_stats(stats), 1, self.lane, self.wide, "step")
         part_ff, part_qkv, stats, *mix = tie(part_ff, part_qkv, stats, *mix_first, *mix[2:])
         part_qkv = self.exchange(part_qkv)
-        stats = self.chip_stats(stats)
         mix_first, mix = mix[:2], mix[2:]
-        mix_last = self.last_sends(mix_first, mix[0], mix[1])
+        mix_x, mix_y = add_call(mix_first, mix[0], mix[1])
+        mix_last = self.send(mix_x, 1), self.send(mix_y, 2)
         stats = self.scatter_stats(stats)
-        low, high = self.lane_sum(mix[2], mix[3], mix_first, mix_last)
-        grad_w_out, grad_w_down = high[rest:], jnp.concatenate([low, high[:rest]], axis=0)
+        grad_w_out, grad_w_down = mixer_sum_call(mix[2], mix[3], mix_first, mix_last, own)
         return grad_w_out, grad_w_down, part_qkv, part_ff, branch, grad_tokens, stats
 
     def joined_sum(self, late, first, last):
-        low, high = self.lane_sum(late[2], late[3], first, last)
-        return jnp.concatenate([low, high], axis=0).astype(BF)
+        return sum_call(late[2], late[3], first, last)
 
     def keep(self, values, axis, place, count, name):
         pick = lambda spot: lax.dynamic_index_in_dim(values, spot, axis, keepdims=False)
@@ -822,7 +894,6 @@
         return self.keep(split, 2, lax.rem(self.member, 2), 2, "dc")
 
     def scatter_stats(self, split):
-        split = self.keep(split, 1, self.lane, self.wide, "step")
         return self.keep(split, 0, self.member // 2, self.outer, "dz")
 
     def relative(self, blocks, axis):

time: 364 us -> 365 us (level)
  Pallas kernels: 95 us -> 110 us
  other arithmetic: 33.6 us -> 22.9 us
  local copies, waits for them, and re-layouts: 36.7 us -> 32 us
    pallas_call x1 -> x5, Pallas kernels: 7.23 us -> 21.5 us  [the longest x1 9.78 us: mixer_grad_call(): pl.pallas_call(kernel, in_specs=[pl.BlockSpec(memory_space=pltpu.SMEM), A...]
    another operation x5 -> x1, other arithmetic: 5.71 us -> 0.18 us
    unnamed x82 -> x68, local copies, waits for them, and re-layouts: 10.6 us -> 7.24 us
  transfers between devices with their start and end apart: 43 -> 43, of which waited for: 20 -> 20; matrix products, arithmetic and copies ran while one was open for 16% -> 13% of each run, Pallas kernels for 25% -> 29%
where the time goes in v2:
time: 365 us; the launch traced here: 364 us
  waiting for transfers between devices  123 us (34%)
  Pallas kernels  110 us (30%)
  starting transfers between devices  62.2 us (17%)
  local copies, waits for them, and re-layouts  32 us (9%)
  other arithmetic  22.9 us (6%)
  between operations  14.5 us (4%)
    ppermute x35, waiting for transfers between devices, send(): return lax.ppermute(value, AXES, pairs)  120 us
    ppermute x35, starting transfers between devices, send(): return lax.ppermute(value, AXES, pairs)  42.6 us
    pallas_call x1, Pallas kernels, backward_call(): pl.pallas_call(functools.partial(backward_kernel, sizes, count, block), g...  29.8 us
    pallas_call x4, Pallas kernels, product_call(): pl.pallas_call(kernel, in_specs=[pl.BlockSpec(memory_space=pltpu.SMEM), A...  26.1 us
    pallas_call x1, Pallas kernels, forward_call(): pl.pallas_call(functools.partial(forward_kernel, sizes, count, block), gr...  24.3 us
    all_to_all x4, starting transfers between devices, exchange(): lax.all_to_all(part, self.token_axes, split_axis=0, concat_axis=0, tiled=...  19.3 us
    pallas_call x1, Pallas kernels, mixer_grad_call(): pl.pallas_call(kernel, in_specs=[pl.BlockSpec(memory_space=pltpu.SMEM), A...  9.78 us
  transfers between devices with their start and end apart: 43, of which 20 were waited for; matrix products, arithmetic and copies ran while one was open for 13% of the time, Pallas kernels for 29%

profile of v2, /device:TPU:0, one launch (start us, length us, event | category | flops | bytes accessed | tf_op | source)
XLA Modules:
  0.0 363.9 jit_solution(8655133316731050984)
XLA Ops:
  13.3 6.5 %all-to-all-start = ((bf16[8,64,1024]{2,1,0:T(8,128)(2,1)}), bf16[8,64,1024]{2,1,0:T(8,128)(2,1)}, u32[]{:S(2)}, u32[]{:S(2)}) async-start(bf16[8,64,1024]{2,1,0:T(8,128)(2,1)} %bitcast.2), calls=%async_computation | async-start | bytes 2097152 | tf_op jit(solution)/shard_map/all_to_all | solution.py:702
  22.8 3.8 %collective-permute-start.6 = (s32[1,4]{1,0:T(1,128)S(1)}, s32[1,4]{1,0:T(1,128)S(1)}, u32[]{:S(2)}, u32[]{:S(2)}) collective-permute-start(s32[1,4]{1,0:T(1,128)S(1)} %copy-done.31), channel_id=1, source_target_pairs={{0,24},{1,25},{2,26},{3,27},{4,28},{5,29},{6,30},{7,31},{8,16},{9,... | collective-permute-start | bytes 56 | tf_op jit(solution)/shard_map/ppermute | solution.py:783
  27.7 16.3 %collective-permute-done.1 = bf16[240,2048]{1,0:T(8,128)(2,1)S(1)} collective-permute-done((bf16[240,2048]{1,0:T(8,128)(2,1)S(1)}, bf16[240,2048]{1,0:T(8,128)(2,1)S(1)}, u32[]{:S(2)}, u32[]{:S(2)}) %collective-permute-start.1) | collective-permute-done | bytes 983072 | tf_op jit(solution)/shard_map/ppermute | solution.py:783
  46.5 4.3 %all-to-all-start.1 = ((bf16[8,64,1152]{2,1,0:T(8,128)(2,1)}), bf16[8,64,1152]{2,1,0:T(8,128)(2,1)}, u32[]{:S(2)}, u32[]{:S(2)}) async-start(bf16[8,64,1152]{2,1,0:T(8,128)(2,1)} %bitcast.4), calls=%async_computation.1 | async-start | bytes 2359296 | tf_op jit(solution)/shard_map/all_to_all | solution.py:702
  61.5 16.5 %collective-permute-done.3.refs_7_.refs_9_ = bf16[512,1024]{1,0:T(8,128)(2,1)} collective-permute-done((bf16[512,1024]{1,0:T(8,128)(2,1)}, bf16[512,1024]{1,0:T(8,128)(2,1)}, u32[]{:S(2)}, u32[]{:S(2)}) %collective-permute-start.3) | collective-permute-done | bytes 1048608 | tf_op jit(solution)/shard_map/ppermute | solution.py:783
  93.3 28.2 %collective-permute-done.11.refs_6_ = bf16[112,2048]{1,0:T(8,128)(2,1)S(1)} collective-permute-done((bf16[112,2048]{1,0:T(8,128)(2,1)S(1)}, bf16[112,2048]{1,0:T(8,128)(2,1)S(1)}, u32[]{:S(2)}, u32[]{:S(2)}) %collective-permute-start.11) | collective-permute-done | bytes 458784 | tf_op jit(solution)/shard_map/ppermute | solution.py:783
  124.8 9.2 %collective-permute-done.12.refs_7_ = bf16[128,2048]{1,0:T(8,128)(2,1)S(1)} collective-permute-done((bf16[128,2048]{1,0:T(8,128)(2,1)S(1)}, bf16[128,2048]{1,0:T(8,128)(2,1)S(1)}, u32[]{:S(2)}, u32[]{:S(2)}) %collective-permute-start.12) | collective-permute-done | bytes 524320 | tf_op jit(solution)/shard_map/ppermute | solution.py:783
  143.0 9.1 %collective-permute-done.15.refs_14_.refs_16_ = bf16[256,1152]{1,0:T(8,128)(2,1)S(1)} collective-permute-done((bf16[256,1152]{1,0:T(8,128)(2,1)S(1)}, bf16[256,1152]{1,0:T(8,128)(2,1)S(1)}, u32[]{:S(2)}, u32[]{:S(2)}) %collective-permute-start.15) | collective-permute-done | bytes 589856 | tf_op jit(solution)/shard_map/ppermute | solution.py:783
  154.1 24.3 %forward.1 = (bf16[1024,960]{1,0:T(8,128)(2,1)}, bf16[1024,768]{1,0:T(8,128)(2,1)}, f32[1024,1408]{1,0:T(8,128)}, bf16[1024,2048]{1,0:T(8,128)(2,1)}) custom-call(bf16[1024,2048]{1,0:T(8,128)(2,1)} %all-gather.3.cloned.1.call-done.refs_0_.lhs_any, f32[8,768]{1,0:T(8,128)} %broadcast_in_dim.101.refs_1_, f32[1024,128]{1,0:T(8,128)} %copy.48.refs_2_.refs_3_, ...), custom_call_target="tpu_custom_call" | custom-call | flops 1 | bytes 1 | tf_op jit(solution)/shard_map/forward/pallas_call | solution.py:279
  178.7 9.8 %mixer_grad.1 = (bf16[224,2048]{1,0:T(8,128)(2,1)}, bf16[256,2048]{1,0:T(8,128)(2,1)}, bf16[128,2048]{1,0:T(8,128)(2,1)}, bf16[112,2048]{1,0:T(8,128)(2,1)}, bf1...) custom-call(s32[1]{0:T(128)} %bitcast.8.lane_ref, bf16[1024,960]{1,0:T(8,128)(2,1)} %get-tuple-element.151.joined_any, ...), custom_call_target="tpu_custom_call" | custom-call | flops 1 | bytes 1 | tf_op jit(solution)/shard_map/mixer_grad/pallas_call | solution.py:515
  189.3 29.8 %backward.1 = (bf16[1024,768]{1,0:T(8,128)(2,1)}, bf16[1024,1408]{1,0:T(8,128)(2,1)}, bf16[1024,2048]{1,0:T(8,128)(2,1)}, f32[8,768]{1,0:T(8,128)}) custom-call(bf16[1024,2048]{1,0:T(8,128)(2,1)} %all-gather.5.cloned.1.call-done.masked_any.refs_0_, f32[1024,1408]{1,0:T(8,128)} %get-tuple-element.162.refs_1_, bf16[1024,768]{1,0:T(8,128)(2,1)} %get-tuple-element.163.refs_2_, ...), custom_call_target="tpu_custom_call" | custom-call | flops 1 | bytes 1 | tf_op jit(solution)/shard_map/backward/pallas_call | solution.py:321
  219.8 7.5 %weight_grad.4 = (bf16[512,1408]{1,0:T(8,128)(2,1)}, bf16[512,1408]{1,0:T(8,128)(2,1)}) custom-call(s32[4]{0:T(128)S(1)} %copy-done.7, bf16[1024,2048]{1,0:T(8,128)(2,1)} %all-gather.3.cloned.1.call-done.refs_0_.lhs_any, bf16[1024,1408]{1,0:T(8,128)(2,1)} %get-tuple-element.170.grad_any), custom_call_target="tpu_custom_call" | custom-call | flops 1 | bytes 1 | tf_op jit(solution)/shard_map/weight_grad/pallas_call | solution.py:391
  230.6 7.8 %weight_grad.5 = (bf16[256,1408]{1,0:T(8,128)(2,1)}, bf16[256,1408]{1,0:T(8,128)(2,1)}, bf16[256,1408]{1,0:T(8,128)(2,1)}, bf16[256,1408]{1,0:T(8,128)(2,1)}) custom-call(s32[4]{0:T(128)S(1)} %copy-done.6, bf16[1024,2048]{1,0:T(8,128)(2,1)} %all-gather.3.cloned.1.call-done.refs_0_.lhs_any, bf16[1024,1408]{1,0:T(8,128)(2,1)} %get-tuple-element.170.grad_any), custom_call_target="tpu_custom_call" | custom-call | flops 1 | bytes 1 | tf_op jit(solution)/shard_map/weight_grad/pallas_call | solution.py:391
  238.4 5.4 %weight_grad.6 = (bf16[512,768]{1,0:T(8,128)(2,1)}, bf16[512,768]{1,0:T(8,128)(2,1)}) custom-call(s32[4]{0:T(128)S(1)} %copy-done.7, bf16[1024,2048]{1,0:T(8,128)(2,1)} %all-gather.3.cloned.1.call-done.refs_0_.lhs_any, bf16[1024,768]{1,0:T(8,128)(2,1)} %get-tuple-element.179.grad_any), custom_call_target="tpu_custom_call" | custom-call | flops 1 | bytes 1 | tf_op jit(solution)/shard_map/weight_grad/pallas_call | solution.py:391
  243.9 5.4 %weight_grad.7 = (bf16[256,768]{1,0:T(8,128)(2,1)}, bf16[256,768]{1,0:T(8,128)(2,1)}, bf16[256,768]{1,0:T(8,128)(2,1)}, bf16[256,768]{1,0:T(8,128)(2,1)}) custom-call(s32[4]{0:T(128)S(1)} %copy-done.6, bf16[1024,2048]{1,0:T(8,128)(2,1)} %all-gather.3.cloned.1.call-done.refs_0_.lhs_any, bf16[1024,768]{1,0:T(8,128)(2,1)} %get-tuple-element.179.grad_any), custom_call_target="tpu_custom_call" | custom-call | flops 1 | bytes 1 | tf_op jit(solution)/shard_map/weight_grad/pallas_call | solution.py:391
  251.6 7.5 %collective-permute-done.18.from_x = bf16[512,1408]{1,0:T(8,128)(2,1)S(1)} collective-permute-done((bf16[512,1408]{1,0:T(8,128)(2,1)}, bf16[512,1408]{1,0:T(8,128)(2,1)S(1)}, u32[]{:S(2)}, u32[]{:S(2)}) %collective-permute-start.18) | collective-permute-done | bytes 1441824 | tf_op jit(solution)/shard_map/ppermute | solution.py:783
  265.2 10.6 %collective-permute-done.21.last_y = bf16[256,1408]{1,0:T(8,128)(2,1)} collective-permute-done((bf16[256,1408]{1,0:T(8,128)(2,1)}, bf16[256,1408]{1,0:T(8,128)(2,1)}, u32[]{:S(2)}, u32[]{:S(2)}) %collective-permute-start.21) | collective-permute-done | bytes 720928 | tf_op jit(solution)/shard_map/ppermute | solution.py:783
  276.7 3.3 sum_lanes.2
  280.1 3.8 %all-to-all-start.2 = ((bf16[8,64,1408]{2,1,0:T(8,128)(2,1)}), bf16[8,64,1408]{2,1,0:T(8,128)(2,1)S(1)}, u32[]{:S(2)}, u32[]{:S(2)}) async-start(bf16[8,64,1408]{2,1,0:T(8,128)(2,1)} %bitcast.53), calls=%async_computation.4 | async-start | bytes 2883584 | tf_op jit(solution)/shard_map/all_to_all | solution.py:702
  314.4 4.6 %collective-permute-done.27 = f32[4,320]{1,0:T(4,128)S(1)} collective-permute-done((f32[4,320]{1,0:T(4,128)S(1)}, f32[4,320]{1,0:T(4,128)S(1)}, u32[]{:S(2)}, u32[]{:S(2)}) %collective-permute-start.27) | collective-permute-done | bytes 5152 | tf_op jit(solution)/shard_map/ppermute | solution.py:783
  324.0 4.8 %all-to-all-start.3 = ((bf16[8,64,768]{2,1,0:T(8,128)(2,1)}), bf16[8,64,768]{2,1,0:T(8,128)(2,1)S(1)}, u32[]{:S(2)}, u32[]{:S(2)}) async-start(bf16[8,64,768]{2,1,0:T(8,128)(2,1)} %bitcast.55), calls=%async_computation.5 | async-start | bytes 1572864 | tf_op jit(solution)/shard_map/all_to_all | solution.py:702
  334.5 3.0 collective-permute-start.31
  341.1 8.8 %collective-permute-done.31 = f32[320]{0:T(512)S(1)} collective-permute-done((f32[320]{0:T(512)S(1)}, f32[320]{0:T(512)S(1)}, u32[]{:S(2)}, u32[]{:S(2)}) %collective-permute-start.31) | collective-permute-done | bytes 1312 | tf_op jit(solution)/shard_map/ppermute | solution.py:783
  351.5 3.3 sum_mixer.1
  (241 shorter events, 116.0 us)
Async XLA Ops:
  13.3 33.2 %all-to-all-start = ((bf16[8,64,1024]{2,1,0:T(8,128)(2,1)}), bf16[8,64,1024]{2,1,0:T(8,128)(2,1)}, u32[]{:S(2)}, u32[]{:S(2)}) async-start(bf16[8,64,1024]{2,1,0:T(8,128)(2,1)} %bitcast.2), calls=%async_computation | async-start | bytes 2097152 | tf_op jit(solution)/shard_map/all_to_all | solution.py:702
  19.8 24.2 %collective-permute-start.1 = (bf16[240,2048]{1,0:T(8,128)(2,1)S(1)}, bf16[240,2048]{1,0:T(8,128)(2,1)S(1)}, u32[]{:S(2)}, u32[]{:S(2)}) collective-permute-start(bf16[240,2048]{1,0:T(8,128)(2,1)S(1)} %join_rows.1), channel_id=1, source_target_pairs={{0,4},{1,5},{2,6},{3,7},{4,0},{5,1},{6,2},{7,3},{8,12},{9,13},{10,... | collective-permute-start | bytes 2949128 | tf_op jit(solution)/shard_map/ppermute | solution.py:783
  21.3 24.0 %collective-permute-start = (bf16[240,2048]{1,0:T(8,128)(2,1)S(1)}, bf16[240,2048]{1,0:T(8,128)(2,1)}, u32[]{:S(2)}, u32[]{:S(2)}) collective-permute-start(bf16[240,2048]{1,0:T(8,128)(2,1)S(1)} %join_rows.1), channel_id=1, source_target_pairs={{0,2},{1,3},{2,0},{3,1},{4,6},{5,7},{6,4},{7,5},{8,10},{9,11},{10,... | collective-permute-start | bytes 2949128 | tf_op jit(solution)/shard_map/ppermute | solution.py:783
  22.8 35.3 %collective-permute-start.6 = (s32[1,4]{1,0:T(1,128)S(1)}, s32[1,4]{1,0:T(1,128)S(1)}, u32[]{:S(2)}, u32[]{:S(2)}) collective-permute-start(s32[1,4]{1,0:T(1,128)S(1)} %copy-done.31), channel_id=1, source_target_pairs={{0,24},{1,25},{2,26},{3,27},{4,28},{5,29},{6,30},{7,31},{8,16},{9,... | collective-permute-start | bytes 56 | tf_op jit(solution)/shard_map/ppermute | solution.py:783
  26.6 31.4 %collective-permute-start.5 = (s32[1,4]{1,0:T(1,128)S(1)}, s32[1,4]{1,0:T(1,128)S(1)}, u32[]{:S(2)}, u32[]{:S(2)}) collective-permute-start(s32[1,4]{1,0:T(1,128)S(1)} %copy-done.31), channel_id=1, source_target_pairs={{0,16},{1,17},{2,18},{3,19},{4,20},{5,21},{6,22},{7,23},{8,24},{9,... | collective-permute-start | bytes 56 | tf_op jit(solution)/shard_map/ppermute | solution.py:783
  26.6 31.4 %collective-permute-start.4 = (s32[1,4]{1,0:T(1,128)S(1)}, s32[1,4]{1,0:T(1,128)S(1)}, u32[]{:S(2)}, u32[]{:S(2)}) collective-permute-start(s32[1,4]{1,0:T(1,128)S(1)} %copy-done.31), channel_id=1, source_target_pairs={{0,8},{1,9},{2,10},{3,11},{4,12},{5,13},{6,14},{7,15},{8,0},{9,1},... | collective-permute-start | bytes 56 | tf_op jit(solution)/shard_map/ppermute | solution.py:783
  46.5 33.7 %all-to-all-start.1 = ((bf16[8,64,1152]{2,1,0:T(8,128)(2,1)}), bf16[8,64,1152]{2,1,0:T(8,128)(2,1)}, u32[]{:S(2)}, u32[]{:S(2)}) async-start(bf16[8,64,1152]{2,1,0:T(8,128)(2,1)} %bitcast.4), calls=%async_computation.1 | async-start | bytes 2359296 | tf_op jit(solution)/shard_map/all_to_all | solution.py:702
  50.8 102.5 %all-gather.3.cloned.1.call-start = ((), (), s32[]{:S(2)}) async-start(), calls=%async_computation.6 | async-start | bytes 4718592 | tf_op jit(solution)/shard_map/all_gather | solution.py:688
  52.2 25.8 %collective-permute-start.3 = (bf16[512,1024]{1,0:T(8,128)(2,1)}, bf16[512,1024]{1,0:T(8,128)(2,1)}, u32[]{:S(2)}, u32[]{:S(2)}) collective-permute-start(bf16[512,1024]{1,0:T(8,128)(2,1)} %bitcast.3.refs_5_.refs_7_), channel_id=1, source_target_pairs={{0,4},{1,5},{2,6},{3,7},{4,0},{5,1},{6,2},{7,3},{8,12},{9,13},{10,... | collective-permute-start | bytes 3145736 | tf_op jit(solution)/shard_map/ppermute | solution.py:783
  53.8 25.4 %collective-permute-start.2 = (bf16[512,1024]{1,0:T(8,128)(2,1)}, bf16[512,1024]{1,0:T(8,128)(2,1)}, u32[]{:S(2)}, u32[]{:S(2)}) collective-permute-start(bf16[512,1024]{1,0:T(8,128)(2,1)} %bitcast.3.refs_5_.refs_7_), channel_id=1, source_target_pairs={{0,2},{1,3},{2,0},{3,1},{4,6},{5,7},{6,4},{7,5},{8,10},{9,11},{10,... | collective-permute-start | bytes 3145736 | tf_op jit(solution)/shard_map/ppermute | solution.py:783
  80.2 98.4 %all-gather.5.cloned.1.call-start = ((), (), s32[]{:S(2)}) async-start(), calls=%async_computation.8 | async-start | bytes 4718592 | tf_op jit(solution)/shard_map/all_gather | solution.py:688
  81.0 168.4 %reduce-scatter.3.cloned.1.call-start = ((), (), s32[]{:S(2)}) async-start(), calls=%async_computation.7 | async-start | bytes 4718592 | tf_op jit(solution)/shard_map/reduce_scatter | solution.py:693
  82.6 52.8 %collective-permute-start.8 = (bf16[512,1152]{1,0:T(8,128)(2,1)}, bf16[512,1152]{1,0:T(8,128)(2,1)}, u32[]{:S(2)}, u32[]{:S(2)}) collective-permute-start(bf16[512,1152]{1,0:T(8,128)(2,1)} %bitcast.5.refs_10_.refs_12_), channel_id=1, source_target_pairs={{0,4},{1,5},{2,6},{3,7},{4,0},{5,1},{6,2},{7,3},{8,12},{9,13},{10,... | collective-permute-start | bytes 3538952 | tf_op jit(solution)/shard_map/ppermute | solution.py:783
  84.1 51.3 %collective-permute-start.7 = (bf16[512,1152]{1,0:T(8,128)(2,1)}, bf16[512,1152]{1,0:T(8,128)(2,1)}, u32[]{:S(2)}, u32[]{:S(2)}) collective-permute-start(bf16[512,1152]{1,0:T(8,128)(2,1)} %bitcast.5.refs_10_.refs_12_), channel_id=1, source_target_pairs={{0,2},{1,3},{2,0},{3,1},{4,6},{5,7},{6,4},{7,5},{8,10},{9,11},{10,... | collective-permute-start | bytes 3538952 | tf_op jit(solution)/shard_map/ppermute | solution.py:783
  85.6 35.9 %collective-permute-start.11 = (bf16[112,2048]{1,0:T(8,128)(2,1)S(1)}, bf16[112,2048]{1,0:T(8,128)(2,1)S(1)}, u32[]{:S(2)}, u32[]{:S(2)}) collective-permute-start(bf16[112,2048]{1,0:T(8,128)(2,1)S(1)} %slice.59.refs_2_), channel_id=1, source_target_pairs={{0,4},{1,5},{2,6},{3,7},{4,0},{5,1},{6,2},{7,3},{8,12},{9,13},{10,... | collective-permute-start | bytes 1376264 | tf_op jit(solution)/shard_map/ppermute | solution.py:783
  89.9 45.5 %collective-permute-start.10 = (bf16[256,1024]{1,0:T(8,128)(2,1)}, bf16[256,1024]{1,0:T(8,128)(2,1)}, u32[]{:S(2)}, u32[]{:S(2)}) collective-permute-start(bf16[256,1024]{1,0:T(8,128)(2,1)} %slice.64), channel_id=1, source_target_pairs={{0,2},{1,3},{2,0},{3,1},{4,6},{5,7},{6,4},{7,5},{8,10},{9,11},{10,... | collective-permute-start | bytes 1572872 | tf_op jit(solution)/shard_map/ppermute | solution.py:783
  90.4 45.0 %collective-permute-start.9 = (bf16[256,1024]{1,0:T(8,128)(2,1)}, bf16[256,1024]{1,0:T(8,128)(2,1)}, u32[]{:S(2)}, u32[]{:S(2)}) collective-permute-start(bf16[256,1024]{1,0:T(8,128)(2,1)} %slice.63), channel_id=1, source_target_pairs={{0,4},{1,5},{2,6},{3,7},{4,0},{5,1},{6,2},{7,3},{8,12},{9,13},{10,... | collective-permute-start | bytes 1572872 | tf_op jit(solution)/shard_map/ppermute | solution.py:783
  178.4 108.7 %reduce-scatter.5.cloned.1.call-start = ((), (), s32[]{:S(2)}) async-start(), calls=%async_computation.9 | async-start | bytes 4718592 | tf_op jit(solution)/shard_map/reduce_scatter | solution.py:693
  188.4 30.7 %collective-permute-start.17 = (bf16[256,2048]{1,0:T(8,128)(2,1)}, bf16[256,2048]{1,0:T(8,128)(2,1)}, u32[]{:S(2)}, u32[]{:S(2)}) collective-permute-start(bf16[256,2048]{1,0:T(8,128)(2,1)} %get-tuple-element.160), channel_id=1, source_target_pairs={{0,4},{1,5},{2,6},{3,7},{4,0},{5,1},{6,2},{7,3},{8,12},{9,13},{10,... | collective-permute-start | bytes 3145736 | tf_op jit(solution)/shard_map/ppermute | solution.py:783
  188.7 30.4 %collective-permute-start.16 = (bf16[224,2048]{1,0:T(8,128)(2,1)}, bf16[224,2048]{1,0:T(8,128)(2,1)}, u32[]{:S(2)}, u32[]{:S(2)}) collective-permute-start(bf16[224,2048]{1,0:T(8,128)(2,1)} %get-tuple-element.159), channel_id=1, source_target_pairs={{0,2},{1,3},{2,0},{3,1},{4,6},{5,7},{6,4},{7,5},{8,10},{9,11},{10,... | collective-permute-start | bytes 2752520 | tf_op jit(solution)/shard_map/ppermute | solution.py:783
  227.3 31.7 %collective-permute-start.18 = (bf16[512,1408]{1,0:T(8,128)(2,1)}, bf16[512,1408]{1,0:T(8,128)(2,1)S(1)}, u32[]{:S(2)}, u32[]{:S(2)}) collective-permute-start(bf16[512,1408]{1,0:T(8,128)(2,1)} %get-tuple-element.181), channel_id=1, source_target_pairs={{0,2},{1,3},{2,0},{3,1},{4,6},{5,7},{6,4},{7,5},{8,10},{9,11},{10,... | collective-permute-start | bytes 4325384 | tf_op jit(solution)/shard_map/ppermute | solution.py:783
  228.8 30.5 %collective-permute-start.19 = (bf16[512,1408]{1,0:T(8,128)(2,1)}, bf16[512,1408]{1,0:T(8,128)(2,1)S(1)}, u32[]{:S(2)}, u32[]{:S(2)}) collective-permute-start(bf16[512,1408]{1,0:T(8,128)(2,1)} %get-tuple-element.182), channel_id=1, source_target_pairs={{0,4},{1,5},{2,6},{3,7},{4,0},{5,1},{6,2},{7,3},{8,12},{9,13},{10,... | collective-permute-start | bytes 4325384 | tf_op jit(solution)/shard_map/ppermute | solution.py:783
  280.1 43.9 %all-to-all-start.2 = ((bf16[8,64,1408]{2,1,0:T(8,128)(2,1)}), bf16[8,64,1408]{2,1,0:T(8,128)(2,1)S(1)}, u32[]{:S(2)}, u32[]{:S(2)}) async-start(bf16[8,64,1408]{2,1,0:T(8,128)(2,1)} %bitcast.53), calls=%async_computation.4 | async-start | bytes 2883584 | tf_op jit(solution)/shard_map/all_to_all | solution.py:702
  324.0 30.8 %all-to-all-start.3 = ((bf16[8,64,768]{2,1,0:T(8,128)(2,1)}), bf16[8,64,768]{2,1,0:T(8,128)(2,1)S(1)}, u32[]{:S(2)}, u32[]{:S(2)}) async-start(bf16[8,64,768]{2,1,0:T(8,128)(2,1)} %bitcast.55), calls=%async_computation.5 | async-start | bytes 1572864 | tf_op jit(solution)/shard_map/all_to_all | solution.py:702
  (51 other events, 440.9 us)
Sparse Core Ops, SparseCore 0:
  80.3 46.3 all-gather.2
  128.9 45.8 all-gather.4
  178.5 47.2 reduce-scatter.2
  228.0 48.0 reduce-scatter.4

commit v3 on v2

--- a/solution.py
+++ b/solution.py
@@ -427,7 +427,7 @@
         compiler_params=stepping(24),
         cost_estimate=HIDDEN_COST,
         name="sum_lanes",
-    )(*kept(own_low, own_high, *first, *last))
+    )(*kept(own_low, own_high, *first), *last)
     return out.reshape(2 * half, width)
 
 
@@ -472,7 +472,7 @@
         compiler_params=stepping(24),
         cost_estimate=HIDDEN_COST,
         name="sum_mixer",
-    )(*kept(own_low, own_high, *first, *last))
+    )(*kept(own_low, own_high, *first), *last)
 
 
 def mixer_grad_call(lane, joined, masked, wide, own, own_ff, cut):
@@ -871,7 +871,7 @@
         *qkv_first, grad_tokens, stats = tie(*qkv_first, *results)
         qkv_last = self.last_sends(qkv_first, qkv_x, qkv_y)
         part_qkv = self.joined_sum((qkv_x, qkv_y, qkv_low, qkv_high), qkv_first, qkv_last)
-        stats = self.keep(self.chip_stats(stats), 1, self.lane, self.wide, "step")
+        stats = self.depth_stats(stats)
         part_ff, part_qkv, stats, *mix = tie(part_ff, part_qkv, stats, *mix_first, *mix[2:])
         part_qkv = self.exchange(part_qkv)
         mix_first, mix = mix[:2], mix[2:]
@@ -889,12 +889,13 @@
         got = [self.send(pick(lax.bitwise_xor(place, j)), **{name: j}) for j in range(1, count)]
         return pick(place) + sum(got)
 
-    def chip_stats(self, stats):
+    def depth_stats(self, stats):
         split = stats.reshape(self.outer, self.wide, 2, -1)
-        return self.keep(split, 2, lax.rem(self.member, 2), 2, "dc")
+        return self.keep(split, 0, self.member // 2, self.outer, "dz")
 
     def scatter_stats(self, split):
-        return self.keep(split, 0, self.member // 2, self.outer, "dz")
+        split = self.keep(split, 0, self.lane, self.wide, "step")
+        return self.keep(split, 0, lax.rem(self.member, 2), 2, "dc")
 
     def relative(self, blocks, axis):
         shape = blocks.shape

time: 365 us -> 360 us (0.986)
  transfers between devices with their start and end apart: 43 -> 43, of which waited for: 20 -> 18; matrix products, arithmetic and copies ran while one was open for 13% -> 13% of each run, Pallas kernels for 29% -> 29%
where the time goes in v3:
time: 360 us; the launch traced here: 359 us
  waiting for transfers between devices  121 us (34%)
  Pallas kernels  109 us (30%)
  starting transfers between devices  60.7 us (17%)
  local copies, waits for them, and re-layouts  29.7 us (8%)
  other arithmetic  24.2 us (7%)
  between operations  14.5 us (4%)
    ppermute x35, waiting for transfers between devices, send(): return lax.ppermute(value, AXES, pairs)  118 us
    ppermute x35, starting transfers between devices, send(): return lax.ppermute(value, AXES, pairs)  42.2 us
    pallas_call x1, Pallas kernels, backward_call(): pl.pallas_call(functools.partial(backward_kernel, sizes, count, block), g...  29.8 us
    pallas_call x4, Pallas kernels, product_call(): pl.pallas_call(kernel, in_specs=[pl.BlockSpec(memory_space=pltpu.SMEM), A...  26.1 us
    pallas_call x1, Pallas kernels, forward_call(): pl.pallas_call(functools.partial(forward_kernel, sizes, count, block), gr...  24.3 us
    all_to_all x4, starting transfers between devices, exchange(): lax.all_to_all(part, self.token_axes, split_axis=0, concat_axis=0, tiled=...  18.1 us
    pallas_call x1, Pallas kernels, mixer_grad_call(): pl.pallas_call(kernel, in_specs=[pl.BlockSpec(memory_space=pltpu.SMEM), A...  9.77 us
  transfers between devices with their start and end apart: 43, of which 18 were waited for; matrix products, arithmetic and copies ran while one was open for 13% of the time, Pallas kernels for 29%

profile of v3, /device:TPU:0, one launch (start us, length us, event | category | flops | bytes accessed | tf_op | source)
XLA Modules:
  0.0 358.9 jit_solution(17534056183668548866)
XLA Ops:
  13.3 6.5 %all-to-all-start = ((bf16[8,64,1024]{2,1,0:T(8,128)(2,1)}), bf16[8,64,1024]{2,1,0:T(8,128)(2,1)}, u32[]{:S(2)}, u32[]{:S(2)}) async-start(bf16[8,64,1024]{2,1,0:T(8,128)(2,1)} %bitcast.2), calls=%async_computation | async-start | bytes 2097152 | tf_op jit(solution)/shard_map/all_to_all | solution.py:702
  22.8 3.8 %collective-permute-start.6 = (s32[1,4]{1,0:T(1,128)S(1)}, s32[1,4]{1,0:T(1,128)S(1)}, u32[]{:S(2)}, u32[]{:S(2)}) collective-permute-start(s32[1,4]{1,0:T(1,128)S(1)} %copy-done.29), channel_id=1, source_target_pairs={{0,24},{1,25},{2,26},{3,27},{4,28},{5,29},{6,30},{7,31},{8,16},{9,... | collective-permute-start | bytes 56 | tf_op jit(solution)/shard_map/ppermute | solution.py:783
  27.7 16.3 %collective-permute-done.1 = bf16[240,2048]{1,0:T(8,128)(2,1)S(1)} collective-permute-done((bf16[240,2048]{1,0:T(8,128)(2,1)S(1)}, bf16[240,2048]{1,0:T(8,128)(2,1)S(1)}, u32[]{:S(2)}, u32[]{:S(2)}) %collective-permute-start.1) | collective-permute-done | bytes 983072 | tf_op jit(solution)/shard_map/ppermute | solution.py:783
  46.5 4.3 %all-to-all-start.1 = ((bf16[8,64,1152]{2,1,0:T(8,128)(2,1)}), bf16[8,64,1152]{2,1,0:T(8,128)(2,1)}, u32[]{:S(2)}, u32[]{:S(2)}) async-start(bf16[8,64,1152]{2,1,0:T(8,128)(2,1)} %bitcast.4), calls=%async_computation.1 | async-start | bytes 2359296 | tf_op jit(solution)/shard_map/all_to_all | solution.py:702
  61.5 16.5 %collective-permute-done.3.refs_7_.refs_9_ = bf16[512,1024]{1,0:T(8,128)(2,1)} collective-permute-done((bf16[512,1024]{1,0:T(8,128)(2,1)}, bf16[512,1024]{1,0:T(8,128)(2,1)}, u32[]{:S(2)}, u32[]{:S(2)}) %collective-permute-start.3) | collective-permute-done | bytes 1048608 | tf_op jit(solution)/shard_map/ppermute | solution.py:783
  93.3 28.2 %collective-permute-done.11.refs_6_ = bf16[112,2048]{1,0:T(8,128)(2,1)S(1)} collective-permute-done((bf16[112,2048]{1,0:T(8,128)(2,1)S(1)}, bf16[112,2048]{1,0:T(8,128)(2,1)S(1)}, u32[]{:S(2)}, u32[]{:S(2)}) %collective-permute-start.11) | collective-permute-done | bytes 458784 | tf_op jit(solution)/shard_map/ppermute | solution.py:783
  124.8 9.2 %collective-permute-done.12.refs_7_ = bf16[128,2048]{1,0:T(8,128)(2,1)S(1)} collective-permute-done((bf16[128,2048]{1,0:T(8,128)(2,1)S(1)}, bf16[128,2048]{1,0:T(8,128)(2,1)S(1)}, u32[]{:S(2)}, u32[]{:S(2)}) %collective-permute-start.12) | collective-permute-done | bytes 524320 | tf_op jit(solution)/shard_map/ppermute | solution.py:783
  143.0 9.1 %collective-permute-done.15.refs_14_.refs_16_ = bf16[256,1152]{1,0:T(8,128)(2,1)S(1)} collective-permute-done((bf16[256,1152]{1,0:T(8,128)(2,1)S(1)}, bf16[256,1152]{1,0:T(8,128)(2,1)S(1)}, u32[]{:S(2)}, u32[]{:S(2)}) %collective-permute-start.15) | collective-permute-done | bytes 589856 | tf_op jit(solution)/shard_map/ppermute | solution.py:783
  154.1 24.3 %forward.1 = (bf16[1024,960]{1,0:T(8,128)(2,1)}, bf16[1024,768]{1,0:T(8,128)(2,1)}, f32[1024,1408]{1,0:T(8,128)}, bf16[1024,2048]{1,0:T(8,128)(2,1)}) custom-call(bf16[1024,2048]{1,0:T(8,128)(2,1)} %all-gather.3.cloned.1.call-done.refs_0_.lhs_any, f32[8,768]{1,0:T(8,128)} %broadcast_in_dim.101.refs_1_, f32[1024,128]{1,0:T(8,128)} %copy.48.refs_2_.refs_3_, ...), custom_call_target="tpu_custom_call" | custom-call | flops 1 | bytes 1 | tf_op jit(solution)/shard_map/forward/pallas_call | solution.py:279
  178.7 9.8 %mixer_grad.1 = (bf16[224,2048]{1,0:T(8,128)(2,1)}, bf16[256,2048]{1,0:T(8,128)(2,1)}, bf16[128,2048]{1,0:T(8,128)(2,1)}, bf16[112,2048]{1,0:T(8,128)(2,1)}, bf1...) custom-call(s32[1]{0:T(128)} %bitcast.8.lane_ref, bf16[1024,960]{1,0:T(8,128)(2,1)} %get-tuple-element.151.joined_any, ...), custom_call_target="tpu_custom_call" | custom-call | flops 1 | bytes 1 | tf_op jit(solution)/shard_map/mixer_grad/pallas_call | solution.py:515
  189.3 29.8 %backward.1 = (bf16[1024,768]{1,0:T(8,128)(2,1)}, bf16[1024,1408]{1,0:T(8,128)(2,1)}, bf16[1024,2048]{1,0:T(8,128)(2,1)}, f32[8,768]{1,0:T(8,128)}) custom-call(bf16[1024,2048]{1,0:T(8,128)(2,1)} %all-gather.5.cloned.1.call-done.masked_any.refs_0_, f32[1024,1408]{1,0:T(8,128)} %get-tuple-element.162.refs_1_, bf16[1024,768]{1,0:T(8,128)(2,1)} %get-tuple-element.163.refs_2_, ...), custom_call_target="tpu_custom_call" | custom-call | flops 1 | bytes 1 | tf_op jit(solution)/shard_map/backward/pallas_call | solution.py:321
  219.8 7.5 %weight_grad.4 = (bf16[512,1408]{1,0:T(8,128)(2,1)}, bf16[512,1408]{1,0:T(8,128)(2,1)}) custom-call(s32[4]{0:T(128)S(1)} %copy-done.7, bf16[1024,2048]{1,0:T(8,128)(2,1)} %all-gather.3.cloned.1.call-done.refs_0_.lhs_any, bf16[1024,1408]{1,0:T(8,128)(2,1)} %get-tuple-element.170.grad_any), custom_call_target="tpu_custom_call" | custom-call | flops 1 | bytes 1 | tf_op jit(solution)/shard_map/weight_grad/pallas_call | solution.py:391
  230.6 7.8 %weight_grad.5 = (bf16[256,1408]{1,0:T(8,128)(2,1)}, bf16[256,1408]{1,0:T(8,128)(2,1)}, bf16[256,1408]{1,0:T(8,128)(2,1)}, bf16[256,1408]{1,0:T(8,128)(2,1)}) custom-call(s32[4]{0:T(128)S(1)} %copy-done.6, bf16[1024,2048]{1,0:T(8,128)(2,1)} %all-gather.3.cloned.1.call-done.refs_0_.lhs_any, bf16[1024,1408]{1,0:T(8,128)(2,1)} %get-tuple-element.170.grad_any), custom_call_target="tpu_custom_call" | custom-call | flops 1 | bytes 1 | tf_op jit(solution)/shard_map/weight_grad/pallas_call | solution.py:391
  238.4 5.4 %weight_grad.6 = (bf16[512,768]{1,0:T(8,128)(2,1)}, bf16[512,768]{1,0:T(8,128)(2,1)}) custom-call(s32[4]{0:T(128)S(1)} %copy-done.7, bf16[1024,2048]{1,0:T(8,128)(2,1)} %all-gather.3.cloned.1.call-done.refs_0_.lhs_any, bf16[1024,768]{1,0:T(8,128)(2,1)} %get-tuple-element.179.grad_any), custom_call_target="tpu_custom_call" | custom-call | flops 1 | bytes 1 | tf_op jit(solution)/shard_map/weight_grad/pallas_call | solution.py:391
  243.8 5.4 %weight_grad.7 = (bf16[256,768]{1,0:T(8,128)(2,1)}, bf16[256,768]{1,0:T(8,128)(2,1)}, bf16[256,768]{1,0:T(8,128)(2,1)}, bf16[256,768]{1,0:T(8,128)(2,1)}) custom-call(s32[4]{0:T(128)S(1)} %copy-done.6, bf16[1024,2048]{1,0:T(8,128)(2,1)} %all-gather.3.cloned.1.call-done.refs_0_.lhs_any, bf16[1024,768]{1,0:T(8,128)(2,1)} %get-tuple-element.179.grad_any), custom_call_target="tpu_custom_call" | custom-call | flops 1 | bytes 1 | tf_op jit(solution)/shard_map/weight_grad/pallas_call | solution.py:391
  251.5 7.5 %collective-permute-done.18.from_x = bf16[512,1408]{1,0:T(8,128)(2,1)S(1)} collective-permute-done((bf16[512,1408]{1,0:T(8,128)(2,1)}, bf16[512,1408]{1,0:T(8,128)(2,1)S(1)}, u32[]{:S(2)}, u32[]{:S(2)}) %collective-permute-start.18) | collective-permute-done | bytes 1441824 | tf_op jit(solution)/shard_map/ppermute | solution.py:783
  266.2 9.4 %collective-permute-done.21.last_y = bf16[256,1408]{1,0:T(8,128)(2,1)S(1)} collective-permute-done((bf16[256,1408]{1,0:T(8,128)(2,1)}, bf16[256,1408]{1,0:T(8,128)(2,1)S(1)}, u32[]{:S(2)}, u32[]{:S(2)}) %collective-permute-start.21) | collective-permute-done | bytes 720928 | tf_op jit(solution)/shard_map/ppermute | solution.py:783
  277.7 2.9 sum_lanes.2
  280.6 3.8 %all-to-all-start.2 = ((bf16[8,64,1408]{2,1,0:T(8,128)(2,1)}), bf16[8,64,1408]{2,1,0:T(8,128)(2,1)S(1)}, u32[]{:S(2)}, u32[]{:S(2)}) async-start(bf16[8,64,1408]{2,1,0:T(8,128)(2,1)} %bitcast.53), calls=%async_computation.4 | async-start | bytes 2883584 | tf_op jit(solution)/shard_map/all_to_all | solution.py:702
  301.7 2.8 fusion.14
  314.4 5.7 %collective-permute-done.27 = f32[4,2,320]{2,1,0:T(2,128)S(1)} collective-permute-done((f32[4,2,320]{2,1,0:T(2,128)S(1)}, f32[4,2,320]{2,1,0:T(2,128)S(1)}, u32[]{:S(2)}, u32[]{:S(2)}) %collective-permute-start.27) | collective-permute-done | bytes 10272 | tf_op jit(solution)/shard_map/ppermute | solution.py:783
  322.5 3.5 all-to-all-start.3
  335.2 7.6 %collective-permute-done.30 = f32[2,320]{1,0:T(2,128)S(1)} collective-permute-done((f32[2,320]{1,0:T(2,128)S(1)}, f32[2,320]{1,0:T(2,128)S(1)}, u32[]{:S(2)}, u32[]{:S(2)}) %collective-permute-start.30) | collective-permute-done | bytes 2592 | tf_op jit(solution)/shard_map/ppermute | solution.py:783
  346.7 3.0 sum_mixer.1
  (233 shorter events, 114.3 us)
Async XLA Ops:
  13.3 33.2 %all-to-all-start = ((bf16[8,64,1024]{2,1,0:T(8,128)(2,1)}), bf16[8,64,1024]{2,1,0:T(8,128)(2,1)}, u32[]{:S(2)}, u32[]{:S(2)}) async-start(bf16[8,64,1024]{2,1,0:T(8,128)(2,1)} %bitcast.2), calls=%async_computation | async-start | bytes 2097152 | tf_op jit(solution)/shard_map/all_to_all | solution.py:702
  19.8 24.2 %collective-permute-start.1 = (bf16[240,2048]{1,0:T(8,128)(2,1)S(1)}, bf16[240,2048]{1,0:T(8,128)(2,1)S(1)}, u32[]{:S(2)}, u32[]{:S(2)}) collective-permute-start(bf16[240,2048]{1,0:T(8,128)(2,1)S(1)} %join_rows.1), channel_id=1, source_target_pairs={{0,4},{1,5},{2,6},{3,7},{4,0},{5,1},{6,2},{7,3},{8,12},{9,13},{10,... | collective-permute-start | bytes 2949128 | tf_op jit(solution)/shard_map/ppermute | solution.py:783
  21.3 24.0 %collective-permute-start = (bf16[240,2048]{1,0:T(8,128)(2,1)S(1)}, bf16[240,2048]{1,0:T(8,128)(2,1)}, u32[]{:S(2)}, u32[]{:S(2)}) collective-permute-start(bf16[240,2048]{1,0:T(8,128)(2,1)S(1)} %join_rows.1), channel_id=1, source_target_pairs={{0,2},{1,3},{2,0},{3,1},{4,6},{5,7},{6,4},{7,5},{8,10},{9,11},{10,... | collective-permute-start | bytes 2949128 | tf_op jit(solution)/shard_map/ppermute | solution.py:783
  22.8 35.3 %collective-permute-start.6 = (s32[1,4]{1,0:T(1,128)S(1)}, s32[1,4]{1,0:T(1,128)S(1)}, u32[]{:S(2)}, u32[]{:S(2)}) collective-permute-start(s32[1,4]{1,0:T(1,128)S(1)} %copy-done.29), channel_id=1, source_target_pairs={{0,24},{1,25},{2,26},{3,27},{4,28},{5,29},{6,30},{7,31},{8,16},{9,... | collective-permute-start | bytes 56 | tf_op jit(solution)/shard_map/ppermute | solution.py:783
  26.6 31.4 %collective-permute-start.5 = (s32[1,4]{1,0:T(1,128)S(1)}, s32[1,4]{1,0:T(1,128)S(1)}, u32[]{:S(2)}, u32[]{:S(2)}) collective-permute-start(s32[1,4]{1,0:T(1,128)S(1)} %copy-done.29), channel_id=1, source_target_pairs={{0,16},{1,17},{2,18},{3,19},{4,20},{5,21},{6,22},{7,23},{8,24},{9,... | collective-permute-start | bytes 56 | tf_op jit(solution)/shard_map/ppermute | solution.py:783
  26.6 31.4 %collective-permute-start.4 = (s32[1,4]{1,0:T(1,128)S(1)}, s32[1,4]{1,0:T(1,128)S(1)}, u32[]{:S(2)}, u32[]{:S(2)}) collective-permute-start(s32[1,4]{1,0:T(1,128)S(1)} %copy-done.29), channel_id=1, source_target_pairs={{0,8},{1,9},{2,10},{3,11},{4,12},{5,13},{6,14},{7,15},{8,0},{9,1},... | collective-permute-start | bytes 56 | tf_op jit(solution)/shard_map/ppermute | solution.py:783
  46.5 33.7 %all-to-all-start.1 = ((bf16[8,64,1152]{2,1,0:T(8,128)(2,1)}), bf16[8,64,1152]{2,1,0:T(8,128)(2,1)}, u32[]{:S(2)}, u32[]{:S(2)}) async-start(bf16[8,64,1152]{2,1,0:T(8,128)(2,1)} %bitcast.4), calls=%async_computation.1 | async-start | bytes 2359296 | tf_op jit(solution)/shard_map/all_to_all | solution.py:702
  50.8 102.5 %all-gather.3.cloned.1.call-start = ((), (), s32[]{:S(2)}) async-start(), calls=%async_computation.6 | async-start | bytes 4718592 | tf_op jit(solution)/shard_map/all_gather | solution.py:688
  52.2 25.8 %collective-permute-start.3 = (bf16[512,1024]{1,0:T(8,128)(2,1)}, bf16[512,1024]{1,0:T(8,128)(2,1)}, u32[]{:S(2)}, u32[]{:S(2)}) collective-permute-start(bf16[512,1024]{1,0:T(8,128)(2,1)} %bitcast.3.refs_5_.refs_7_), channel_id=1, source_target_pairs={{0,4},{1,5},{2,6},{3,7},{4,0},{5,1},{6,2},{7,3},{8,12},{9,13},{10,... | collective-permute-start | bytes 3145736 | tf_op jit(solution)/shard_map/ppermute | solution.py:783
  53.8 25.4 %collective-permute-start.2 = (bf16[512,1024]{1,0:T(8,128)(2,1)}, bf16[512,1024]{1,0:T(8,128)(2,1)}, u32[]{:S(2)}, u32[]{:S(2)}) collective-permute-start(bf16[512,1024]{1,0:T(8,128)(2,1)} %bitcast.3.refs_5_.refs_7_), channel_id=1, source_target_pairs={{0,2},{1,3},{2,0},{3,1},{4,6},{5,7},{6,4},{7,5},{8,10},{9,11},{10,... | collective-permute-start | bytes 3145736 | tf_op jit(solution)/shard_map/ppermute | solution.py:783
  80.2 98.4 %all-gather.5.cloned.1.call-start = ((), (), s32[]{:S(2)}) async-start(), calls=%async_computation.8 | async-start | bytes 4718592 | tf_op jit(solution)/shard_map/all_gather | solution.py:688
  81.0 168.3 %reduce-scatter.3.cloned.1.call-start = ((), (), s32[]{:S(2)}) async-start(), calls=%async_computation.7 | async-start | bytes 4718592 | tf_op jit(solution)/shard_map/reduce_scatter | solution.py:693
  82.6 52.8 %collective-permute-start.8 = (bf16[512,1152]{1,0:T(8,128)(2,1)}, bf16[512,1152]{1,0:T(8,128)(2,1)}, u32[]{:S(2)}, u32[]{:S(2)}) collective-permute-start(bf16[512,1152]{1,0:T(8,128)(2,1)} %bitcast.5.refs_10_.refs_12_), channel_id=1, source_target_pairs={{0,4},{1,5},{2,6},{3,7},{4,0},{5,1},{6,2},{7,3},{8,12},{9,13},{10,... | collective-permute-start | bytes 3538952 | tf_op jit(solution)/shard_map/ppermute | solution.py:783
  84.1 51.3 %collective-permute-start.7 = (bf16[512,1152]{1,0:T(8,128)(2,1)}, bf16[512,1152]{1,0:T(8,128)(2,1)}, u32[]{:S(2)}, u32[]{:S(2)}) collective-permute-start(bf16[512,1152]{1,0:T(8,128)(2,1)} %bitcast.5.refs_10_.refs_12_), channel_id=1, source_target_pairs={{0,2},{1,3},{2,0},{3,1},{4,6},{5,7},{6,4},{7,5},{8,10},{9,11},{10,... | collective-permute-start | bytes 3538952 | tf_op jit(solution)/shard_map/ppermute | solution.py:783
  85.6 35.9 %collective-permute-start.11 = (bf16[112,2048]{1,0:T(8,128)(2,1)S(1)}, bf16[112,2048]{1,0:T(8,128)(2,1)S(1)}, u32[]{:S(2)}, u32[]{:S(2)}) collective-permute-start(bf16[112,2048]{1,0:T(8,128)(2,1)S(1)} %slice.59.refs_2_), channel_id=1, source_target_pairs={{0,4},{1,5},{2,6},{3,7},{4,0},{5,1},{6,2},{7,3},{8,12},{9,13},{10,... | collective-permute-start | bytes 1376264 | tf_op jit(solution)/shard_map/ppermute | solution.py:783
  89.9 45.5 %collective-permute-start.10 = (bf16[256,1024]{1,0:T(8,128)(2,1)}, bf16[256,1024]{1,0:T(8,128)(2,1)}, u32[]{:S(2)}, u32[]{:S(2)}) collective-permute-start(bf16[256,1024]{1,0:T(8,128)(2,1)} %slice.64), channel_id=1, source_target_pairs={{0,2},{1,3},{2,0},{3,1},{4,6},{5,7},{6,4},{7,5},{8,10},{9,11},{10,... | collective-permute-start | bytes 1572872 | tf_op jit(solution)/shard_map/ppermute | solution.py:783
  90.4 45.0 %collective-permute-start.9 = (bf16[256,1024]{1,0:T(8,128)(2,1)}, bf16[256,1024]{1,0:T(8,128)(2,1)}, u32[]{:S(2)}, u32[]{:S(2)}) collective-permute-start(bf16[256,1024]{1,0:T(8,128)(2,1)} %slice.63), channel_id=1, source_target_pairs={{0,4},{1,5},{2,6},{3,7},{4,0},{5,1},{6,2},{7,3},{8,12},{9,13},{10,... | collective-permute-start | bytes 1572872 | tf_op jit(solution)/shard_map/ppermute | solution.py:783
  178.4 109.1 %reduce-scatter.5.cloned.1.call-start = ((), (), s32[]{:S(2)}) async-start(), calls=%async_computation.9 | async-start | bytes 4718592 | tf_op jit(solution)/shard_map/reduce_scatter | solution.py:693
  188.4 30.7 %collective-permute-start.17 = (bf16[256,2048]{1,0:T(8,128)(2,1)}, bf16[256,2048]{1,0:T(8,128)(2,1)}, u32[]{:S(2)}, u32[]{:S(2)}) collective-permute-start(bf16[256,2048]{1,0:T(8,128)(2,1)} %get-tuple-element.160), channel_id=1, source_target_pairs={{0,4},{1,5},{2,6},{3,7},{4,0},{5,1},{6,2},{7,3},{8,12},{9,13},{10,... | collective-permute-start | bytes 3145736 | tf_op jit(solution)/shard_map/ppermute | solution.py:783
  188.7 30.4 %collective-permute-start.16 = (bf16[224,2048]{1,0:T(8,128)(2,1)}, bf16[224,2048]{1,0:T(8,128)(2,1)}, u32[]{:S(2)}, u32[]{:S(2)}) collective-permute-start(bf16[224,2048]{1,0:T(8,128)(2,1)} %get-tuple-element.159), channel_id=1, source_target_pairs={{0,2},{1,3},{2,0},{3,1},{4,6},{5,7},{6,4},{7,5},{8,10},{9,11},{10,... | collective-permute-start | bytes 2752520 | tf_op jit(solution)/shard_map/ppermute | solution.py:783
  227.3 31.7 %collective-permute-start.18 = (bf16[512,1408]{1,0:T(8,128)(2,1)}, bf16[512,1408]{1,0:T(8,128)(2,1)S(1)}, u32[]{:S(2)}, u32[]{:S(2)}) collective-permute-start(bf16[512,1408]{1,0:T(8,128)(2,1)} %get-tuple-element.181), channel_id=1, source_target_pairs={{0,2},{1,3},{2,0},{3,1},{4,6},{5,7},{6,4},{7,5},{8,10},{9,11},{10,... | collective-permute-start | bytes 4325384 | tf_op jit(solution)/shard_map/ppermute | solution.py:783
  228.8 30.6 %collective-permute-start.19 = (bf16[512,1408]{1,0:T(8,128)(2,1)}, bf16[512,1408]{1,0:T(8,128)(2,1)}, u32[]{:S(2)}, u32[]{:S(2)}) collective-permute-start(bf16[512,1408]{1,0:T(8,128)(2,1)} %get-tuple-element.182), channel_id=1, source_target_pairs={{0,4},{1,5},{2,6},{3,7},{4,0},{5,1},{6,2},{7,3},{8,12},{9,13},{10,... | collective-permute-start | bytes 4325384 | tf_op jit(solution)/shard_map/ppermute | solution.py:783
  280.6 41.9 %all-to-all-start.2 = ((bf16[8,64,1408]{2,1,0:T(8,128)(2,1)}), bf16[8,64,1408]{2,1,0:T(8,128)(2,1)S(1)}, u32[]{:S(2)}, u32[]{:S(2)}) async-start(bf16[8,64,1408]{2,1,0:T(8,128)(2,1)} %bitcast.53), calls=%async_computation.4 | async-start | bytes 2883584 | tf_op jit(solution)/shard_map/all_to_all | solution.py:702
  322.5 27.2 %all-to-all-start.3 = ((bf16[8,64,768]{2,1,0:T(8,128)(2,1)}), bf16[8,64,768]{2,1,0:T(8,128)(2,1)S(1)}, u32[]{:S(2)}, u32[]{:S(2)}) async-start(bf16[8,64,768]{2,1,0:T(8,128)(2,1)} %bitcast.55), calls=%async_computation.5 | async-start | bytes 1572864 | tf_op jit(solution)/shard_map/all_to_all | solution.py:702
  (49 other events, 443.1 us)
Sparse Core Ops, SparseCore 0:
  80.4 46.3 all-gather.2
  128.9 45.8 all-gather.4
  178.5 47.3 reduce-scatter.2
  228.0 48.0 reduce-scatter.4

commit v4 on v3

--- a/solution.py
+++ b/solution.py
@@ -551,7 +551,8 @@
 
 
 def pack_kernel(plan, tp, bases, *refs):
-    arrays, packed = refs[:3], refs[3:]
+    packed, arrays, sem = refs[3:5], refs[5:8], refs[8]
+    run_copies(list(zip(refs[:3], arrays)), sem)
     rows = arrays[0].shape[0]
     edge = packed[0].shape[1]
     for member in range(tp):
@@ -571,12 +572,14 @@
     edge = total // 2 // TILE * TILE
     return pl.pallas_call(
         functools.partial(pack_kernel, plan, tp, (0, widths[0], total - widths[0])),
-        in_specs=[HELD] * 3,
+        in_specs=[ANYWHERE] * 3,
         out_specs=[HELD] * 2,
         out_shape=[jax.ShapeDtypeStruct((tp * rows, w), BF) for w in (edge, total - edge)],
+        scratch_shapes=[pltpu.VMEM(array.shape, BF) for array in arrays]
+        + [pltpu.SemaphoreType.DMA((3,))],
         compiler_params=pltpu.CompilerParams(vmem_limit_bytes=32 << 20),
         name="pack_columns",
-    )(*arrays)
+    )(*kept(*arrays))
 
 
 def unpack_kernel(plan, tp, part, *refs):

time: 360 us -> 361 us (level)
  no operation moved by 1% of the time
where the time goes in v4:
time: 361 us; the launch traced here: 359 us
  waiting for transfers between devices  121 us (34%)
  Pallas kernels  110 us (30%)
  starting transfers between devices  60.7 us (17%)
  local copies, waits for them, and re-layouts  28.5 us (8%)
  other arithmetic  24.2 us (7%)
  between operations  14.5 us (4%)
    ppermute x35, waiting for transfers between devices, send(): return lax.ppermute(value, AXES, pairs)  118 us
    ppermute x35, starting transfers between devices, send(): return lax.ppermute(value, AXES, pairs)  42.3 us
    pallas_call x1, Pallas kernels, backward_call(): pl.pallas_call(functools.partial(backward_kernel, sizes, count, block), g...  29.8 us
    pallas_call x4, Pallas kernels, product_call(): pl.pallas_call(kernel, in_specs=[pl.BlockSpec(memory_space=pltpu.SMEM), A...  26.1 us
    pallas_call x1, Pallas kernels, forward_call(): pl.pallas_call(functools.partial(forward_kernel, sizes, count, block), gr...  24.3 us
    all_to_all x4, starting transfers between devices, exchange(): lax.all_to_all(part, self.token_axes, split_axis=0, concat_axis=0, tiled=...  18.1 us
    pallas_call x1, Pallas kernels, mixer_grad_call(): pl.pallas_call(kernel, in_specs=[pl.BlockSpec(memory_space=pltpu.SMEM), A...  9.78 us
  transfers between devices with their start and end apart: 43, of which 18 were waited for; matrix products, arithmetic and copies ran while one was open for 13% of the time, Pallas kernels for 29%

profile of v4, /device:TPU:0, one launch (start us, length us, event | category | flops | bytes accessed | tf_op | source)
XLA Modules:
  0.0 359.3 jit_solution(6861193555322698778)
XLA Ops:
  9.6 4.1 %pack_columns.1 = (bf16[512,1024]{1,0:T(8,128)(2,1)}, bf16[512,1152]{1,0:T(8,128)(2,1)}) custom-call(bf16[64,6144]{1,0:T(8,128)(2,1)} %refs_0_.3, bf16[64,5632]{1,0:T(8,128)(2,1)} %refs_1_.3, bf16[64,5632]{1,0:T(8,128)(2,1)} %refs_2_.1), custom_call_target="tpu_custom_call" | custom-call | tf_op jit(solution)/shard_map/pack_columns/pallas_call | solution.py:573
  13.7 6.5 %all-to-all-start = ((bf16[8,64,1024]{2,1,0:T(8,128)(2,1)}), bf16[8,64,1024]{2,1,0:T(8,128)(2,1)}, u32[]{:S(2)}, u32[]{:S(2)}) async-start(bf16[8,64,1024]{2,1,0:T(8,128)(2,1)} %bitcast.2), calls=%async_computation | async-start | bytes 2097152 | tf_op jit(solution)/shard_map/all_to_all | solution.py:705
  23.2 3.8 %collective-permute-start.6 = (s32[1,4]{1,0:T(1,128)S(1)}, s32[1,4]{1,0:T(1,128)S(1)}, u32[]{:S(2)}, u32[]{:S(2)}) collective-permute-start(s32[1,4]{1,0:T(1,128)S(1)} %copy-done.26), channel_id=1, source_target_pairs={{0,24},{1,25},{2,26},{3,27},{4,28},{5,29},{6,30},{7,31},{8,16},{9,... | collective-permute-start | bytes 56 | tf_op jit(solution)/shard_map/ppermute | solution.py:786
  28.1 16.3 %collective-permute-done.1 = bf16[240,2048]{1,0:T(8,128)(2,1)S(1)} collective-permute-done((bf16[240,2048]{1,0:T(8,128)(2,1)S(1)}, bf16[240,2048]{1,0:T(8,128)(2,1)S(1)}, u32[]{:S(2)}, u32[]{:S(2)}) %collective-permute-start.1) | collective-permute-done | bytes 983072 | tf_op jit(solution)/shard_map/ppermute | solution.py:786
  46.9 4.3 %all-to-all-start.1 = ((bf16[8,64,1152]{2,1,0:T(8,128)(2,1)}), bf16[8,64,1152]{2,1,0:T(8,128)(2,1)}, u32[]{:S(2)}, u32[]{:S(2)}) async-start(bf16[8,64,1152]{2,1,0:T(8,128)(2,1)} %bitcast.4), calls=%async_computation.1 | async-start | bytes 2359296 | tf_op jit(solution)/shard_map/all_to_all | solution.py:705
  61.8 16.5 %collective-permute-done.3.refs_7_.refs_9_ = bf16[512,1024]{1,0:T(8,128)(2,1)} collective-permute-done((bf16[512,1024]{1,0:T(8,128)(2,1)}, bf16[512,1024]{1,0:T(8,128)(2,1)}, u32[]{:S(2)}, u32[]{:S(2)}) %collective-permute-start.3) | collective-permute-done | bytes 1048608 | tf_op jit(solution)/shard_map/ppermute | solution.py:786
  93.7 28.2 %collective-permute-done.11.refs_6_ = bf16[112,2048]{1,0:T(8,128)(2,1)S(1)} collective-permute-done((bf16[112,2048]{1,0:T(8,128)(2,1)S(1)}, bf16[112,2048]{1,0:T(8,128)(2,1)S(1)}, u32[]{:S(2)}, u32[]{:S(2)}) %collective-permute-start.11) | collective-permute-done | bytes 458784 | tf_op jit(solution)/shard_map/ppermute | solution.py:786
  125.2 9.2 %collective-permute-done.12.refs_7_ = bf16[128,2048]{1,0:T(8,128)(2,1)S(1)} collective-permute-done((bf16[128,2048]{1,0:T(8,128)(2,1)S(1)}, bf16[128,2048]{1,0:T(8,128)(2,1)S(1)}, u32[]{:S(2)}, u32[]{:S(2)}) %collective-permute-start.12) | collective-permute-done | bytes 524320 | tf_op jit(solution)/shard_map/ppermute | solution.py:786
  143.5 9.0 %collective-permute-done.15.refs_14_.refs_16_ = bf16[256,1152]{1,0:T(8,128)(2,1)S(1)} collective-permute-done((bf16[256,1152]{1,0:T(8,128)(2,1)S(1)}, bf16[256,1152]{1,0:T(8,128)(2,1)S(1)}, u32[]{:S(2)}, u32[]{:S(2)}) %collective-permute-start.15) | collective-permute-done | bytes 589856 | tf_op jit(solution)/shard_map/ppermute | solution.py:786
  154.5 24.3 %forward.1 = (bf16[1024,960]{1,0:T(8,128)(2,1)}, bf16[1024,768]{1,0:T(8,128)(2,1)}, f32[1024,1408]{1,0:T(8,128)}, bf16[1024,2048]{1,0:T(8,128)(2,1)}) custom-call(bf16[1024,2048]{1,0:T(8,128)(2,1)} %all-gather.3.cloned.1.call-done.refs_0_.lhs_any, f32[8,768]{1,0:T(8,128)} %broadcast_in_dim.101.refs_1_, f32[1024,128]{1,0:T(8,128)} %copy.48.refs_2_.refs_3_, ...), custom_call_target="tpu_custom_call" | custom-call | flops 1 | bytes 1 | tf_op jit(solution)/shard_map/forward/pallas_call | solution.py:279
  179.0 9.8 %mixer_grad.1 = (bf16[224,2048]{1,0:T(8,128)(2,1)}, bf16[256,2048]{1,0:T(8,128)(2,1)}, bf16[128,2048]{1,0:T(8,128)(2,1)}, bf16[112,2048]{1,0:T(8,128)(2,1)}, bf1...) custom-call(s32[1]{0:T(128)} %bitcast.8.lane_ref, bf16[1024,960]{1,0:T(8,128)(2,1)} %get-tuple-element.151.joined_any, ...), custom_call_target="tpu_custom_call" | custom-call | flops 1 | bytes 1 | tf_op jit(solution)/shard_map/mixer_grad/pallas_call | solution.py:515
  189.7 29.8 %backward.1 = (bf16[1024,768]{1,0:T(8,128)(2,1)}, bf16[1024,1408]{1,0:T(8,128)(2,1)}, bf16[1024,2048]{1,0:T(8,128)(2,1)}, f32[8,768]{1,0:T(8,128)}) custom-call(bf16[1024,2048]{1,0:T(8,128)(2,1)} %all-gather.5.cloned.1.call-done.masked_any.refs_0_, f32[1024,1408]{1,0:T(8,128)} %get-tuple-element.162.refs_1_, bf16[1024,768]{1,0:T(8,128)(2,1)} %get-tuple-element.163.refs_2_, ...), custom_call_target="tpu_custom_call" | custom-call | flops 1 | bytes 1 | tf_op jit(solution)/shard_map/backward/pallas_call | solution.py:321
  220.2 7.5 %weight_grad.4 = (bf16[512,1408]{1,0:T(8,128)(2,1)}, bf16[512,1408]{1,0:T(8,128)(2,1)}) custom-call(s32[4]{0:T(128)S(1)} %copy-done.4, bf16[1024,2048]{1,0:T(8,128)(2,1)} %all-gather.3.cloned.1.call-done.refs_0_.lhs_any, bf16[1024,1408]{1,0:T(8,128)(2,1)} %get-tuple-element.170.grad_any), custom_call_target="tpu_custom_call" | custom-call | flops 1 | bytes 1 | tf_op jit(solution)/shard_map/weight_grad/pallas_call | solution.py:391
  231.0 7.8 %weight_grad.5 = (bf16[256,1408]{1,0:T(8,128)(2,1)}, bf16[256,1408]{1,0:T(8,128)(2,1)}, bf16[256,1408]{1,0:T(8,128)(2,1)}, bf16[256,1408]{1,0:T(8,128)(2,1)}) custom-call(s32[4]{0:T(128)S(1)} %copy-done.3, bf16[1024,2048]{1,0:T(8,128)(2,1)} %all-gather.3.cloned.1.call-done.refs_0_.lhs_any, bf16[1024,1408]{1,0:T(8,128)(2,1)} %get-tuple-element.170.grad_any), custom_call_target="tpu_custom_call" | custom-call | flops 1 | bytes 1 | tf_op jit(solution)/shard_map/weight_grad/pallas_call | solution.py:391
  238.8 5.4 %weight_grad.6 = (bf16[512,768]{1,0:T(8,128)(2,1)}, bf16[512,768]{1,0:T(8,128)(2,1)}) custom-call(s32[4]{0:T(128)S(1)} %copy-done.4, bf16[1024,2048]{1,0:T(8,128)(2,1)} %all-gather.3.cloned.1.call-done.refs_0_.lhs_any, bf16[1024,768]{1,0:T(8,128)(2,1)} %get-tuple-element.179.grad_any), custom_call_target="tpu_custom_call" | custom-call | flops 1 | bytes 1 | tf_op jit(solution)/shard_map/weight_grad/pallas_call | solution.py:391
  244.2 5.4 %weight_grad.7 = (bf16[256,768]{1,0:T(8,128)(2,1)}, bf16[256,768]{1,0:T(8,128)(2,1)}, bf16[256,768]{1,0:T(8,128)(2,1)}, bf16[256,768]{1,0:T(8,128)(2,1)}) custom-call(s32[4]{0:T(128)S(1)} %copy-done.3, bf16[1024,2048]{1,0:T(8,128)(2,1)} %all-gather.3.cloned.1.call-done.refs_0_.lhs_any, bf16[1024,768]{1,0:T(8,128)(2,1)} %get-tuple-element.179.grad_any), custom_call_target="tpu_custom_call" | custom-call | flops 1 | bytes 1 | tf_op jit(solution)/shard_map/weight_grad/pallas_call | solution.py:391
  251.9 7.5 %collective-permute-done.18.from_x = bf16[512,1408]{1,0:T(8,128)(2,1)S(1)} collective-permute-done((bf16[512,1408]{1,0:T(8,128)(2,1)}, bf16[512,1408]{1,0:T(8,128)(2,1)S(1)}, u32[]{:S(2)}, u32[]{:S(2)}) %collective-permute-start.18) | collective-permute-done | bytes 1441824 | tf_op jit(solution)/shard_map/ppermute | solution.py:786
  266.6 9.4 %collective-permute-done.21.last_y = bf16[256,1408]{1,0:T(8,128)(2,1)S(1)} collective-permute-done((bf16[256,1408]{1,0:T(8,128)(2,1)}, bf16[256,1408]{1,0:T(8,128)(2,1)S(1)}, u32[]{:S(2)}, u32[]{:S(2)}) %collective-permute-start.21) | collective-permute-done | bytes 720928 | tf_op jit(solution)/shard_map/ppermute | solution.py:786
  278.1 2.9 sum_lanes.2
  281.0 3.8 %all-to-all-start.2 = ((bf16[8,64,1408]{2,1,0:T(8,128)(2,1)}), bf16[8,64,1408]{2,1,0:T(8,128)(2,1)S(1)}, u32[]{:S(2)}, u32[]{:S(2)}) async-start(bf16[8,64,1408]{2,1,0:T(8,128)(2,1)} %bitcast.53), calls=%async_computation.4 | async-start | bytes 2883584 | tf_op jit(solution)/shard_map/all_to_all | solution.py:705
  314.8 5.7 %collective-permute-done.27 = f32[4,2,320]{2,1,0:T(2,128)S(1)} collective-permute-done((f32[4,2,320]{2,1,0:T(2,128)S(1)}, f32[4,2,320]{2,1,0:T(2,128)S(1)}, u32[]{:S(2)}, u32[]{:S(2)}) %collective-permute-start.27) | collective-permute-done | bytes 10272 | tf_op jit(solution)/shard_map/ppermute | solution.py:786
  322.9 3.5 all-to-all-start.3
  335.6 7.6 %collective-permute-done.30 = f32[2,320]{1,0:T(2,128)S(1)} collective-permute-done((f32[2,320]{1,0:T(2,128)S(1)}, f32[2,320]{1,0:T(2,128)S(1)}, u32[]{:S(2)}, u32[]{:S(2)}) %collective-permute-start.30) | collective-permute-done | bytes 2592 | tf_op jit(solution)/shard_map/ppermute | solution.py:786
  347.1 3.0 sum_mixer.1
  (227 shorter events, 113.5 us)
Async XLA Ops:
  13.7 33.2 %all-to-all-start = ((bf16[8,64,1024]{2,1,0:T(8,128)(2,1)}), bf16[8,64,1024]{2,1,0:T(8,128)(2,1)}, u32[]{:S(2)}, u32[]{:S(2)}) async-start(bf16[8,64,1024]{2,1,0:T(8,128)(2,1)} %bitcast.2), calls=%async_computation | async-start | bytes 2097152 | tf_op jit(solution)/shard_map/all_to_all | solution.py:705
  20.2 24.2 %collective-permute-start.1 = (bf16[240,2048]{1,0:T(8,128)(2,1)S(1)}, bf16[240,2048]{1,0:T(8,128)(2,1)S(1)}, u32[]{:S(2)}, u32[]{:S(2)}) collective-permute-start(bf16[240,2048]{1,0:T(8,128)(2,1)S(1)} %join_rows.1), channel_id=1, source_target_pairs={{0,4},{1,5},{2,6},{3,7},{4,0},{5,1},{6,2},{7,3},{8,12},{9,13},{10,... | collective-permute-start | bytes 2949128 | tf_op jit(solution)/shard_map/ppermute | solution.py:786
  21.7 24.0 %collective-permute-start = (bf16[240,2048]{1,0:T(8,128)(2,1)S(1)}, bf16[240,2048]{1,0:T(8,128)(2,1)}, u32[]{:S(2)}, u32[]{:S(2)}) collective-permute-start(bf16[240,2048]{1,0:T(8,128)(2,1)S(1)} %join_rows.1), channel_id=1, source_target_pairs={{0,2},{1,3},{2,0},{3,1},{4,6},{5,7},{6,4},{7,5},{8,10},{9,11},{10,... | collective-permute-start | bytes 2949128 | tf_op jit(solution)/shard_map/ppermute | solution.py:786
  23.2 35.3 %collective-permute-start.6 = (s32[1,4]{1,0:T(1,128)S(1)}, s32[1,4]{1,0:T(1,128)S(1)}, u32[]{:S(2)}, u32[]{:S(2)}) collective-permute-start(s32[1,4]{1,0:T(1,128)S(1)} %copy-done.26), channel_id=1, source_target_pairs={{0,24},{1,25},{2,26},{3,27},{4,28},{5,29},{6,30},{7,31},{8,16},{9,... | collective-permute-start | bytes 56 | tf_op jit(solution)/shard_map/ppermute | solution.py:786
  27.0 31.4 %collective-permute-start.5 = (s32[1,4]{1,0:T(1,128)S(1)}, s32[1,4]{1,0:T(1,128)S(1)}, u32[]{:S(2)}, u32[]{:S(2)}) collective-permute-start(s32[1,4]{1,0:T(1,128)S(1)} %copy-done.26), channel_id=1, source_target_pairs={{0,16},{1,17},{2,18},{3,19},{4,20},{5,21},{6,22},{7,23},{8,24},{9,... | collective-permute-start | bytes 56 | tf_op jit(solution)/shard_map/ppermute | solution.py:786
  27.0 31.4 %collective-permute-start.4 = (s32[1,4]{1,0:T(1,128)S(1)}, s32[1,4]{1,0:T(1,128)S(1)}, u32[]{:S(2)}, u32[]{:S(2)}) collective-permute-start(s32[1,4]{1,0:T(1,128)S(1)} %copy-done.26), channel_id=1, source_target_pairs={{0,8},{1,9},{2,10},{3,11},{4,12},{5,13},{6,14},{7,15},{8,0},{9,1},... | collective-permute-start | bytes 56 | tf_op jit(solution)/shard_map/ppermute | solution.py:786
  46.9 33.7 %all-to-all-start.1 = ((bf16[8,64,1152]{2,1,0:T(8,128)(2,1)}), bf16[8,64,1152]{2,1,0:T(8,128)(2,1)}, u32[]{:S(2)}, u32[]{:S(2)}) async-start(bf16[8,64,1152]{2,1,0:T(8,128)(2,1)} %bitcast.4), calls=%async_computation.1 | async-start | bytes 2359296 | tf_op jit(solution)/shard_map/all_to_all | solution.py:705
  51.2 102.5 %all-gather.3.cloned.1.call-start = ((), (), s32[]{:S(2)}) async-start(), calls=%async_computation.6 | async-start | bytes 4718592 | tf_op jit(solution)/shard_map/all_gather | solution.py:691
  52.6 25.8 %collective-permute-start.3 = (bf16[512,1024]{1,0:T(8,128)(2,1)}, bf16[512,1024]{1,0:T(8,128)(2,1)}, u32[]{:S(2)}, u32[]{:S(2)}) collective-permute-start(bf16[512,1024]{1,0:T(8,128)(2,1)} %bitcast.3.refs_5_.refs_7_), channel_id=1, source_target_pairs={{0,4},{1,5},{2,6},{3,7},{4,0},{5,1},{6,2},{7,3},{8,12},{9,13},{10,... | collective-permute-start | bytes 3145736 | tf_op jit(solution)/shard_map/ppermute | solution.py:786
  54.2 25.4 %collective-permute-start.2 = (bf16[512,1024]{1,0:T(8,128)(2,1)}, bf16[512,1024]{1,0:T(8,128)(2,1)}, u32[]{:S(2)}, u32[]{:S(2)}) collective-permute-start(bf16[512,1024]{1,0:T(8,128)(2,1)} %bitcast.3.refs_5_.refs_7_), channel_id=1, source_target_pairs={{0,2},{1,3},{2,0},{3,1},{4,6},{5,7},{6,4},{7,5},{8,10},{9,11},{10,... | collective-permute-start | bytes 3145736 | tf_op jit(solution)/shard_map/ppermute | solution.py:786
  80.6 98.4 %all-gather.5.cloned.1.call-start = ((), (), s32[]{:S(2)}) async-start(), calls=%async_computation.8 | async-start | bytes 4718592 | tf_op jit(solution)/shard_map/all_gather | solution.py:691
  81.4 168.3 %reduce-scatter.3.cloned.1.call-start = ((), (), s32[]{:S(2)}) async-start(), calls=%async_computation.7 | async-start | bytes 4718592 | tf_op jit(solution)/shard_map/reduce_scatter | solution.py:696
  83.0 52.8 %collective-permute-start.8 = (bf16[512,1152]{1,0:T(8,128)(2,1)}, bf16[512,1152]{1,0:T(8,128)(2,1)}, u32[]{:S(2)}, u32[]{:S(2)}) collective-permute-start(bf16[512,1152]{1,0:T(8,128)(2,1)} %bitcast.5.refs_10_.refs_12_), channel_id=1, source_target_pairs={{0,4},{1,5},{2,6},{3,7},{4,0},{5,1},{6,2},{7,3},{8,12},{9,13},{10,... | collective-permute-start | bytes 3538952 | tf_op jit(solution)/shard_map/ppermute | solution.py:786
  84.5 51.3 %collective-permute-start.7 = (bf16[512,1152]{1,0:T(8,128)(2,1)}, bf16[512,1152]{1,0:T(8,128)(2,1)}, u32[]{:S(2)}, u32[]{:S(2)}) collective-permute-start(bf16[512,1152]{1,0:T(8,128)(2,1)} %bitcast.5.refs_10_.refs_12_), channel_id=1, source_target_pairs={{0,2},{1,3},{2,0},{3,1},{4,6},{5,7},{6,4},{7,5},{8,10},{9,11},{10,... | collective-permute-start | bytes 3538952 | tf_op jit(solution)/shard_map/ppermute | solution.py:786
  86.0 35.9 %collective-permute-start.11 = (bf16[112,2048]{1,0:T(8,128)(2,1)S(1)}, bf16[112,2048]{1,0:T(8,128)(2,1)S(1)}, u32[]{:S(2)}, u32[]{:S(2)}) collective-permute-start(bf16[112,2048]{1,0:T(8,128)(2,1)S(1)} %slice.59.refs_2_), channel_id=1, source_target_pairs={{0,4},{1,5},{2,6},{3,7},{4,0},{5,1},{6,2},{7,3},{8,12},{9,13},{10,... | collective-permute-start | bytes 1376264 | tf_op jit(solution)/shard_map/ppermute | solution.py:786
  90.3 45.5 %collective-permute-start.10 = (bf16[256,1024]{1,0:T(8,128)(2,1)}, bf16[256,1024]{1,0:T(8,128)(2,1)}, u32[]{:S(2)}, u32[]{:S(2)}) collective-permute-start(bf16[256,1024]{1,0:T(8,128)(2,1)} %slice.64), channel_id=1, source_target_pairs={{0,2},{1,3},{2,0},{3,1},{4,6},{5,7},{6,4},{7,5},{8,10},{9,11},{10,... | collective-permute-start | bytes 1572872 | tf_op jit(solution)/shard_map/ppermute | solution.py:786
  90.8 45.0 %collective-permute-start.9 = (bf16[256,1024]{1,0:T(8,128)(2,1)}, bf16[256,1024]{1,0:T(8,128)(2,1)}, u32[]{:S(2)}, u32[]{:S(2)}) collective-permute-start(bf16[256,1024]{1,0:T(8,128)(2,1)} %slice.63), channel_id=1, source_target_pairs={{0,4},{1,5},{2,6},{3,7},{4,0},{5,1},{6,2},{7,3},{8,12},{9,13},{10,... | collective-permute-start | bytes 1572872 | tf_op jit(solution)/shard_map/ppermute | solution.py:786
  178.8 109.1 %reduce-scatter.5.cloned.1.call-start = ((), (), s32[]{:S(2)}) async-start(), calls=%async_computation.9 | async-start | bytes 4718592 | tf_op jit(solution)/shard_map/reduce_scatter | solution.py:696
  188.8 30.7 %collective-permute-start.17 = (bf16[256,2048]{1,0:T(8,128)(2,1)}, bf16[256,2048]{1,0:T(8,128)(2,1)}, u32[]{:S(2)}, u32[]{:S(2)}) collective-permute-start(bf16[256,2048]{1,0:T(8,128)(2,1)} %get-tuple-element.160), channel_id=1, source_target_pairs={{0,4},{1,5},{2,6},{3,7},{4,0},{5,1},{6,2},{7,3},{8,12},{9,13},{10,... | collective-permute-start | bytes 3145736 | tf_op jit(solution)/shard_map/ppermute | solution.py:786
  189.1 30.4 %collective-permute-start.16 = (bf16[224,2048]{1,0:T(8,128)(2,1)}, bf16[224,2048]{1,0:T(8,128)(2,1)}, u32[]{:S(2)}, u32[]{:S(2)}) collective-permute-start(bf16[224,2048]{1,0:T(8,128)(2,1)} %get-tuple-element.159), channel_id=1, source_target_pairs={{0,2},{1,3},{2,0},{3,1},{4,6},{5,7},{6,4},{7,5},{8,10},{9,11},{10,... | collective-permute-start | bytes 2752520 | tf_op jit(solution)/shard_map/ppermute | solution.py:786
  227.7 31.7 %collective-permute-start.18 = (bf16[512,1408]{1,0:T(8,128)(2,1)}, bf16[512,1408]{1,0:T(8,128)(2,1)S(1)}, u32[]{:S(2)}, u32[]{:S(2)}) collective-permute-start(bf16[512,1408]{1,0:T(8,128)(2,1)} %get-tuple-element.181), channel_id=1, source_target_pairs={{0,2},{1,3},{2,0},{3,1},{4,6},{5,7},{6,4},{7,5},{8,10},{9,11},{10,... | collective-permute-start | bytes 4325384 | tf_op jit(solution)/shard_map/ppermute | solution.py:786
  229.2 30.6 %collective-permute-start.19 = (bf16[512,1408]{1,0:T(8,128)(2,1)}, bf16[512,1408]{1,0:T(8,128)(2,1)}, u32[]{:S(2)}, u32[]{:S(2)}) collective-permute-start(bf16[512,1408]{1,0:T(8,128)(2,1)} %get-tuple-element.182), channel_id=1, source_target_pairs={{0,4},{1,5},{2,6},{3,7},{4,0},{5,1},{6,2},{7,3},{8,12},{9,13},{10,... | collective-permute-start | bytes 4325384 | tf_op jit(solution)/shard_map/ppermute | solution.py:786
  281.0 41.9 %all-to-all-start.2 = ((bf16[8,64,1408]{2,1,0:T(8,128)(2,1)}), bf16[8,64,1408]{2,1,0:T(8,128)(2,1)S(1)}, u32[]{:S(2)}, u32[]{:S(2)}) async-start(bf16[8,64,1408]{2,1,0:T(8,128)(2,1)} %bitcast.53), calls=%async_computation.4 | async-start | bytes 2883584 | tf_op jit(solution)/shard_map/all_to_all | solution.py:705
  322.9 27.2 %all-to-all-start.3 = ((bf16[8,64,768]{2,1,0:T(8,128)(2,1)}), bf16[8,64,768]{2,1,0:T(8,128)(2,1)S(1)}, u32[]{:S(2)}, u32[]{:S(2)}) async-start(bf16[8,64,768]{2,1,0:T(8,128)(2,1)} %bitcast.55), calls=%async_computation.5 | async-start | bytes 1572864 | tf_op jit(solution)/shard_map/all_to_all | solution.py:705
  (46 other events, 437.1 us)
Sparse Core Ops, SparseCore 0:
  80.7 46.3 all-gather.2
  129.3 45.8 all-gather.4
  178.9 47.3 reduce-scatter.2
  228.4 48.0 reduce-scatter.4

commit v5 on v3

--- a/solution.py
+++ b/solution.py
@@ -741,7 +741,6 @@
         norm, branch = self.scatter_tokens(norm), self.scatter_tokens(branch)
         part_qkv, part_ff = [self.exchange(part) for part in parts]
         grad_tokens, stats = tail(norm, bias_part)
-        stats = self.scatter_stats(stats)
         return grads[0], grads[1], part_qkv, part_ff, branch, grad_tokens, stats
 
     def relative(self, blocks, axis):
@@ -877,7 +876,6 @@
         mix_first, mix = mix[:2], mix[2:]
         mix_x, mix_y = add_call(mix_first, mix[0], mix[1])
         mix_last = self.send(mix_x, 1), self.send(mix_y, 2)
-        stats = self.scatter_stats(stats)
         grad_w_out, grad_w_down = mixer_sum_call(mix[2], mix[3], mix_first, mix_last, own)
         return grad_w_out, grad_w_down, part_qkv, part_ff, branch, grad_tokens, stats
 
@@ -1004,6 +1002,8 @@
     grad_w_gate, grad_w_up = unpack_call(
         part_ff, 1, plan, tp, [w_gate.shape[1], w_up.shape[1]]
     )
+    stats, grad_w_gate, grad_w_up = tie(stats, grad_w_gate, grad_w_up)
+    stats = net.scatter_stats(stats)
     part_qkv, stats, grad_w_gate, grad_w_up = tie(part_qkv, stats, grad_w_gate, grad_w_up)
     (grad_w_qkv,) = unpack_call(part_qkv, 0, plan, tp, [w_qkv.shape[1]])
     return (

time: 360 us -> 359 us (level)
  transfers between devices with their start and end apart: 43 -> 43, of which waited for: 18 -> 19; matrix products, arithmetic and copies ran while one was open for 13% -> 13% of each run, Pallas kernels for 29% -> 29%
where the time goes in v5:
time: 359 us; the launch traced here: 358 us
  waiting for transfers between devices  120 us (33%)
  Pallas kernels  109 us (30%)
  starting transfers between devices  60.7 us (17%)
  local copies, waits for them, and re-layouts  29.7 us (8%)
  other arithmetic  24.2 us (7%)
  between operations  14.5 us (4%)
    ppermute x35, waiting for transfers between devices, send(): return lax.ppermute(value, AXES, pairs)  117 us
    ppermute x35, starting transfers between devices, send(): return lax.ppermute(value, AXES, pairs)  42.2 us
    pallas_call x1, Pallas kernels, backward_call(): pl.pallas_call(functools.partial(backward_kernel, sizes, count, block), g...  29.8 us
    pallas_call x4, Pallas kernels, product_call(): pl.pallas_call(kernel, in_specs=[pl.BlockSpec(memory_space=pltpu.SMEM), A...  26.1 us
    pallas_call x1, Pallas kernels, forward_call(): pl.pallas_call(functools.partial(forward_kernel, sizes, count, block), gr...  24.3 us
    all_to_all x4, starting transfers between devices, exchange(): lax.all_to_all(part, self.token_axes, split_axis=0, concat_axis=0, tiled=...  18.1 us
    pallas_call x1, Pallas kernels, mixer_grad_call(): pl.pallas_call(kernel, in_specs=[pl.BlockSpec(memory_space=pltpu.SMEM), A...  9.77 us
  transfers between devices with their start and end apart: 43, of which 19 were waited for; matrix products, arithmetic and copies ran while one was open for 13% of the time, Pallas kernels for 29%

profile of v5, /device:TPU:0, one launch (start us, length us, event | category | flops | bytes accessed | tf_op | source)
XLA Modules:
  0.0 357.8 jit_solution(3680428190750341081)
XLA Ops:
  13.3 6.5 %all-to-all-start = ((bf16[8,64,1024]{2,1,0:T(8,128)(2,1)}), bf16[8,64,1024]{2,1,0:T(8,128)(2,1)}, u32[]{:S(2)}, u32[]{:S(2)}) async-start(bf16[8,64,1024]{2,1,0:T(8,128)(2,1)} %bitcast.2), calls=%async_computation | async-start | bytes 2097152 | tf_op jit(solution)/shard_map/all_to_all | solution.py:702
  22.8 3.8 %collective-permute-start.6 = (s32[1,4]{1,0:T(1,128)S(1)}, s32[1,4]{1,0:T(1,128)S(1)}, u32[]{:S(2)}, u32[]{:S(2)}) collective-permute-start(s32[1,4]{1,0:T(1,128)S(1)} %copy-done.29), channel_id=1, source_target_pairs={{0,24},{1,25},{2,26},{3,27},{4,28},{5,29},{6,30},{7,31},{8,16},{9,... | collective-permute-start | bytes 56 | tf_op jit(solution)/shard_map/ppermute | solution.py:782
  27.7 16.3 %collective-permute-done.1 = bf16[240,2048]{1,0:T(8,128)(2,1)S(1)} collective-permute-done((bf16[240,2048]{1,0:T(8,128)(2,1)S(1)}, bf16[240,2048]{1,0:T(8,128)(2,1)S(1)}, u32[]{:S(2)}, u32[]{:S(2)}) %collective-permute-start.1) | collective-permute-done | bytes 983072 | tf_op jit(solution)/shard_map/ppermute | solution.py:782
  46.5 4.3 %all-to-all-start.1 = ((bf16[8,64,1152]{2,1,0:T(8,128)(2,1)}), bf16[8,64,1152]{2,1,0:T(8,128)(2,1)}, u32[]{:S(2)}, u32[]{:S(2)}) async-start(bf16[8,64,1152]{2,1,0:T(8,128)(2,1)} %bitcast.4), calls=%async_computation.1 | async-start | bytes 2359296 | tf_op jit(solution)/shard_map/all_to_all | solution.py:702
  61.5 16.5 %collective-permute-done.3.refs_7_.refs_9_ = bf16[512,1024]{1,0:T(8,128)(2,1)} collective-permute-done((bf16[512,1024]{1,0:T(8,128)(2,1)}, bf16[512,1024]{1,0:T(8,128)(2,1)}, u32[]{:S(2)}, u32[]{:S(2)}) %collective-permute-start.3) | collective-permute-done | bytes 1048608 | tf_op jit(solution)/shard_map/ppermute | solution.py:782
  93.3 28.2 %collective-permute-done.11.refs_6_ = bf16[112,2048]{1,0:T(8,128)(2,1)S(1)} collective-permute-done((bf16[112,2048]{1,0:T(8,128)(2,1)S(1)}, bf16[112,2048]{1,0:T(8,128)(2,1)S(1)}, u32[]{:S(2)}, u32[]{:S(2)}) %collective-permute-start.11) | collective-permute-done | bytes 458784 | tf_op jit(solution)/shard_map/ppermute | solution.py:782
  124.8 9.2 %collective-permute-done.12.refs_7_ = bf16[128,2048]{1,0:T(8,128)(2,1)S(1)} collective-permute-done((bf16[128,2048]{1,0:T(8,128)(2,1)S(1)}, bf16[128,2048]{1,0:T(8,128)(2,1)S(1)}, u32[]{:S(2)}, u32[]{:S(2)}) %collective-permute-start.12) | collective-permute-done | bytes 524320 | tf_op jit(solution)/shard_map/ppermute | solution.py:782
  143.0 9.1 %collective-permute-done.15.refs_14_.refs_16_ = bf16[256,1152]{1,0:T(8,128)(2,1)S(1)} collective-permute-done((bf16[256,1152]{1,0:T(8,128)(2,1)S(1)}, bf16[256,1152]{1,0:T(8,128)(2,1)S(1)}, u32[]{:S(2)}, u32[]{:S(2)}) %collective-permute-start.15) | collective-permute-done | bytes 589856 | tf_op jit(solution)/shard_map/ppermute | solution.py:782
  154.1 24.3 %forward.1 = (bf16[1024,960]{1,0:T(8,128)(2,1)}, bf16[1024,768]{1,0:T(8,128)(2,1)}, f32[1024,1408]{1,0:T(8,128)}, bf16[1024,2048]{1,0:T(8,128)(2,1)}) custom-call(bf16[1024,2048]{1,0:T(8,128)(2,1)} %all-gather.3.cloned.1.call-done.refs_0_.lhs_any, f32[8,768]{1,0:T(8,128)} %broadcast_in_dim.101.refs_1_, f32[1024,128]{1,0:T(8,128)} %copy.48.refs_2_.refs_3_, ...), custom_call_target="tpu_custom_call" | custom-call | flops 1 | bytes 1 | tf_op jit(solution)/shard_map/forward/pallas_call | solution.py:279
  178.7 9.8 %mixer_grad.1 = (bf16[224,2048]{1,0:T(8,128)(2,1)}, bf16[256,2048]{1,0:T(8,128)(2,1)}, bf16[128,2048]{1,0:T(8,128)(2,1)}, bf16[112,2048]{1,0:T(8,128)(2,1)}, bf1...) custom-call(s32[1]{0:T(128)} %bitcast.8.lane_ref, bf16[1024,960]{1,0:T(8,128)(2,1)} %get-tuple-element.154.joined_any, ...), custom_call_target="tpu_custom_call" | custom-call | flops 1 | bytes 1 | tf_op jit(solution)/shard_map/mixer_grad/pallas_call | solution.py:515
  189.3 29.8 %backward.1 = (bf16[1024,768]{1,0:T(8,128)(2,1)}, bf16[1024,1408]{1,0:T(8,128)(2,1)}, bf16[1024,2048]{1,0:T(8,128)(2,1)}, f32[8,768]{1,0:T(8,128)}) custom-call(bf16[1024,2048]{1,0:T(8,128)(2,1)} %all-gather.5.cloned.1.call-done.masked_any.refs_0_, f32[1024,1408]{1,0:T(8,128)} %get-tuple-element.165.refs_1_, bf16[1024,768]{1,0:T(8,128)(2,1)} %get-tuple-element.166.refs_2_, ...), custom_call_target="tpu_custom_call" | custom-call | flops 1 | bytes 1 | tf_op jit(solution)/shard_map/backward/pallas_call | solution.py:321
  219.8 7.5 %weight_grad.4 = (bf16[512,1408]{1,0:T(8,128)(2,1)}, bf16[512,1408]{1,0:T(8,128)(2,1)}) custom-call(s32[4]{0:T(128)S(1)} %copy-done.7, bf16[1024,2048]{1,0:T(8,128)(2,1)} %all-gather.3.cloned.1.call-done.refs_0_.lhs_any, bf16[1024,1408]{1,0:T(8,128)(2,1)} %get-tuple-element.173.grad_any), custom_call_target="tpu_custom_call" | custom-call | flops 1 | bytes 1 | tf_op jit(solution)/shard_map/weight_grad/pallas_call | solution.py:391
  230.6 7.8 %weight_grad.5 = (bf16[256,1408]{1,0:T(8,128)(2,1)}, bf16[256,1408]{1,0:T(8,128)(2,1)}, bf16[256,1408]{1,0:T(8,128)(2,1)}, bf16[256,1408]{1,0:T(8,128)(2,1)}) custom-call(s32[4]{0:T(128)S(1)} %copy-done.6, bf16[1024,2048]{1,0:T(8,128)(2,1)} %all-gather.3.cloned.1.call-done.refs_0_.lhs_any, bf16[1024,1408]{1,0:T(8,128)(2,1)} %get-tuple-element.173.grad_any), custom_call_target="tpu_custom_call" | custom-call | flops 1 | bytes 1 | tf_op jit(solution)/shard_map/weight_grad/pallas_call | solution.py:391
  238.4 5.4 %weight_grad.6 = (bf16[512,768]{1,0:T(8,128)(2,1)}, bf16[512,768]{1,0:T(8,128)(2,1)}) custom-call(s32[4]{0:T(128)S(1)} %copy-done.7, bf16[1024,2048]{1,0:T(8,128)(2,1)} %all-gather.3.cloned.1.call-done.refs_0_.lhs_any, bf16[1024,768]{1,0:T(8,128)(2,1)} %get-tuple-element.182.grad_any), custom_call_target="tpu_custom_call" | custom-call | flops 1 | bytes 1 | tf_op jit(solution)/shard_map/weight_grad/pallas_call | solution.py:391
  243.8 5.4 %weight_grad.7 = (bf16[256,768]{1,0:T(8,128)(2,1)}, bf16[256,768]{1,0:T(8,128)(2,1)}, bf16[256,768]{1,0:T(8,128)(2,1)}, bf16[256,768]{1,0:T(8,128)(2,1)}) custom-call(s32[4]{0:T(128)S(1)} %copy-done.6, bf16[1024,2048]{1,0:T(8,128)(2,1)} %all-gather.3.cloned.1.call-done.refs_0_.lhs_any, bf16[1024,768]{1,0:T(8,128)(2,1)} %get-tuple-element.182.grad_any), custom_call_target="tpu_custom_call" | custom-call | flops 1 | bytes 1 | tf_op jit(solution)/shard_map/weight_grad/pallas_call | solution.py:391
  251.5 7.5 %collective-permute-done.18.from_x = bf16[512,1408]{1,0:T(8,128)(2,1)S(1)} collective-permute-done((bf16[512,1408]{1,0:T(8,128)(2,1)}, bf16[512,1408]{1,0:T(8,128)(2,1)S(1)}, u32[]{:S(2)}, u32[]{:S(2)}) %collective-permute-start.18) | collective-permute-done | bytes 1441824 | tf_op jit(solution)/shard_map/ppermute | solution.py:782
  266.2 9.4 %collective-permute-done.21.last_y = bf16[256,1408]{1,0:T(8,128)(2,1)S(1)} collective-permute-done((bf16[256,1408]{1,0:T(8,128)(2,1)}, bf16[256,1408]{1,0:T(8,128)(2,1)S(1)}, u32[]{:S(2)}, u32[]{:S(2)}) %collective-permute-start.21) | collective-permute-done | bytes 720928 | tf_op jit(solution)/shard_map/ppermute | solution.py:782
  277.7 2.9 sum_lanes.2
  280.6 3.8 %all-to-all-start.2 = ((bf16[8,64,1408]{2,1,0:T(8,128)(2,1)}), bf16[8,64,1408]{2,1,0:T(8,128)(2,1)S(1)}, u32[]{:S(2)}, u32[]{:S(2)}) async-start(bf16[8,64,1408]{2,1,0:T(8,128)(2,1)} %bitcast.53), calls=%async_computation.4 | async-start | bytes 2883584 | tf_op jit(solution)/shard_map/all_to_all | solution.py:702
  301.7 2.8 fusion.14
  314.4 5.7 %collective-permute-done.27 = f32[4,2,320]{2,1,0:T(2,128)S(1)} collective-permute-done((f32[4,2,320]{2,1,0:T(2,128)S(1)}, f32[4,2,320]{2,1,0:T(2,128)S(1)}, u32[]{:S(2)}, u32[]{:S(2)}) %collective-permute-start.27) | collective-permute-done | bytes 10272 | tf_op jit(solution)/shard_map/ppermute | solution.py:782
  322.5 3.5 all-to-all-start.3
  337.3 5.5 %collective-permute-done.30 = f32[2,320]{1,0:T(2,128)S(1)} collective-permute-done((f32[2,320]{1,0:T(2,128)S(1)}, f32[2,320]{1,0:T(2,128)S(1)}, u32[]{:S(2)}, u32[]{:S(2)}) %collective-permute-start.30) | collective-permute-done | bytes 2592 | tf_op jit(solution)/shard_map/ppermute | solution.py:782
  345.7 3.0 sum_mixer.1
  (233 shorter events, 115.5 us)
Async XLA Ops:
  13.3 33.2 %all-to-all-start = ((bf16[8,64,1024]{2,1,0:T(8,128)(2,1)}), bf16[8,64,1024]{2,1,0:T(8,128)(2,1)}, u32[]{:S(2)}, u32[]{:S(2)}) async-start(bf16[8,64,1024]{2,1,0:T(8,128)(2,1)} %bitcast.2), calls=%async_computation | async-start | bytes 2097152 | tf_op jit(solution)/shard_map/all_to_all | solution.py:702
  19.8 24.2 %collective-permute-start.1 = (bf16[240,2048]{1,0:T(8,128)(2,1)S(1)}, bf16[240,2048]{1,0:T(8,128)(2,1)S(1)}, u32[]{:S(2)}, u32[]{:S(2)}) collective-permute-start(bf16[240,2048]{1,0:T(8,128)(2,1)S(1)} %join_rows.1), channel_id=1, source_target_pairs={{0,4},{1,5},{2,6},{3,7},{4,0},{5,1},{6,2},{7,3},{8,12},{9,13},{10,... | collective-permute-start | bytes 2949128 | tf_op jit(solution)/shard_map/ppermute | solution.py:782
  21.3 24.0 %collective-permute-start = (bf16[240,2048]{1,0:T(8,128)(2,1)S(1)}, bf16[240,2048]{1,0:T(8,128)(2,1)}, u32[]{:S(2)}, u32[]{:S(2)}) collective-permute-start(bf16[240,2048]{1,0:T(8,128)(2,1)S(1)} %join_rows.1), channel_id=1, source_target_pairs={{0,2},{1,3},{2,0},{3,1},{4,6},{5,7},{6,4},{7,5},{8,10},{9,11},{10,... | collective-permute-start | bytes 2949128 | tf_op jit(solution)/shard_map/ppermute | solution.py:782
  22.8 35.3 %collective-permute-start.6 = (s32[1,4]{1,0:T(1,128)S(1)}, s32[1,4]{1,0:T(1,128)S(1)}, u32[]{:S(2)}, u32[]{:S(2)}) collective-permute-start(s32[1,4]{1,0:T(1,128)S(1)} %copy-done.29), channel_id=1, source_target_pairs={{0,24},{1,25},{2,26},{3,27},{4,28},{5,29},{6,30},{7,31},{8,16},{9,... | collective-permute-start | bytes 56 | tf_op jit(solution)/shard_map/ppermute | solution.py:782
  26.6 31.4 %collective-permute-start.5 = (s32[1,4]{1,0:T(1,128)S(1)}, s32[1,4]{1,0:T(1,128)S(1)}, u32[]{:S(2)}, u32[]{:S(2)}) collective-permute-start(s32[1,4]{1,0:T(1,128)S(1)} %copy-done.29), channel_id=1, source_target_pairs={{0,16},{1,17},{2,18},{3,19},{4,20},{5,21},{6,22},{7,23},{8,24},{9,... | collective-permute-start | bytes 56 | tf_op jit(solution)/shard_map/ppermute | solution.py:782
  26.6 31.4 %collective-permute-start.4 = (s32[1,4]{1,0:T(1,128)S(1)}, s32[1,4]{1,0:T(1,128)S(1)}, u32[]{:S(2)}, u32[]{:S(2)}) collective-permute-start(s32[1,4]{1,0:T(1,128)S(1)} %copy-done.29), channel_id=1, source_target_pairs={{0,8},{1,9},{2,10},{3,11},{4,12},{5,13},{6,14},{7,15},{8,0},{9,1},... | collective-permute-start | bytes 56 | tf_op jit(solution)/shard_map/ppermute | solution.py:782
  46.5 33.7 %all-to-all-start.1 = ((bf16[8,64,1152]{2,1,0:T(8,128)(2,1)}), bf16[8,64,1152]{2,1,0:T(8,128)(2,1)}, u32[]{:S(2)}, u32[]{:S(2)}) async-start(bf16[8,64,1152]{2,1,0:T(8,128)(2,1)} %bitcast.4), calls=%async_computation.1 | async-start | bytes 2359296 | tf_op jit(solution)/shard_map/all_to_all | solution.py:702
  50.8 102.5 %all-gather.3.cloned.1.call-start = ((), (), s32[]{:S(2)}) async-start(), calls=%async_computation.6 | async-start | bytes 4718592 | tf_op jit(solution)/shard_map/all_gather | solution.py:688
  52.2 25.8 %collective-permute-start.3 = (bf16[512,1024]{1,0:T(8,128)(2,1)}, bf16[512,1024]{1,0:T(8,128)(2,1)}, u32[]{:S(2)}, u32[]{:S(2)}) collective-permute-start(bf16[512,1024]{1,0:T(8,128)(2,1)} %bitcast.3.refs_5_.refs_7_), channel_id=1, source_target_pairs={{0,4},{1,5},{2,6},{3,7},{4,0},{5,1},{6,2},{7,3},{8,12},{9,13},{10,... | collective-permute-start | bytes 3145736 | tf_op jit(solution)/shard_map/ppermute | solution.py:782
  53.8 25.4 %collective-permute-start.2 = (bf16[512,1024]{1,0:T(8,128)(2,1)}, bf16[512,1024]{1,0:T(8,128)(2,1)}, u32[]{:S(2)}, u32[]{:S(2)}) collective-permute-start(bf16[512,1024]{1,0:T(8,128)(2,1)} %bitcast.3.refs_5_.refs_7_), channel_id=1, source_target_pairs={{0,2},{1,3},{2,0},{3,1},{4,6},{5,7},{6,4},{7,5},{8,10},{9,11},{10,... | collective-permute-start | bytes 3145736 | tf_op jit(solution)/shard_map/ppermute | solution.py:782
  80.2 98.4 %all-gather.5.cloned.1.call-start = ((), (), s32[]{:S(2)}) async-start(), calls=%async_computation.8 | async-start | bytes 4718592 | tf_op jit(solution)/shard_map/all_gather | solution.py:688
  81.0 168.3 %reduce-scatter.3.cloned.1.call-start = ((), (), s32[]{:S(2)}) async-start(), calls=%async_computation.7 | async-start | bytes 4718592 | tf_op jit(solution)/shard_map/reduce_scatter | solution.py:693
  82.6 52.8 %collective-permute-start.8 = (bf16[512,1152]{1,0:T(8,128)(2,1)}, bf16[512,1152]{1,0:T(8,128)(2,1)}, u32[]{:S(2)}, u32[]{:S(2)}) collective-permute-start(bf16[512,1152]{1,0:T(8,128)(2,1)} %bitcast.5.refs_10_.refs_12_), channel_id=1, source_target_pairs={{0,4},{1,5},{2,6},{3,7},{4,0},{5,1},{6,2},{7,3},{8,12},{9,13},{10,... | collective-permute-start | bytes 3538952 | tf_op jit(solution)/shard_map/ppermute | solution.py:782
  84.1 51.3 %collective-permute-start.7 = (bf16[512,1152]{1,0:T(8,128)(2,1)}, bf16[512,1152]{1,0:T(8,128)(2,1)}, u32[]{:S(2)}, u32[]{:S(2)}) collective-permute-start(bf16[512,1152]{1,0:T(8,128)(2,1)} %bitcast.5.refs_10_.refs_12_), channel_id=1, source_target_pairs={{0,2},{1,3},{2,0},{3,1},{4,6},{5,7},{6,4},{7,5},{8,10},{9,11},{10,... | collective-permute-start | bytes 3538952 | tf_op jit(solution)/shard_map/ppermute | solution.py:782
  85.6 35.9 %collective-permute-start.11 = (bf16[112,2048]{1,0:T(8,128)(2,1)S(1)}, bf16[112,2048]{1,0:T(8,128)(2,1)S(1)}, u32[]{:S(2)}, u32[]{:S(2)}) collective-permute-start(bf16[112,2048]{1,0:T(8,128)(2,1)S(1)} %slice.59.refs_2_), channel_id=1, source_target_pairs={{0,4},{1,5},{2,6},{3,7},{4,0},{5,1},{6,2},{7,3},{8,12},{9,13},{10,... | collective-permute-start | bytes 1376264 | tf_op jit(solution)/shard_map/ppermute | solution.py:782
  89.9 45.5 %collective-permute-start.10 = (bf16[256,1024]{1,0:T(8,128)(2,1)}, bf16[256,1024]{1,0:T(8,128)(2,1)}, u32[]{:S(2)}, u32[]{:S(2)}) collective-permute-start(bf16[256,1024]{1,0:T(8,128)(2,1)} %slice.64), channel_id=1, source_target_pairs={{0,2},{1,3},{2,0},{3,1},{4,6},{5,7},{6,4},{7,5},{8,10},{9,11},{10,... | collective-permute-start | bytes 1572872 | tf_op jit(solution)/shard_map/ppermute | solution.py:782
  90.4 45.0 %collective-permute-start.9 = (bf16[256,1024]{1,0:T(8,128)(2,1)}, bf16[256,1024]{1,0:T(8,128)(2,1)}, u32[]{:S(2)}, u32[]{:S(2)}) collective-permute-start(bf16[256,1024]{1,0:T(8,128)(2,1)} %slice.63), channel_id=1, source_target_pairs={{0,4},{1,5},{2,6},{3,7},{4,0},{5,1},{6,2},{7,3},{8,12},{9,13},{10,... | collective-permute-start | bytes 1572872 | tf_op jit(solution)/shard_map/ppermute | solution.py:782
  178.4 109.1 %reduce-scatter.5.cloned.1.call-start = ((), (), s32[]{:S(2)}) async-start(), calls=%async_computation.9 | async-start | bytes 4718592 | tf_op jit(solution)/shard_map/reduce_scatter | solution.py:693
  188.4 30.7 %collective-permute-start.17 = (bf16[256,2048]{1,0:T(8,128)(2,1)}, bf16[256,2048]{1,0:T(8,128)(2,1)}, u32[]{:S(2)}, u32[]{:S(2)}) collective-permute-start(bf16[256,2048]{1,0:T(8,128)(2,1)} %get-tuple-element.163), channel_id=1, source_target_pairs={{0,4},{1,5},{2,6},{3,7},{4,0},{5,1},{6,2},{7,3},{8,12},{9,13},{10,... | collective-permute-start | bytes 3145736 | tf_op jit(solution)/shard_map/ppermute | solution.py:782
  188.7 30.4 %collective-permute-start.16 = (bf16[224,2048]{1,0:T(8,128)(2,1)}, bf16[224,2048]{1,0:T(8,128)(2,1)}, u32[]{:S(2)}, u32[]{:S(2)}) collective-permute-start(bf16[224,2048]{1,0:T(8,128)(2,1)} %get-tuple-element.162), channel_id=1, source_target_pairs={{0,2},{1,3},{2,0},{3,1},{4,6},{5,7},{6,4},{7,5},{8,10},{9,11},{10,... | collective-permute-start | bytes 2752520 | tf_op jit(solution)/shard_map/ppermute | solution.py:782
  227.3 31.7 %collective-permute-start.18 = (bf16[512,1408]{1,0:T(8,128)(2,1)}, bf16[512,1408]{1,0:T(8,128)(2,1)S(1)}, u32[]{:S(2)}, u32[]{:S(2)}) collective-permute-start(bf16[512,1408]{1,0:T(8,128)(2,1)} %get-tuple-element.184), channel_id=1, source_target_pairs={{0,2},{1,3},{2,0},{3,1},{4,6},{5,7},{6,4},{7,5},{8,10},{9,11},{10,... | collective-permute-start | bytes 4325384 | tf_op jit(solution)/shard_map/ppermute | solution.py:782
  228.8 30.6 %collective-permute-start.19 = (bf16[512,1408]{1,0:T(8,128)(2,1)}, bf16[512,1408]{1,0:T(8,128)(2,1)}, u32[]{:S(2)}, u32[]{:S(2)}) collective-permute-start(bf16[512,1408]{1,0:T(8,128)(2,1)} %get-tuple-element.185), channel_id=1, source_target_pairs={{0,4},{1,5},{2,6},{3,7},{4,0},{5,1},{6,2},{7,3},{8,12},{9,13},{10,... | collective-permute-start | bytes 4325384 | tf_op jit(solution)/shard_map/ppermute | solution.py:782
  280.6 41.9 %all-to-all-start.2 = ((bf16[8,64,1408]{2,1,0:T(8,128)(2,1)}), bf16[8,64,1408]{2,1,0:T(8,128)(2,1)S(1)}, u32[]{:S(2)}, u32[]{:S(2)}) async-start(bf16[8,64,1408]{2,1,0:T(8,128)(2,1)} %bitcast.53), calls=%async_computation.4 | async-start | bytes 2883584 | tf_op jit(solution)/shard_map/all_to_all | solution.py:702
  322.5 26.2 %all-to-all-start.3 = ((bf16[8,64,768]{2,1,0:T(8,128)(2,1)}), bf16[8,64,768]{2,1,0:T(8,128)(2,1)S(1)}, u32[]{:S(2)}, u32[]{:S(2)}) async-start(bf16[8,64,768]{2,1,0:T(8,128)(2,1)} %bitcast.55), calls=%async_computation.5 | async-start | bytes 1572864 | tf_op jit(solution)/shard_map/all_to_all | solution.py:702
  (49 other events, 433.6 us)
Sparse Core Ops, SparseCore 0:
  80.4 46.3 all-gather.2
  128.9 45.8 all-gather.4
  178.5 47.3 reduce-scatter.2
  228.0 48.0 reduce-scatter.4

commit v6 on v4

--- a/solution.py
+++ b/solution.py
@@ -744,7 +744,6 @@
         norm, branch = self.scatter_tokens(norm), self.scatter_tokens(branch)
         part_qkv, part_ff = [self.exchange(part) for part in parts]
         grad_tokens, stats = tail(norm, bias_part)
-        stats = self.scatter_stats(stats)
         return grads[0], grads[1], part_qkv, part_ff, branch, grad_tokens, stats
 
     def relative(self, blocks, axis):
@@ -880,7 +879,6 @@
         mix_first, mix = mix[:2], mix[2:]
         mix_x, mix_y = add_call(mix_first, mix[0], mix[1])
         mix_last = self.send(mix_x, 1), self.send(mix_y, 2)
-        stats = self.scatter_stats(stats)
         grad_w_out, grad_w_down = mixer_sum_call(mix[2], mix[3], mix_first, mix_last, own)
         return grad_w_out, grad_w_down, part_qkv, part_ff, branch, grad_tokens, stats
 
@@ -1007,6 +1005,8 @@
     grad_w_gate, grad_w_up = unpack_call(
         part_ff, 1, plan, tp, [w_gate.shape[1], w_up.shape[1]]
     )
+    stats, grad_w_gate, grad_w_up = tie(stats, grad_w_gate, grad_w_up)
+    stats = net.scatter_stats(stats)
     part_qkv, stats, grad_w_gate, grad_w_up = tie(part_qkv, stats, grad_w_gate, grad_w_up)
     (grad_w_qkv,) = unpack_call(part_qkv, 0, plan, tp, [w_qkv.shape[1]])
     return (

time: 361 us -> 360 us (level)
  transfers between devices with their start and end apart: 43 -> 43, of which waited for: 18 -> 19; matrix products, arithmetic and copies ran while one was open for 13% -> 13% of each run, Pallas kernels for 29% -> 29%
where the time goes in v6:
time: 360 us; the launch traced here: 358 us
  waiting for transfers between devices  120 us (33%)
  Pallas kernels  110 us (31%)
  starting transfers between devices  60.7 us (17%)
  local copies, waits for them, and re-layouts  28.5 us (8%)
  other arithmetic  24.2 us (7%)
  between operations  14.5 us (4%)
    ppermute x35, waiting for transfers between devices, send(): return lax.ppermute(value, AXES, pairs)  117 us
    ppermute x35, starting transfers between devices, send(): return lax.ppermute(value, AXES, pairs)  42.3 us
    pallas_call x1, Pallas kernels, backward_call(): pl.pallas_call(functools.partial(backward_kernel, sizes, count, block), g...  29.8 us
    pallas_call x4, Pallas kernels, product_call(): pl.pallas_call(kernel, in_specs=[pl.BlockSpec(memory_space=pltpu.SMEM), A...  26.1 us
    pallas_call x1, Pallas kernels, forward_call(): pl.pallas_call(functools.partial(forward_kernel, sizes, count, block), gr...  24.3 us
    all_to_all x4, starting transfers between devices, exchange(): lax.all_to_all(part, self.token_axes, split_axis=0, concat_axis=0, tiled=...  18.1 us
    pallas_call x1, Pallas kernels, mixer_grad_call(): pl.pallas_call(kernel, in_specs=[pl.BlockSpec(memory_space=pltpu.SMEM), A...  9.78 us
  transfers between devices with their start and end apart: 43, of which 19 were waited for; matrix products, arithmetic and copies ran while one was open for 13% of the time, Pallas kernels for 29%

profile of v6, /device:TPU:0, one launch (start us, length us, event | category | flops | bytes accessed | tf_op | source)
XLA Modules:
  0.0 358.2 jit_solution(3281452114868273142)
XLA Ops:
  9.6 4.1 %pack_columns.1 = (bf16[512,1024]{1,0:T(8,128)(2,1)}, bf16[512,1152]{1,0:T(8,128)(2,1)}) custom-call(bf16[64,6144]{1,0:T(8,128)(2,1)} %refs_0_.3, bf16[64,5632]{1,0:T(8,128)(2,1)} %refs_1_.3, bf16[64,5632]{1,0:T(8,128)(2,1)} %refs_2_.1), custom_call_target="tpu_custom_call" | custom-call | tf_op jit(solution)/shard_map/pack_columns/pallas_call | solution.py:573
  13.7 6.5 %all-to-all-start = ((bf16[8,64,1024]{2,1,0:T(8,128)(2,1)}), bf16[8,64,1024]{2,1,0:T(8,128)(2,1)}, u32[]{:S(2)}, u32[]{:S(2)}) async-start(bf16[8,64,1024]{2,1,0:T(8,128)(2,1)} %bitcast.2), calls=%async_computation | async-start | bytes 2097152 | tf_op jit(solution)/shard_map/all_to_all | solution.py:705
  23.2 3.8 %collective-permute-start.6 = (s32[1,4]{1,0:T(1,128)S(1)}, s32[1,4]{1,0:T(1,128)S(1)}, u32[]{:S(2)}, u32[]{:S(2)}) collective-permute-start(s32[1,4]{1,0:T(1,128)S(1)} %copy-done.26), channel_id=1, source_target_pairs={{0,24},{1,25},{2,26},{3,27},{4,28},{5,29},{6,30},{7,31},{8,16},{9,... | collective-permute-start | bytes 56 | tf_op jit(solution)/shard_map/ppermute | solution.py:785
  28.1 16.3 %collective-permute-done.1 = bf16[240,2048]{1,0:T(8,128)(2,1)S(1)} collective-permute-done((bf16[240,2048]{1,0:T(8,128)(2,1)S(1)}, bf16[240,2048]{1,0:T(8,128)(2,1)S(1)}, u32[]{:S(2)}, u32[]{:S(2)}) %collective-permute-start.1) | collective-permute-done | bytes 983072 | tf_op jit(solution)/shard_map/ppermute | solution.py:785
  46.9 4.3 %all-to-all-start.1 = ((bf16[8,64,1152]{2,1,0:T(8,128)(2,1)}), bf16[8,64,1152]{2,1,0:T(8,128)(2,1)}, u32[]{:S(2)}, u32[]{:S(2)}) async-start(bf16[8,64,1152]{2,1,0:T(8,128)(2,1)} %bitcast.4), calls=%async_computation.1 | async-start | bytes 2359296 | tf_op jit(solution)/shard_map/all_to_all | solution.py:705
  61.8 16.5 %collective-permute-done.3.refs_7_.refs_9_ = bf16[512,1024]{1,0:T(8,128)(2,1)} collective-permute-done((bf16[512,1024]{1,0:T(8,128)(2,1)}, bf16[512,1024]{1,0:T(8,128)(2,1)}, u32[]{:S(2)}, u32[]{:S(2)}) %collective-permute-start.3) | collective-permute-done | bytes 1048608 | tf_op jit(solution)/shard_map/ppermute | solution.py:785
  93.7 28.2 %collective-permute-done.11.refs_6_ = bf16[112,2048]{1,0:T(8,128)(2,1)S(1)} collective-permute-done((bf16[112,2048]{1,0:T(8,128)(2,1)S(1)}, bf16[112,2048]{1,0:T(8,128)(2,1)S(1)}, u32[]{:S(2)}, u32[]{:S(2)}) %collective-permute-start.11) | collective-permute-done | bytes 458784 | tf_op jit(solution)/shard_map/ppermute | solution.py:785
  125.2 9.2 %collective-permute-done.12.refs_7_ = bf16[128,2048]{1,0:T(8,128)(2,1)S(1)} collective-permute-done((bf16[128,2048]{1,0:T(8,128)(2,1)S(1)}, bf16[128,2048]{1,0:T(8,128)(2,1)S(1)}, u32[]{:S(2)}, u32[]{:S(2)}) %collective-permute-start.12) | collective-permute-done | bytes 524320 | tf_op jit(solution)/shard_map/ppermute | solution.py:785
  143.5 9.0 %collective-permute-done.15.refs_14_.refs_16_ = bf16[256,1152]{1,0:T(8,128)(2,1)S(1)} collective-permute-done((bf16[256,1152]{1,0:T(8,128)(2,1)S(1)}, bf16[256,1152]{1,0:T(8,128)(2,1)S(1)}, u32[]{:S(2)}, u32[]{:S(2)}) %collective-permute-start.15) | collective-permute-done | bytes 589856 | tf_op jit(solution)/shard_map/ppermute | solution.py:785
  154.5 24.3 %forward.1 = (bf16[1024,960]{1,0:T(8,128)(2,1)}, bf16[1024,768]{1,0:T(8,128)(2,1)}, f32[1024,1408]{1,0:T(8,128)}, bf16[1024,2048]{1,0:T(8,128)(2,1)}) custom-call(bf16[1024,2048]{1,0:T(8,128)(2,1)} %all-gather.3.cloned.1.call-done.refs_0_.lhs_any, f32[8,768]{1,0:T(8,128)} %broadcast_in_dim.101.refs_1_, f32[1024,128]{1,0:T(8,128)} %copy.48.refs_2_.refs_3_, ...), custom_call_target="tpu_custom_call" | custom-call | flops 1 | bytes 1 | tf_op jit(solution)/shard_map/forward/pallas_call | solution.py:279
  179.0 9.8 %mixer_grad.1 = (bf16[224,2048]{1,0:T(8,128)(2,1)}, bf16[256,2048]{1,0:T(8,128)(2,1)}, bf16[128,2048]{1,0:T(8,128)(2,1)}, bf16[112,2048]{1,0:T(8,128)(2,1)}, bf1...) custom-call(s32[1]{0:T(128)} %bitcast.8.lane_ref, bf16[1024,960]{1,0:T(8,128)(2,1)} %get-tuple-element.154.joined_any, ...), custom_call_target="tpu_custom_call" | custom-call | flops 1 | bytes 1 | tf_op jit(solution)/shard_map/mixer_grad/pallas_call | solution.py:515
  189.7 29.8 %backward.1 = (bf16[1024,768]{1,0:T(8,128)(2,1)}, bf16[1024,1408]{1,0:T(8,128)(2,1)}, bf16[1024,2048]{1,0:T(8,128)(2,1)}, f32[8,768]{1,0:T(8,128)}) custom-call(bf16[1024,2048]{1,0:T(8,128)(2,1)} %all-gather.5.cloned.1.call-done.masked_any.refs_0_, f32[1024,1408]{1,0:T(8,128)} %get-tuple-element.165.refs_1_, bf16[1024,768]{1,0:T(8,128)(2,1)} %get-tuple-element.166.refs_2_, ...), custom_call_target="tpu_custom_call" | custom-call | flops 1 | bytes 1 | tf_op jit(solution)/shard_map/backward/pallas_call | solution.py:321
  220.2 7.5 %weight_grad.4 = (bf16[512,1408]{1,0:T(8,128)(2,1)}, bf16[512,1408]{1,0:T(8,128)(2,1)}) custom-call(s32[4]{0:T(128)S(1)} %copy-done.4, bf16[1024,2048]{1,0:T(8,128)(2,1)} %all-gather.3.cloned.1.call-done.refs_0_.lhs_any, bf16[1024,1408]{1,0:T(8,128)(2,1)} %get-tuple-element.173.grad_any), custom_call_target="tpu_custom_call" | custom-call | flops 1 | bytes 1 | tf_op jit(solution)/shard_map/weight_grad/pallas_call | solution.py:391
  231.0 7.8 %weight_grad.5 = (bf16[256,1408]{1,0:T(8,128)(2,1)}, bf16[256,1408]{1,0:T(8,128)(2,1)}, bf16[256,1408]{1,0:T(8,128)(2,1)}, bf16[256,1408]{1,0:T(8,128)(2,1)}) custom-call(s32[4]{0:T(128)S(1)} %copy-done.3, bf16[1024,2048]{1,0:T(8,128)(2,1)} %all-gather.3.cloned.1.call-done.refs_0_.lhs_any, bf16[1024,1408]{1,0:T(8,128)(2,1)} %get-tuple-element.173.grad_any), custom_call_target="tpu_custom_call" | custom-call | flops 1 | bytes 1 | tf_op jit(solution)/shard_map/weight_grad/pallas_call | solution.py:391
  238.8 5.4 %weight_grad.6 = (bf16[512,768]{1,0:T(8,128)(2,1)}, bf16[512,768]{1,0:T(8,128)(2,1)}) custom-call(s32[4]{0:T(128)S(1)} %copy-done.4, bf16[1024,2048]{1,0:T(8,128)(2,1)} %all-gather.3.cloned.1.call-done.refs_0_.lhs_any, bf16[1024,768]{1,0:T(8,128)(2,1)} %get-tuple-element.182.grad_any), custom_call_target="tpu_custom_call" | custom-call | flops 1 | bytes 1 | tf_op jit(solution)/shard_map/weight_grad/pallas_call | solution.py:391
  244.2 5.4 %weight_grad.7 = (bf16[256,768]{1,0:T(8,128)(2,1)}, bf16[256,768]{1,0:T(8,128)(2,1)}, bf16[256,768]{1,0:T(8,128)(2,1)}, bf16[256,768]{1,0:T(8,128)(2,1)}) custom-call(s32[4]{0:T(128)S(1)} %copy-done.3, bf16[1024,2048]{1,0:T(8,128)(2,1)} %all-gather.3.cloned.1.call-done.refs_0_.lhs_any, bf16[1024,768]{1,0:T(8,128)(2,1)} %get-tuple-element.182.grad_any), custom_call_target="tpu_custom_call" | custom-call | flops 1 | bytes 1 | tf_op jit(solution)/shard_map/weight_grad/pallas_call | solution.py:391
  251.9 7.5 %collective-permute-done.18.from_x = bf16[512,1408]{1,0:T(8,128)(2,1)S(1)} collective-permute-done((bf16[512,1408]{1,0:T(8,128)(2,1)}, bf16[512,1408]{1,0:T(8,128)(2,1)S(1)}, u32[]{:S(2)}, u32[]{:S(2)}) %collective-permute-start.18) | collective-permute-done | bytes 1441824 | tf_op jit(solution)/shard_map/ppermute | solution.py:785
  266.6 9.4 %collective-permute-done.21.last_y = bf16[256,1408]{1,0:T(8,128)(2,1)S(1)} collective-permute-done((bf16[256,1408]{1,0:T(8,128)(2,1)}, bf16[256,1408]{1,0:T(8,128)(2,1)S(1)}, u32[]{:S(2)}, u32[]{:S(2)}) %collective-permute-start.21) | collective-permute-done | bytes 720928 | tf_op jit(solution)/shard_map/ppermute | solution.py:785
  278.1 2.9 sum_lanes.2
  281.0 3.8 %all-to-all-start.2 = ((bf16[8,64,1408]{2,1,0:T(8,128)(2,1)}), bf16[8,64,1408]{2,1,0:T(8,128)(2,1)S(1)}, u32[]{:S(2)}, u32[]{:S(2)}) async-start(bf16[8,64,1408]{2,1,0:T(8,128)(2,1)} %bitcast.53), calls=%async_computation.4 | async-start | bytes 2883584 | tf_op jit(solution)/shard_map/all_to_all | solution.py:705
  314.8 5.7 %collective-permute-done.27 = f32[4,2,320]{2,1,0:T(2,128)S(1)} collective-permute-done((f32[4,2,320]{2,1,0:T(2,128)S(1)}, f32[4,2,320]{2,1,0:T(2,128)S(1)}, u32[]{:S(2)}, u32[]{:S(2)}) %collective-permute-start.27) | collective-permute-done | bytes 10272 | tf_op jit(solution)/shard_map/ppermute | solution.py:785
  322.9 3.5 all-to-all-start.3
  337.7 5.5 %collective-permute-done.30 = f32[2,320]{1,0:T(2,128)S(1)} collective-permute-done((f32[2,320]{1,0:T(2,128)S(1)}, f32[2,320]{1,0:T(2,128)S(1)}, u32[]{:S(2)}, u32[]{:S(2)}) %collective-permute-start.30) | collective-permute-done | bytes 2592 | tf_op jit(solution)/shard_map/ppermute | solution.py:785
  346.1 3.0 sum_mixer.1
  (227 shorter events, 114.6 us)
Async XLA Ops:
  13.7 33.2 %all-to-all-start = ((bf16[8,64,1024]{2,1,0:T(8,128)(2,1)}), bf16[8,64,1024]{2,1,0:T(8,128)(2,1)}, u32[]{:S(2)}, u32[]{:S(2)}) async-start(bf16[8,64,1024]{2,1,0:T(8,128)(2,1)} %bitcast.2), calls=%async_computation | async-start | bytes 2097152 | tf_op jit(solution)/shard_map/all_to_all | solution.py:705
  20.2 24.2 %collective-permute-start.1 = (bf16[240,2048]{1,0:T(8,128)(2,1)S(1)}, bf16[240,2048]{1,0:T(8,128)(2,1)S(1)}, u32[]{:S(2)}, u32[]{:S(2)}) collective-permute-start(bf16[240,2048]{1,0:T(8,128)(2,1)S(1)} %join_rows.1), channel_id=1, source_target_pairs={{0,4},{1,5},{2,6},{3,7},{4,0},{5,1},{6,2},{7,3},{8,12},{9,13},{10,... | collective-permute-start | bytes 2949128 | tf_op jit(solution)/shard_map/ppermute | solution.py:785
  21.7 24.0 %collective-permute-start = (bf16[240,2048]{1,0:T(8,128)(2,1)S(1)}, bf16[240,2048]{1,0:T(8,128)(2,1)}, u32[]{:S(2)}, u32[]{:S(2)}) collective-permute-start(bf16[240,2048]{1,0:T(8,128)(2,1)S(1)} %join_rows.1), channel_id=1, source_target_pairs={{0,2},{1,3},{2,0},{3,1},{4,6},{5,7},{6,4},{7,5},{8,10},{9,11},{10,... | collective-permute-start | bytes 2949128 | tf_op jit(solution)/shard_map/ppermute | solution.py:785
  23.2 35.3 %collective-permute-start.6 = (s32[1,4]{1,0:T(1,128)S(1)}, s32[1,4]{1,0:T(1,128)S(1)}, u32[]{:S(2)}, u32[]{:S(2)}) collective-permute-start(s32[1,4]{1,0:T(1,128)S(1)} %copy-done.26), channel_id=1, source_target_pairs={{0,24},{1,25},{2,26},{3,27},{4,28},{5,29},{6,30},{7,31},{8,16},{9,... | collective-permute-start | bytes 56 | tf_op jit(solution)/shard_map/ppermute | solution.py:785
  27.0 31.4 %collective-permute-start.5 = (s32[1,4]{1,0:T(1,128)S(1)}, s32[1,4]{1,0:T(1,128)S(1)}, u32[]{:S(2)}, u32[]{:S(2)}) collective-permute-start(s32[1,4]{1,0:T(1,128)S(1)} %copy-done.26), channel_id=1, source_target_pairs={{0,16},{1,17},{2,18},{3,19},{4,20},{5,21},{6,22},{7,23},{8,24},{9,... | collective-permute-start | bytes 56 | tf_op jit(solution)/shard_map/ppermute | solution.py:785
  27.0 31.4 %collective-permute-start.4 = (s32[1,4]{1,0:T(1,128)S(1)}, s32[1,4]{1,0:T(1,128)S(1)}, u32[]{:S(2)}, u32[]{:S(2)}) collective-permute-start(s32[1,4]{1,0:T(1,128)S(1)} %copy-done.26), channel_id=1, source_target_pairs={{0,8},{1,9},{2,10},{3,11},{4,12},{5,13},{6,14},{7,15},{8,0},{9,1},... | collective-permute-start | bytes 56 | tf_op jit(solution)/shard_map/ppermute | solution.py:785
  46.9 33.7 %all-to-all-start.1 = ((bf16[8,64,1152]{2,1,0:T(8,128)(2,1)}), bf16[8,64,1152]{2,1,0:T(8,128)(2,1)}, u32[]{:S(2)}, u32[]{:S(2)}) async-start(bf16[8,64,1152]{2,1,0:T(8,128)(2,1)} %bitcast.4), calls=%async_computation.1 | async-start | bytes 2359296 | tf_op jit(solution)/shard_map/all_to_all | solution.py:705
  51.2 102.5 %all-gather.3.cloned.1.call-start = ((), (), s32[]{:S(2)}) async-start(), calls=%async_computation.6 | async-start | bytes 4718592 | tf_op jit(solution)/shard_map/all_gather | solution.py:691
  52.6 25.8 %collective-permute-start.3 = (bf16[512,1024]{1,0:T(8,128)(2,1)}, bf16[512,1024]{1,0:T(8,128)(2,1)}, u32[]{:S(2)}, u32[]{:S(2)}) collective-permute-start(bf16[512,1024]{1,0:T(8,128)(2,1)} %bitcast.3.refs_5_.refs_7_), channel_id=1, source_target_pairs={{0,4},{1,5},{2,6},{3,7},{4,0},{5,1},{6,2},{7,3},{8,12},{9,13},{10,... | collective-permute-start | bytes 3145736 | tf_op jit(solution)/shard_map/ppermute | solution.py:785
  54.2 25.4 %collective-permute-start.2 = (bf16[512,1024]{1,0:T(8,128)(2,1)}, bf16[512,1024]{1,0:T(8,128)(2,1)}, u32[]{:S(2)}, u32[]{:S(2)}) collective-permute-start(bf16[512,1024]{1,0:T(8,128)(2,1)} %bitcast.3.refs_5_.refs_7_), channel_id=1, source_target_pairs={{0,2},{1,3},{2,0},{3,1},{4,6},{5,7},{6,4},{7,5},{8,10},{9,11},{10,... | collective-permute-start | bytes 3145736 | tf_op jit(solution)/shard_map/ppermute | solution.py:785
  80.6 98.4 %all-gather.5.cloned.1.call-start = ((), (), s32[]{:S(2)}) async-start(), calls=%async_computation.8 | async-start | bytes 4718592 | tf_op jit(solution)/shard_map/all_gather | solution.py:691
  81.4 168.3 %reduce-scatter.3.cloned.1.call-start = ((), (), s32[]{:S(2)}) async-start(), calls=%async_computation.7 | async-start | bytes 4718592 | tf_op jit(solution)/shard_map/reduce_scatter | solution.py:696
  83.0 52.8 %collective-permute-start.8 = (bf16[512,1152]{1,0:T(8,128)(2,1)}, bf16[512,1152]{1,0:T(8,128)(2,1)}, u32[]{:S(2)}, u32[]{:S(2)}) collective-permute-start(bf16[512,1152]{1,0:T(8,128)(2,1)} %bitcast.5.refs_10_.refs_12_), channel_id=1, source_target_pairs={{0,4},{1,5},{2,6},{3,7},{4,0},{5,1},{6,2},{7,3},{8,12},{9,13},{10,... | collective-permute-start | bytes 3538952 | tf_op jit(solution)/shard_map/ppermute | solution.py:785
  84.5 51.3 %collective-permute-start.7 = (bf16[512,1152]{1,0:T(8,128)(2,1)}, bf16[512,1152]{1,0:T(8,128)(2,1)}, u32[]{:S(2)}, u32[]{:S(2)}) collective-permute-start(bf16[512,1152]{1,0:T(8,128)(2,1)} %bitcast.5.refs_10_.refs_12_), channel_id=1, source_target_pairs={{0,2},{1,3},{2,0},{3,1},{4,6},{5,7},{6,4},{7,5},{8,10},{9,11},{10,... | collective-permute-start | bytes 3538952 | tf_op jit(solution)/shard_map/ppermute | solution.py:785
  86.0 35.9 %collective-permute-start.11 = (bf16[112,2048]{1,0:T(8,128)(2,1)S(1)}, bf16[112,2048]{1,0:T(8,128)(2,1)S(1)}, u32[]{:S(2)}, u32[]{:S(2)}) collective-permute-start(bf16[112,2048]{1,0:T(8,128)(2,1)S(1)} %slice.59.refs_2_), channel_id=1, source_target_pairs={{0,4},{1,5},{2,6},{3,7},{4,0},{5,1},{6,2},{7,3},{8,12},{9,13},{10,... | collective-permute-start | bytes 1376264 | tf_op jit(solution)/shard_map/ppermute | solution.py:785
  90.3 45.5 %collective-permute-start.10 = (bf16[256,1024]{1,0:T(8,128)(2,1)}, bf16[256,1024]{1,0:T(8,128)(2,1)}, u32[]{:S(2)}, u32[]{:S(2)}) collective-permute-start(bf16[256,1024]{1,0:T(8,128)(2,1)} %slice.64), channel_id=1, source_target_pairs={{0,2},{1,3},{2,0},{3,1},{4,6},{5,7},{6,4},{7,5},{8,10},{9,11},{10,... | collective-permute-start | bytes 1572872 | tf_op jit(solution)/shard_map/ppermute | solution.py:785
  90.8 45.0 %collective-permute-start.9 = (bf16[256,1024]{1,0:T(8,128)(2,1)}, bf16[256,1024]{1,0:T(8,128)(2,1)}, u32[]{:S(2)}, u32[]{:S(2)}) collective-permute-start(bf16[256,1024]{1,0:T(8,128)(2,1)} %slice.63), channel_id=1, source_target_pairs={{0,4},{1,5},{2,6},{3,7},{4,0},{5,1},{6,2},{7,3},{8,12},{9,13},{10,... | collective-permute-start | bytes 1572872 | tf_op jit(solution)/shard_map/ppermute | solution.py:785
  178.8 109.1 %reduce-scatter.5.cloned.1.call-start = ((), (), s32[]{:S(2)}) async-start(), calls=%async_computation.9 | async-start | bytes 4718592 | tf_op jit(solution)/shard_map/reduce_scatter | solution.py:696
  188.8 30.7 %collective-permute-start.17 = (bf16[256,2048]{1,0:T(8,128)(2,1)}, bf16[256,2048]{1,0:T(8,128)(2,1)}, u32[]{:S(2)}, u32[]{:S(2)}) collective-permute-start(bf16[256,2048]{1,0:T(8,128)(2,1)} %get-tuple-element.163), channel_id=1, source_target_pairs={{0,4},{1,5},{2,6},{3,7},{4,0},{5,1},{6,2},{7,3},{8,12},{9,13},{10,... | collective-permute-start | bytes 3145736 | tf_op jit(solution)/shard_map/ppermute | solution.py:785
  189.1 30.4 %collective-permute-start.16 = (bf16[224,2048]{1,0:T(8,128)(2,1)}, bf16[224,2048]{1,0:T(8,128)(2,1)}, u32[]{:S(2)}, u32[]{:S(2)}) collective-permute-start(bf16[224,2048]{1,0:T(8,128)(2,1)} %get-tuple-element.162), channel_id=1, source_target_pairs={{0,2},{1,3},{2,0},{3,1},{4,6},{5,7},{6,4},{7,5},{8,10},{9,11},{10,... | collective-permute-start | bytes 2752520 | tf_op jit(solution)/shard_map/ppermute | solution.py:785
  227.7 31.7 %collective-permute-start.18 = (bf16[512,1408]{1,0:T(8,128)(2,1)}, bf16[512,1408]{1,0:T(8,128)(2,1)S(1)}, u32[]{:S(2)}, u32[]{:S(2)}) collective-permute-start(bf16[512,1408]{1,0:T(8,128)(2,1)} %get-tuple-element.184), channel_id=1, source_target_pairs={{0,2},{1,3},{2,0},{3,1},{4,6},{5,7},{6,4},{7,5},{8,10},{9,11},{10,... | collective-permute-start | bytes 4325384 | tf_op jit(solution)/shard_map/ppermute | solution.py:785
  229.2 30.6 %collective-permute-start.19 = (bf16[512,1408]{1,0:T(8,128)(2,1)}, bf16[512,1408]{1,0:T(8,128)(2,1)}, u32[]{:S(2)}, u32[]{:S(2)}) collective-permute-start(bf16[512,1408]{1,0:T(8,128)(2,1)} %get-tuple-element.185), channel_id=1, source_target_pairs={{0,4},{1,5},{2,6},{3,7},{4,0},{5,1},{6,2},{7,3},{8,12},{9,13},{10,... | collective-permute-start | bytes 4325384 | tf_op jit(solution)/shard_map/ppermute | solution.py:785
  281.0 41.9 %all-to-all-start.2 = ((bf16[8,64,1408]{2,1,0:T(8,128)(2,1)}), bf16[8,64,1408]{2,1,0:T(8,128)(2,1)S(1)}, u32[]{:S(2)}, u32[]{:S(2)}) async-start(bf16[8,64,1408]{2,1,0:T(8,128)(2,1)} %bitcast.53), calls=%async_computation.4 | async-start | bytes 2883584 | tf_op jit(solution)/shard_map/all_to_all | solution.py:705
  322.9 26.1 %all-to-all-start.3 = ((bf16[8,64,768]{2,1,0:T(8,128)(2,1)}), bf16[8,64,768]{2,1,0:T(8,128)(2,1)S(1)}, u32[]{:S(2)}, u32[]{:S(2)}) async-start(bf16[8,64,768]{2,1,0:T(8,128)(2,1)} %bitcast.55), calls=%async_computation.5 | async-start | bytes 1572864 | tf_op jit(solution)/shard_map/all_to_all | solution.py:705
  (46 other events, 427.5 us)
Sparse Core Ops, SparseCore 0:
  80.7 46.3 all-gather.2
  129.3 45.8 all-gather.4
  178.9 47.3 reduce-scatter.2
  228.4 48.0 reduce-scatter.4
